TPU v7x, 32 devices: a whole 2x2x4 slice. The times are simulated.
32 devices in a mesh: slab: 8 (over z, x), row: 4 (over y, core).
Axes of the slice: x: 2, y: 2, z: 4, core: 2. Of those that a mesh axis runs over, the one named last changes fastest.
Arguments:
- edge_weights: int32 [3, 16, 32, 512], P(None, 'slab', 'row'), may hold values from 1 to 15
- seeds: int32 [16, 32, 512], P('slab', 'row'), may hold values from -8 to 7
- supervoxel: int32 [16, 32, 512], P('slab', 'row'), may hold values from 0 to 127
- coarse_blocks: float32 [4, 1024, 1024], P('row', 'slab'), as said below
Outputs:
- potentials: float32 [8, 16, 32, 512], P(None, 'slab', 'row')
Inputs may be any that keep to these rules, and one draw needn't show every extreme that they name: `seeds`: a negative value marks an unseeded voxel. `coarse_blocks`: the entries named by dc lie between 0.6 and 1.2 times 2 * 8 * 4.
All inputs are finite; a program needn't handle non-finite values.
Results may differ from a plain program's by a relative error of at most 0.00024.
Values sent between devices are 32-bit elements; how exact they have to be, the bound alone decides.
No kernel may reach another device: no remote copies, remote signals or barrier semaphores. Data moves between devices by JAX's collectives and lax.ppermute only.
A program may use at most 64 MiB of HBM per device.

v0:
```python
import math

import jax
import jax.numpy as jnp
from jax import lax
from jax.sharding import PartitionSpec as P

LABELS = 8
CZ = 2
CY = 8
NX = 512
CC = 128
CYCLES = 2


prior_mass = 0.25
seed_weight = 4.0
smooth_step = 0.8
coarse_step = 0.7
weight_unit = 0.125


def padded(cells, sides, width):
    for axis, dim in sides:
        count = lax.axis_size(axis)
        ends = count - 1
        head = lax.slice_in_dim(cells, 0, width, axis=dim)
        tail = lax.slice_in_dim(cells, cells.shape[dim] - width, cells.shape[dim], axis=dim)
        cells = jnp.concatenate(
            [
                lax.ppermute(tail, axis, [(i, (i + 1) % count) for i in range(ends)]),
                cells,
                lax.ppermute(head, axis, [((i + 1) % count, i) for i in range(ends)]),
            ],
            axis=dim,
        )
    return cells


def shifted(block, axis, distance):
    devices = range(lax.axis_size(axis))
    route = [(i - distance, i) for i in devices if i - distance in devices]
    return lax.ppermute(block, axis, route)


def lower_x(a):
    return jnp.pad(a[..., :-1], [(0, 0)] * (a.ndim - 1) + [(1, 0)])


def upper_x(a):
    return jnp.pad(a[..., 1:], [(0, 0)] * (a.ndim - 1) + [(0, 1)])


def crop(a, margin):
    return a[..., margin : a.shape[-3] - margin, margin : a.shape[-2] - margin, :]


def rim_one(field):
    return padded(field, (("slab", 1), ("row", 2)), 1)


def per_device(edge_weights, seeds, supervoxel, coarse_blocks):
    n_slab = lax.axis_size("slab")
    n_row = lax.axis_size("row")
    group = min(16, n_slab)
    sections = n_slab // group
    slab_pos = lax.axis_index("slab")
    row_pos = lax.axis_index("row")
    stacked = jnp.concatenate([edge_weights, seeds[None]], axis=0)
    lower_plane = shifted(edge_weights[0, -1:], "slab", 1)
    lower_row = shifted(edge_weights[1, :, -1:], "row", 1)
    framed = jnp.pad(stacked, ((0, 0), (1, 1), (1, 1), (0, 0)))
    framed = framed.at[0, :1, 1:-1].set(lower_plane)
    framed = framed.at[1, 1:-1, :1].set(lower_row)
    width = (framed.shape[1] - CZ) // 2
    weights = framed[:3].astype(jnp.float32) * weight_unit
    plane_ids = slab_pos * CZ - width + jnp.arange(CZ + 2 * width, dtype=jnp.int32)
    line_ids = row_pos * CY - width + jnp.arange(CY + 2 * width, dtype=jnp.int32)
    keep_z = (plane_ids != CZ * n_slab - 1).astype(jnp.float32)[:, None, None]
    keep_y = (line_ids != CY * n_row - 1).astype(jnp.float32)[None, :, None]
    keep_x = (jnp.arange(NX) < NX - 1).astype(jnp.float32)[None, None, :]
    w_z = weights[0] * keep_z
    w_y = weights[1] * keep_y
    w_x = weights[2] * keep_x
    seed_inner = crop(framed[3], 1)
    inner_x = crop(w_x, 1)
    diag = (
        prior_mass
        + seed_weight * (seed_inner >= 0).astype(jnp.float32)
        + crop(w_z, 1)
        + crop(w_y, 1)
        + inner_x
        + w_z[:-2, 1:-1]
        + w_y[1:-1, :-2]
        + lower_x(inner_x)
    )
    label_ids = jnp.arange(LABELS, dtype=jnp.int32)
    source = seed_weight * (seed_inner[None] == label_ids[:, None, None, None]).astype(jnp.float32)

    def residual_on(frame, rim):
        margin = width - rim - 1
        face_z = crop(w_z, margin)
        face_y = crop(w_y, margin)
        face_x = crop(w_x, margin)[1:-1, 1:-1]
        centre = frame[:, 1:-1, 1:-1]
        near = face_z[1:-1, 1:-1] * frame[:, 2:, 1:-1] + face_z[:-2, 1:-1] * frame[:, :-2, 1:-1]
        near = (
            near + face_y[1:-1, 1:-1] * frame[:, 1:-1, 2:] + face_y[1:-1, :-2] * frame[:, 1:-1, :-2]
        )
        near = near + face_x * upper_x(centre) + lower_x(face_x) * lower_x(centre)
        local_diag = crop(diag, width - 1 - rim)
        local_source = crop(source, width - 1 - rim)
        return (local_source - (local_diag * centre - near), local_diag, centre)

    def sweep(field):
        change, local_diag, centre = residual_on(rim_one(field), 0)
        return centre + smooth_step * change / local_diag

    block_row = coarse_blocks[0]
    turn = slab_pos // sections
    section_id = slab_pos % sections
    own_block = lax.dynamic_slice_in_dim(block_row, turn * CC, CC, 1)
    coarse_diag = jnp.diagonal(own_block)
    cells = CZ * CY * NX
    span = math.gcd(cells, 2048)
    flat_ids = supervoxel.reshape(cells)
    coarse_ids = jnp.arange(CC, dtype=jnp.int32)
    field = jnp.zeros((LABELS, CZ, CY, NX), jnp.float32)
    for cycle in range(CYCLES):
        field = sweep(sweep(field))
        residual, unused_diag, unused_centre = residual_on(rim_one(field), 0)
        flat_rows = residual.reshape(LABELS, cells)

        def collect_block(index, total):
            piece = lax.dynamic_slice_in_dim(flat_rows, index * span, span, 1)
            piece_ids = lax.dynamic_slice_in_dim(flat_ids, index * span, span, 0)
            onehot = (piece_ids[:, None] == coarse_ids[None, :]).astype(jnp.float32)
            return total + jnp.dot(
                piece, onehot, precision=lax.Precision.HIGHEST, preferred_element_type=jnp.float32
            )

        coarse_rhs = lax.fori_loop(
            0, cells // span, collect_block, jnp.zeros((LABELS, CC), jnp.float32)
        )
        first = coarse_step * coarse_rhs / coarse_diag
        gathered = lax.all_gather(first, "slab", axis=1, tiled=True)
        arranged = gathered.reshape(LABELS, group, sections, CC)
        section = lax.dynamic_slice_in_dim(arranged, section_id, 1, 2).reshape(LABELS, group * CC)
        second = (
            first
            + coarse_step
            * (
                coarse_rhs
                - lax.dot_general(
                    section,
                    block_row,
                    (((1,), (1,)), ((), ())),
                    precision=lax.Precision.HIGHEST,
                    preferred_element_type=jnp.float32,
                )
            )
            / coarse_diag
        )
        correction = jnp.take(second, flat_ids, axis=1).reshape(LABELS, CZ, CY, NX)
        field = sweep(field + correction)
    return field


def solution(mesh):
    in_specs = (
        P(None, "slab", "row", None),
        P("slab", "row", None),
        P("slab", "row", None),
        P("row", "slab", None),
    )
    out_specs = P(None, "slab", "row", None)
    return jax.shard_map(
        per_device, mesh=mesh, in_specs=in_specs, out_specs=out_specs, check_vma=False
    )
```

profile of v0, /device:TPU:6, one launch (start us, length us, event | category | flops | bytes accessed | tf_op | source)
XLA Modules:
  0.0 296.9 jit_solution(196694166765577341)
XLA Ops:
  0.0 2.6 collective-permute-start.2
  2.6 4.3 %collective-permute-start.3 = (f32[8,1,8,512]{3,2,1,0:T(8,128)S(1)}, f32[8,1,8,512]{3,2,1,0:T(8,128)S(1)}, u32[]{:S(2)}, u32[]{:S(2)}) collective-permute-start(f32[8,1,8,512]{3,2,1,0:T(8,128)S(1)} %broadcast.145), channel_id=1, source_target_pairs={{0,4},{4,8},{8,12},{12,16},{16,20},{20,24},{24,28},{1,5},{5,9},{9,... | collective-permute-start | bytes 393224 | tf_op jit(solution)/shard_map/ppermute | solution.py:31
  7.6 2.5 collective-permute-start
  16.7 3.6 %collective-permute-start.4 = (f32[8,4,1,512]{3,2,1,0:T(1,128)S(1)}, f32[8,4,1,512]{3,2,1,0:T(1,128)S(1)}, u32[]{:S(2)}, u32[]{:S(2)}) collective-permute-start(f32[8,4,1,512]{3,2,1,0:T(1,128)S(1)} %get-tuple-element.286), channel_id=1, source_target_pairs={{1,0},{2,1},{3,2},{5,4},{6,5},{7,6},{9,8},{10,9},{11,10},{13,12},{... | collective-permute-start | bytes 196616 | tf_op jit(solution)/shard_map/ppermute | solution.py:33
  22.4 3.6 %collective-permute-done.5 = f32[8,4,1,512]{3,2,1,0:T(1,128)S(1)} collective-permute-done((f32[8,4,1,512]{3,2,1,0:T(1,128)S(1)}, f32[8,4,1,512]{3,2,1,0:T(1,128)S(1)}, u32[]{:S(2)}, u32[]{:S(2)}) %collective-permute-start.5) | collective-permute-done | bytes 65568 | tf_op jit(solution)/shard_map/ppermute | solution.py:31
  26.2 3.3 %collective-permute-start.6 = (f32[8,1,8,512]{3,2,1,0:T(8,128)S(1)}, f32[8,1,8,512]{3,2,1,0:T(8,128)S(1)}, u32[]{:S(2)}, u32[]{:S(2)}) collective-permute-start(f32[8,1,8,512]{3,2,1,0:T(8,128)S(1)} %get-tuple-element.318), channel_id=1, source_target_pairs={{4,0},{8,4},{12,8},{16,12},{20,16},{24,20},{28,24},{5,1},{9,5},{13... | collective-permute-start | bytes 393224 | tf_op jit(solution)/shard_map/ppermute | solution.py:33
  29.5 3.5 %collective-permute-start.7 = (f32[8,1,8,512]{3,2,1,0:T(8,128)S(1)}, f32[8,1,8,512]{3,2,1,0:T(8,128)S(1)}, u32[]{:S(2)}, u32[]{:S(2)}) collective-permute-start(f32[8,1,8,512]{3,2,1,0:T(8,128)S(1)} %get-tuple-element.317), channel_id=1, source_target_pairs={{0,4},{4,8},{8,12},{12,16},{16,20},{20,24},{24,28},{1,5},{5,9},{9,... | collective-permute-start | bytes 393224 | tf_op jit(solution)/shard_map/ppermute | solution.py:31
  41.0 3.0 %collective-permute-done.9 = f32[8,4,1,512]{3,2,1,0:T(1,128)S(1)} collective-permute-done((f32[8,4,1,512]{3,2,1,0:T(1,128)S(1)}, f32[8,4,1,512]{3,2,1,0:T(1,128)S(1)}, u32[]{:S(2)}, u32[]{:S(2)}) %collective-permute-start.9) | collective-permute-done | bytes 65568 | tf_op jit(solution)/shard_map/ppermute | solution.py:31
  46.2 4.8 %collective-permute-start.11 = (f32[8,1,8,512]{3,2,1,0:T(8,128)S(1)}, f32[8,1,8,512]{3,2,1,0:T(8,128)S(1)}, u32[]{:S(2)}, u32[]{:S(2)}) collective-permute-start(f32[8,1,8,512]{3,2,1,0:T(8,128)S(1)} %get-tuple-element.313), channel_id=1, source_target_pairs={{0,4},{4,8},{8,12},{12,16},{16,20},{20,24},{24,28},{1,5},{5,9},{9,... | collective-permute-start | bytes 393224 | tf_op jit(solution)/shard_map/ppermute | solution.py:31
  58.1 3.0 %collective-permute-done.13 = f32[8,4,1,512]{3,2,1,0:T(1,128)S(1)} collective-permute-done((f32[8,4,1,512]{3,2,1,0:T(1,128)S(1)}, f32[8,4,1,512]{3,2,1,0:T(1,128)S(1)}, u32[]{:S(2)}, u32[]{:S(2)}) %collective-permute-start.13) | collective-permute-done | bytes 65568 | tf_op jit(solution)/shard_map/ppermute | solution.py:31
  61.6 2.5 while.30
  64.1 31.9 %all_gather.6 = f32[8,1024]{1,0:T(8,128)S(1)} all-gather(f32[8,128]{1,0:T(8,128)S(1)} %multiply_divide_fusion.1), channel_id=1, replica_groups=mesh['slab'=8,'row'=4] {'slab'}, dimensions={1}, use_global_device_ids=true | all-gather | bytes 36864 | tf_op jit(solution)/shard_map/all_gather | solution.py:146
  96.6 27.9 %gather_fusion.1 = f32[8192,8]{1,0:T(8,128)} fusion(f32[8,128]{0,1:T(8,128)S(1)} %copy.9, s32[8192]{0:T(1024)S(1)} %fusion.122), kind=kCustom, calls=%fused_computation.clone | custom fusion | bytes 557056 | tf_op jit(solution)/shard_map/jit(_take)/gather | solution.py:164
  124.5 7.5 %broadcast_select_fusion.1 = f32[8192,8]{1,0:T(8,128)} fusion(f32[8192,8]{1,0:T(8,128)} %gather_fusion.1, pred[8192]{0:T(1024)(128)(4,1)S(1)} %compare_and_fusion), kind=kLoop, calls=%fused_computation.16 | loop fusion | flops 65536 | bytes 532480 | tf_op jit(solution)/shard_map/jit(_take)/select_n | solution.py:164
  131.9 2.8 copy.10
  134.8 3.3 %collective-permute-start.14 = (f32[8,1,8,512]{3,2,1,0:T(8,128)S(1)}, f32[8,1,8,512]{3,2,1,0:T(8,128)S(1)}, u32[]{:S(2)}, u32[]{:S(2)}) collective-permute-start(f32[8,1,8,512]{3,2,1,0:T(8,128)S(1)} %get-tuple-element.310), channel_id=1, source_target_pairs={{4,0},{8,4},{12,8},{16,12},{20,16},{24,20},{28,24},{5,1},{9,5},{13... | collective-permute-start | bytes 393224 | tf_op jit(solution)/shard_map/ppermute | solution.py:33
  138.1 3.5 %collective-permute-start.15 = (f32[8,1,8,512]{3,2,1,0:T(8,128)S(1)}, f32[8,1,8,512]{3,2,1,0:T(8,128)S(1)}, u32[]{:S(2)}, u32[]{:S(2)}) collective-permute-start(f32[8,1,8,512]{3,2,1,0:T(8,128)S(1)} %get-tuple-element.309), channel_id=1, source_target_pairs={{0,4},{4,8},{8,12},{12,16},{16,20},{20,24},{24,28},{1,5},{5,9},{9,... | collective-permute-start | bytes 393224 | tf_op jit(solution)/shard_map/ppermute | solution.py:31
  149.6 3.0 %collective-permute-done.17 = f32[8,4,1,512]{3,2,1,0:T(1,128)S(1)} collective-permute-done((f32[8,4,1,512]{3,2,1,0:T(1,128)S(1)}, f32[8,4,1,512]{3,2,1,0:T(1,128)S(1)}, u32[]{:S(2)}, u32[]{:S(2)}) %collective-permute-start.17) | collective-permute-done | bytes 65568 | tf_op jit(solution)/shard_map/ppermute | solution.py:31
  154.8 4.8 %collective-permute-start.19 = (f32[8,1,8,512]{3,2,1,0:T(8,128)S(1)}, f32[8,1,8,512]{3,2,1,0:T(8,128)S(1)}, u32[]{:S(2)}, u32[]{:S(2)}) collective-permute-start(f32[8,1,8,512]{3,2,1,0:T(8,128)S(1)} %get-tuple-element.305), channel_id=1, source_target_pairs={{0,4},{4,8},{8,12},{12,16},{16,20},{20,24},{24,28},{1,5},{5,9},{9,... | collective-permute-start | bytes 393224 | tf_op jit(solution)/shard_map/ppermute | solution.py:31
  166.7 3.0 %collective-permute-done.21 = f32[8,4,1,512]{3,2,1,0:T(1,128)S(1)} collective-permute-done((f32[8,4,1,512]{3,2,1,0:T(1,128)S(1)}, f32[8,4,1,512]{3,2,1,0:T(1,128)S(1)}, u32[]{:S(2)}, u32[]{:S(2)}) %collective-permute-start.21) | collective-permute-done | bytes 65568 | tf_op jit(solution)/shard_map/ppermute | solution.py:31
  172.0 5.3 %collective-permute-start.23 = (f32[8,1,8,512]{3,2,1,0:T(8,128)S(1)}, f32[8,1,8,512]{3,2,1,0:T(8,128)S(1)}, u32[]{:S(2)}, u32[]{:S(2)}) collective-permute-start(f32[8,1,8,512]{3,2,1,0:T(8,128)S(1)} %get-tuple-element.301), channel_id=1, source_target_pairs={{0,4},{4,8},{8,12},{12,16},{16,20},{20,24},{24,28},{1,5},{5,9},{9,... | collective-permute-start | bytes 393224 | tf_op jit(solution)/shard_map/ppermute | solution.py:31
  184.4 3.0 %collective-permute-done.25 = f32[8,4,1,512]{3,2,1,0:T(1,128)S(1)} collective-permute-done((f32[8,4,1,512]{3,2,1,0:T(1,128)S(1)}, f32[8,4,1,512]{3,2,1,0:T(1,128)S(1)}, u32[]{:S(2)}, u32[]{:S(2)}) %collective-permute-start.25) | collective-permute-done | bytes 65568 | tf_op jit(solution)/shard_map/ppermute | solution.py:31
  189.7 5.2 %collective-permute-start.27 = (f32[8,1,8,512]{3,2,1,0:T(8,128)S(1)}, f32[8,1,8,512]{3,2,1,0:T(8,128)S(1)}, u32[]{:S(2)}, u32[]{:S(2)}) collective-permute-start(f32[8,1,8,512]{3,2,1,0:T(8,128)S(1)} %get-tuple-element.297), channel_id=1, source_target_pairs={{0,4},{4,8},{8,12},{12,16},{16,20},{20,24},{24,28},{1,5},{5,9},{9,... | collective-permute-start | bytes 393224 | tf_op jit(solution)/shard_map/ppermute | solution.py:31
  202.0 3.0 %collective-permute-done.29 = f32[8,4,1,512]{3,2,1,0:T(1,128)S(1)} collective-permute-done((f32[8,4,1,512]{3,2,1,0:T(1,128)S(1)}, f32[8,4,1,512]{3,2,1,0:T(1,128)S(1)}, u32[]{:S(2)}, u32[]{:S(2)}) %collective-permute-start.29) | collective-permute-done | bytes 65568 | tf_op jit(solution)/shard_map/ppermute | solution.py:31
  205.5 2.5 while.31
  208.0 30.0 %all_gather.7 = f32[8,1024]{1,0:T(8,128)S(1)} all-gather(f32[8,128]{1,0:T(8,128)S(1)} %multiply_divide_fusion), channel_id=1, replica_groups=mesh['slab'=8,'row'=4] {'slab'}, dimensions={1}, use_global_device_ids=true | all-gather | bytes 36864 | tf_op jit(solution)/shard_map/all_gather | solution.py:146
  238.6 27.9 %gather_fusion.2 = f32[8192,8]{1,0:T(8,128)} fusion(f32[8,128]{0,1:T(8,128)S(1)} %copy.11, s32[8192]{0:T(1024)S(1)} %fusion.122), kind=kCustom, calls=%fused_computation.1.clone | custom fusion | bytes 557056 | tf_op jit(solution)/shard_map/jit(_take)/gather | solution.py:164
  266.5 7.5 %broadcast_select_fusion = f32[8192,8]{1,0:T(8,128)} fusion(f32[8192,8]{1,0:T(8,128)} %gather_fusion.2, pred[8192]{0:T(1024)(128)(4,1)S(1)} %compare_and_fusion), kind=kLoop, calls=%fused_computation.15 | loop fusion | flops 65536 | bytes 532480 | tf_op jit(solution)/shard_map/jit(_take)/select_n | solution.py:164
  273.9 2.8 copy.12
  276.8 4.6 %collective-permute-start.30 = (f32[8,1,8,512]{3,2,1,0:T(8,128)S(1)}, f32[8,1,8,512]{3,2,1,0:T(8,128)S(1)}, u32[]{:S(2)}, u32[]{:S(2)}) collective-permute-start(f32[8,1,8,512]{3,2,1,0:T(8,128)S(1)} %get-tuple-element.294), channel_id=1, source_target_pairs={{4,0},{8,4},{12,8},{16,12},{20,16},{24,20},{28,24},{5,1},{9,5},{13... | collective-permute-start | bytes 393224 | tf_op jit(solution)/shard_map/ppermute | solution.py:33
  284.6 3.7 %collective-permute-done.31 = f32[8,1,8,512]{3,2,1,0:T(8,128)S(1)} collective-permute-done((f32[8,1,8,512]{3,2,1,0:T(8,128)S(1)}, f32[8,1,8,512]{3,2,1,0:T(8,128)S(1)}, u32[]{:S(2)}, u32[]{:S(2)}) %collective-permute-start.31) | collective-permute-done | bytes 131104 | tf_op jit(solution)/shard_map/ppermute | solution.py:31
  292.9 3.0 %collective-permute-done.33 = f32[8,4,1,512]{3,2,1,0:T(1,128)S(1)} collective-permute-done((f32[8,4,1,512]{3,2,1,0:T(1,128)S(1)}, f32[8,4,1,512]{3,2,1,0:T(1,128)S(1)}, u32[]{:S(2)}, u32[]{:S(2)}) %collective-permute-start.33) | collective-permute-done | bytes 65568 | tf_op jit(solution)/shard_map/ppermute | solution.py:31
  (131 shorter events, 78.0 us)
Async XLA Ops:
  0.0 16.5 %collective-permute-start.2 = (f32[8,1,8,512]{3,2,1,0:T(8,128)S(1)}, f32[8,1,8,512]{3,2,1,0:T(8,128)S(1)}, u32[]{:S(2)}, u32[]{:S(2)}) collective-permute-start(f32[8,1,8,512]{3,2,1,0:T(8,128)S(1)} %broadcast.145), channel_id=1, source_target_pairs={{4,0},{8,4},{12,8},{16,12},{20,16},{24,20},{28,24},{5,1},{9,5},{13... | collective-permute-start | bytes 393224 | tf_op jit(solution)/shard_map/ppermute | solution.py:33
  2.6 14.0 %collective-permute-start.3 = (f32[8,1,8,512]{3,2,1,0:T(8,128)S(1)}, f32[8,1,8,512]{3,2,1,0:T(8,128)S(1)}, u32[]{:S(2)}, u32[]{:S(2)}) collective-permute-start(f32[8,1,8,512]{3,2,1,0:T(8,128)S(1)} %broadcast.145), channel_id=1, source_target_pairs={{0,4},{4,8},{8,12},{12,16},{16,20},{20,24},{24,28},{1,5},{5,9},{9,... | collective-permute-start | bytes 393224 | tf_op jit(solution)/shard_map/ppermute | solution.py:31
  7.6 8.4 %collective-permute-start = (s32[1,8,512]{2,1,0:T(8,128)S(1)}, s32[1,8,512]{2,1,0:T(8,128)S(1)}, u32[]{:S(2)}, u32[]{:S(2)}) collective-permute-start(s32[1,8,512]{2,1,0:T(8,128)S(1)} %slice_bitcast_fusion.4), channel_id=1, source_target_pairs={{0,4},{4,8},{8,12},{12,16},{16,20},{20,24},{24,28},{1,5},{5,9},{9,... | collective-permute-start | bytes 49160 | tf_op jit(solution)/shard_map/ppermute | solution.py:43
  10.9 5.3 %collective-permute-start.1 = (s32[2,1,512]{2,1,0:T(1,128)S(1)}, s32[2,1,512]{2,1,0:T(1,128)S(1)}, u32[]{:S(2)}, u32[]{:S(2)}) collective-permute-start(s32[2,1,512]{2,1,0:T(1,128)S(1)} %slice_bitcast_fusion.5), channel_id=1, source_target_pairs={{0,1},{1,2},{2,3},{4,5},{5,6},{6,7},{8,9},{9,10},{10,11},{12,13},{... | collective-permute-start | bytes 12296 | tf_op jit(solution)/shard_map/ppermute | solution.py:43
  16.7 5.7 %collective-permute-start.4 = (f32[8,4,1,512]{3,2,1,0:T(1,128)S(1)}, f32[8,4,1,512]{3,2,1,0:T(1,128)S(1)}, u32[]{:S(2)}, u32[]{:S(2)}) collective-permute-start(f32[8,4,1,512]{3,2,1,0:T(1,128)S(1)} %get-tuple-element.286), channel_id=1, source_target_pairs={{1,0},{2,1},{3,2},{5,4},{6,5},{7,6},{9,8},{10,9},{11,10},{13,12},{... | collective-permute-start | bytes 196616 | tf_op jit(solution)/shard_map/ppermute | solution.py:33
  20.3 5.6 %collective-permute-start.5 = (f32[8,4,1,512]{3,2,1,0:T(1,128)S(1)}, f32[8,4,1,512]{3,2,1,0:T(1,128)S(1)}, u32[]{:S(2)}, u32[]{:S(2)}) collective-permute-start(f32[8,4,1,512]{3,2,1,0:T(1,128)S(1)} %get-tuple-element.287), channel_id=1, source_target_pairs={{0,1},{1,2},{2,3},{4,5},{5,6},{6,7},{8,9},{9,10},{10,11},{12,13},{... | collective-permute-start | bytes 196616 | tf_op jit(solution)/shard_map/ppermute | solution.py:31
  26.2 7.9 %collective-permute-start.6 = (f32[8,1,8,512]{3,2,1,0:T(8,128)S(1)}, f32[8,1,8,512]{3,2,1,0:T(8,128)S(1)}, u32[]{:S(2)}, u32[]{:S(2)}) collective-permute-start(f32[8,1,8,512]{3,2,1,0:T(8,128)S(1)} %get-tuple-element.318), channel_id=1, source_target_pairs={{4,0},{8,4},{12,8},{16,12},{20,16},{24,20},{28,24},{5,1},{9,5},{13... | collective-permute-start | bytes 393224 | tf_op jit(solution)/shard_map/ppermute | solution.py:33
  29.5 6.9 %collective-permute-start.7 = (f32[8,1,8,512]{3,2,1,0:T(8,128)S(1)}, f32[8,1,8,512]{3,2,1,0:T(8,128)S(1)}, u32[]{:S(2)}, u32[]{:S(2)}) collective-permute-start(f32[8,1,8,512]{3,2,1,0:T(8,128)S(1)} %get-tuple-element.317), channel_id=1, source_target_pairs={{0,4},{4,8},{8,12},{12,16},{16,20},{20,24},{24,28},{1,5},{5,9},{9,... | collective-permute-start | bytes 393224 | tf_op jit(solution)/shard_map/ppermute | solution.py:31
  36.5 4.5 %collective-permute-start.8 = (f32[8,4,1,512]{3,2,1,0:T(1,128)S(1)}, f32[8,4,1,512]{3,2,1,0:T(1,128)S(1)}, u32[]{:S(2)}, u32[]{:S(2)}) collective-permute-start(f32[8,4,1,512]{3,2,1,0:T(1,128)S(1)} %get-tuple-element.284), channel_id=1, source_target_pairs={{1,0},{2,1},{3,2},{5,4},{6,5},{7,6},{9,8},{10,9},{11,10},{13,12},{... | collective-permute-start | bytes 196616 | tf_op jit(solution)/shard_map/ppermute | solution.py:33
  38.4 5.6 %collective-permute-start.9 = (f32[8,4,1,512]{3,2,1,0:T(1,128)S(1)}, f32[8,4,1,512]{3,2,1,0:T(1,128)S(1)}, u32[]{:S(2)}, u32[]{:S(2)}) collective-permute-start(f32[8,4,1,512]{3,2,1,0:T(1,128)S(1)} %get-tuple-element.285), channel_id=1, source_target_pairs={{0,1},{1,2},{2,3},{4,5},{5,6},{6,7},{8,9},{9,10},{10,11},{12,13},{... | collective-permute-start | bytes 196616 | tf_op jit(solution)/shard_map/ppermute | solution.py:31
  44.3 7.8 %collective-permute-start.10 = (f32[8,1,8,512]{3,2,1,0:T(8,128)S(1)}, f32[8,1,8,512]{3,2,1,0:T(8,128)S(1)}, u32[]{:S(2)}, u32[]{:S(2)}) collective-permute-start(f32[8,1,8,512]{3,2,1,0:T(8,128)S(1)} %get-tuple-element.314), channel_id=1, source_target_pairs={{4,0},{8,4},{12,8},{16,12},{20,16},{24,20},{28,24},{5,1},{9,5},{13... | collective-permute-start | bytes 393224 | tf_op jit(solution)/shard_map/ppermute | solution.py:33
  46.2 7.3 %collective-permute-start.11 = (f32[8,1,8,512]{3,2,1,0:T(8,128)S(1)}, f32[8,1,8,512]{3,2,1,0:T(8,128)S(1)}, u32[]{:S(2)}, u32[]{:S(2)}) collective-permute-start(f32[8,1,8,512]{3,2,1,0:T(8,128)S(1)} %get-tuple-element.313), channel_id=1, source_target_pairs={{0,4},{4,8},{8,12},{12,16},{16,20},{20,24},{24,28},{1,5},{5,9},{9,... | collective-permute-start | bytes 393224 | tf_op jit(solution)/shard_map/ppermute | solution.py:31
  53.6 4.5 %collective-permute-start.12 = (f32[8,4,1,512]{3,2,1,0:T(1,128)S(1)}, f32[8,4,1,512]{3,2,1,0:T(1,128)S(1)}, u32[]{:S(2)}, u32[]{:S(2)}) collective-permute-start(f32[8,4,1,512]{3,2,1,0:T(1,128)S(1)} %get-tuple-element.282), channel_id=1, source_target_pairs={{1,0},{2,1},{3,2},{5,4},{6,5},{7,6},{9,8},{10,9},{11,10},{13,12},{... | collective-permute-start | bytes 196616 | tf_op jit(solution)/shard_map/ppermute | solution.py:33
  55.6 5.6 %collective-permute-start.13 = (f32[8,4,1,512]{3,2,1,0:T(1,128)S(1)}, f32[8,4,1,512]{3,2,1,0:T(1,128)S(1)}, u32[]{:S(2)}, u32[]{:S(2)}) collective-permute-start(f32[8,4,1,512]{3,2,1,0:T(1,128)S(1)} %get-tuple-element.283), channel_id=1, source_target_pairs={{0,1},{1,2},{2,3},{4,5},{5,6},{6,7},{8,9},{9,10},{10,11},{12,13},{... | collective-permute-start | bytes 196616 | tf_op jit(solution)/shard_map/ppermute | solution.py:31
  134.8 7.8 %collective-permute-start.14 = (f32[8,1,8,512]{3,2,1,0:T(8,128)S(1)}, f32[8,1,8,512]{3,2,1,0:T(8,128)S(1)}, u32[]{:S(2)}, u32[]{:S(2)}) collective-permute-start(f32[8,1,8,512]{3,2,1,0:T(8,128)S(1)} %get-tuple-element.310), channel_id=1, source_target_pairs={{4,0},{8,4},{12,8},{16,12},{20,16},{24,20},{28,24},{5,1},{9,5},{13... | collective-permute-start | bytes 393224 | tf_op jit(solution)/shard_map/ppermute | solution.py:33
  138.1 6.9 %collective-permute-start.15 = (f32[8,1,8,512]{3,2,1,0:T(8,128)S(1)}, f32[8,1,8,512]{3,2,1,0:T(8,128)S(1)}, u32[]{:S(2)}, u32[]{:S(2)}) collective-permute-start(f32[8,1,8,512]{3,2,1,0:T(8,128)S(1)} %get-tuple-element.309), channel_id=1, source_target_pairs={{0,4},{4,8},{8,12},{12,16},{16,20},{20,24},{24,28},{1,5},{5,9},{9,... | collective-permute-start | bytes 393224 | tf_op jit(solution)/shard_map/ppermute | solution.py:31
  145.1 4.5 %collective-permute-start.16 = (f32[8,4,1,512]{3,2,1,0:T(1,128)S(1)}, f32[8,4,1,512]{3,2,1,0:T(1,128)S(1)}, u32[]{:S(2)}, u32[]{:S(2)}) collective-permute-start(f32[8,4,1,512]{3,2,1,0:T(1,128)S(1)} %get-tuple-element.280), channel_id=1, source_target_pairs={{1,0},{2,1},{3,2},{5,4},{6,5},{7,6},{9,8},{10,9},{11,10},{13,12},{... | collective-permute-start | bytes 196616 | tf_op jit(solution)/shard_map/ppermute | solution.py:33
  147.0 5.6 %collective-permute-start.17 = (f32[8,4,1,512]{3,2,1,0:T(1,128)S(1)}, f32[8,4,1,512]{3,2,1,0:T(1,128)S(1)}, u32[]{:S(2)}, u32[]{:S(2)}) collective-permute-start(f32[8,4,1,512]{3,2,1,0:T(1,128)S(1)} %get-tuple-element.281), channel_id=1, source_target_pairs={{0,1},{1,2},{2,3},{4,5},{5,6},{6,7},{8,9},{9,10},{10,11},{12,13},{... | collective-permute-start | bytes 196616 | tf_op jit(solution)/shard_map/ppermute | solution.py:31
  152.9 7.8 %collective-permute-start.18 = (f32[8,1,8,512]{3,2,1,0:T(8,128)S(1)}, f32[8,1,8,512]{3,2,1,0:T(8,128)S(1)}, u32[]{:S(2)}, u32[]{:S(2)}) collective-permute-start(f32[8,1,8,512]{3,2,1,0:T(8,128)S(1)} %get-tuple-element.306), channel_id=1, source_target_pairs={{4,0},{8,4},{12,8},{16,12},{20,16},{24,20},{28,24},{5,1},{9,5},{13... | collective-permute-start | bytes 393224 | tf_op jit(solution)/shard_map/ppermute | solution.py:33
  154.8 7.3 %collective-permute-start.19 = (f32[8,1,8,512]{3,2,1,0:T(8,128)S(1)}, f32[8,1,8,512]{3,2,1,0:T(8,128)S(1)}, u32[]{:S(2)}, u32[]{:S(2)}) collective-permute-start(f32[8,1,8,512]{3,2,1,0:T(8,128)S(1)} %get-tuple-element.305), channel_id=1, source_target_pairs={{0,4},{4,8},{8,12},{12,16},{16,20},{20,24},{24,28},{1,5},{5,9},{9,... | collective-permute-start | bytes 393224 | tf_op jit(solution)/shard_map/ppermute | solution.py:31
  164.2 5.6 %collective-permute-start.21 = (f32[8,4,1,512]{3,2,1,0:T(1,128)S(1)}, f32[8,4,1,512]{3,2,1,0:T(1,128)S(1)}, u32[]{:S(2)}, u32[]{:S(2)}) collective-permute-start(f32[8,4,1,512]{3,2,1,0:T(1,128)S(1)} %get-tuple-element.279), channel_id=1, source_target_pairs={{0,1},{1,2},{2,3},{4,5},{5,6},{6,7},{8,9},{9,10},{10,11},{12,13},{... | collective-permute-start | bytes 196616 | tf_op jit(solution)/shard_map/ppermute | solution.py:31
  170.1 8.3 %collective-permute-start.22 = (f32[8,1,8,512]{3,2,1,0:T(8,128)S(1)}, f32[8,1,8,512]{3,2,1,0:T(8,128)S(1)}, u32[]{:S(2)}, u32[]{:S(2)}) collective-permute-start(f32[8,1,8,512]{3,2,1,0:T(8,128)S(1)} %get-tuple-element.302), channel_id=1, source_target_pairs={{4,0},{8,4},{12,8},{16,12},{20,16},{24,20},{28,24},{5,1},{9,5},{13... | collective-permute-start | bytes 393224 | tf_op jit(solution)/shard_map/ppermute | solution.py:33
  172.0 7.8 %collective-permute-start.23 = (f32[8,1,8,512]{3,2,1,0:T(8,128)S(1)}, f32[8,1,8,512]{3,2,1,0:T(8,128)S(1)}, u32[]{:S(2)}, u32[]{:S(2)}) collective-permute-start(f32[8,1,8,512]{3,2,1,0:T(8,128)S(1)} %get-tuple-element.301), channel_id=1, source_target_pairs={{0,4},{4,8},{8,12},{12,16},{16,20},{20,24},{24,28},{1,5},{5,9},{9,... | collective-permute-start | bytes 393224 | tf_op jit(solution)/shard_map/ppermute | solution.py:31
  179.9 4.5 %collective-permute-start.24 = (f32[8,4,1,512]{3,2,1,0:T(1,128)S(1)}, f32[8,4,1,512]{3,2,1,0:T(1,128)S(1)}, u32[]{:S(2)}, u32[]{:S(2)}) collective-permute-start(f32[8,4,1,512]{3,2,1,0:T(1,128)S(1)} %get-tuple-element.276), channel_id=1, source_target_pairs={{1,0},{2,1},{3,2},{5,4},{6,5},{7,6},{9,8},{10,9},{11,10},{13,12},{... | collective-permute-start | bytes 196616 | tf_op jit(solution)/shard_map/ppermute | solution.py:33
  181.9 5.6 %collective-permute-start.25 = (f32[8,4,1,512]{3,2,1,0:T(1,128)S(1)}, f32[8,4,1,512]{3,2,1,0:T(1,128)S(1)}, u32[]{:S(2)}, u32[]{:S(2)}) collective-permute-start(f32[8,4,1,512]{3,2,1,0:T(1,128)S(1)} %get-tuple-element.277), channel_id=1, source_target_pairs={{0,1},{1,2},{2,3},{4,5},{5,6},{6,7},{8,9},{9,10},{10,11},{12,13},{... | collective-permute-start | bytes 196616 | tf_op jit(solution)/shard_map/ppermute | solution.py:31
  187.8 8.2 %collective-permute-start.26 = (f32[8,1,8,512]{3,2,1,0:T(8,128)S(1)}, f32[8,1,8,512]{3,2,1,0:T(8,128)S(1)}, u32[]{:S(2)}, u32[]{:S(2)}) collective-permute-start(f32[8,1,8,512]{3,2,1,0:T(8,128)S(1)} %get-tuple-element.298), channel_id=1, source_target_pairs={{4,0},{8,4},{12,8},{16,12},{20,16},{24,20},{28,24},{5,1},{9,5},{13... | collective-permute-start | bytes 393224 | tf_op jit(solution)/shard_map/ppermute | solution.py:33
  189.7 7.8 %collective-permute-start.27 = (f32[8,1,8,512]{3,2,1,0:T(8,128)S(1)}, f32[8,1,8,512]{3,2,1,0:T(8,128)S(1)}, u32[]{:S(2)}, u32[]{:S(2)}) collective-permute-start(f32[8,1,8,512]{3,2,1,0:T(8,128)S(1)} %get-tuple-element.297), channel_id=1, source_target_pairs={{0,4},{4,8},{8,12},{12,16},{16,20},{20,24},{24,28},{1,5},{5,9},{9,... | collective-permute-start | bytes 393224 | tf_op jit(solution)/shard_map/ppermute | solution.py:31
  197.5 4.5 %collective-permute-start.28 = (f32[8,4,1,512]{3,2,1,0:T(1,128)S(1)}, f32[8,4,1,512]{3,2,1,0:T(1,128)S(1)}, u32[]{:S(2)}, u32[]{:S(2)}) collective-permute-start(f32[8,4,1,512]{3,2,1,0:T(1,128)S(1)} %get-tuple-element.274), channel_id=1, source_target_pairs={{1,0},{2,1},{3,2},{5,4},{6,5},{7,6},{9,8},{10,9},{11,10},{13,12},{... | collective-permute-start | bytes 196616 | tf_op jit(solution)/shard_map/ppermute | solution.py:33
  199.5 5.6 %collective-permute-start.29 = (f32[8,4,1,512]{3,2,1,0:T(1,128)S(1)}, f32[8,4,1,512]{3,2,1,0:T(1,128)S(1)}, u32[]{:S(2)}, u32[]{:S(2)}) collective-permute-start(f32[8,4,1,512]{3,2,1,0:T(1,128)S(1)} %get-tuple-element.275), channel_id=1, source_target_pairs={{0,1},{1,2},{2,3},{4,5},{5,6},{6,7},{8,9},{9,10},{10,11},{12,13},{... | collective-permute-start | bytes 196616 | tf_op jit(solution)/shard_map/ppermute | solution.py:31
  276.8 7.8 %collective-permute-start.30 = (f32[8,1,8,512]{3,2,1,0:T(8,128)S(1)}, f32[8,1,8,512]{3,2,1,0:T(8,128)S(1)}, u32[]{:S(2)}, u32[]{:S(2)}) collective-permute-start(f32[8,1,8,512]{3,2,1,0:T(8,128)S(1)} %get-tuple-element.294), channel_id=1, source_target_pairs={{4,0},{8,4},{12,8},{16,12},{20,16},{24,20},{28,24},{5,1},{9,5},{13... | collective-permute-start | bytes 393224 | tf_op jit(solution)/shard_map/ppermute | solution.py:33
  281.4 6.9 %collective-permute-start.31 = (f32[8,1,8,512]{3,2,1,0:T(8,128)S(1)}, f32[8,1,8,512]{3,2,1,0:T(8,128)S(1)}, u32[]{:S(2)}, u32[]{:S(2)}) collective-permute-start(f32[8,1,8,512]{3,2,1,0:T(8,128)S(1)} %get-tuple-element.293), channel_id=1, source_target_pairs={{0,4},{4,8},{8,12},{12,16},{16,20},{20,24},{24,28},{1,5},{5,9},{9,... | collective-permute-start | bytes 393224 | tf_op jit(solution)/shard_map/ppermute | solution.py:31
  290.3 5.6 %collective-permute-start.33 = (f32[8,4,1,512]{3,2,1,0:T(1,128)S(1)}, f32[8,4,1,512]{3,2,1,0:T(1,128)S(1)}, u32[]{:S(2)}, u32[]{:S(2)}) collective-permute-start(f32[8,4,1,512]{3,2,1,0:T(1,128)S(1)} %get-tuple-element.273), channel_id=1, source_target_pairs={{0,1},{1,2},{2,3},{4,5},{5,6},{6,7},{8,9},{9,10},{10,11},{12,13},{... | collective-permute-start | bytes 196616 | tf_op jit(solution)/shard_map/ppermute | solution.py:31
  (3 other events, 22.8 us)
where the time goes:
time: 298 us; the launch traced here: 297 us
  starting transfers between devices  95.1 us (32%)
  local copies, waits for them, and re-layouts  66.9 us (22%)
  blocking collectives  61.9 us (21%)
  waiting for transfers between devices  46.4 us (16%)
  other arithmetic  19.8 us (7%)
  matrix products  5.65 us (2%)
    all_gather x2, blocking collectives, per_device(): gathered = lax.all_gather(first, 'slab', axis=1, tiled=True)  61.9 us
    gather x2, local copies, waits for them, and re-layouts, per_device(): correction = jnp.take(second, flat_ids, axis=1).reshape(LABELS, CZ, CY, NX)  55.7 us
    ppermute x16, starting transfers between devices, padded(): lax.ppermute(tail, axis, [(i, (i + 1) % count) for i in range(ends)])  52.2 us
    ppermute x16, waiting for transfers between devices, padded(): lax.ppermute(tail, axis, [(i, (i + 1) % count) for i in range(ends)])  39 us
    ppermute x16, starting transfers between devices, padded(): lax.ppermute(head, axis, [((i + 1) % count, i) for i in range(ends)])  38.5 us
    select_n x2, other arithmetic, per_device(): correction = jnp.take(second, flat_ids, axis=1).reshape(LABELS, CZ, CY, NX)  14.9 us
    ppermute x16, waiting for transfers between devices, padded(): lax.ppermute(head, axis, [((i + 1) % count, i) for i in range(ends)])  7.38 us
  transfers between devices with their start and end apart: 34, of which 22 were waited for; matrix products, arithmetic and copies ran while one was open for 2% of the time, Pallas kernels for 0%

commit v1 on v0

v1 whole, which is shorter than its diff:
```python
import math

import jax
import jax.numpy as jnp
from jax import lax
from jax.experimental import pallas as pl
from jax.experimental.pallas import tpu as pltpu
from jax.sharding import PartitionSpec as P

LABELS = 8
CYCLES = 2

prior_mass = 0.25
seed_weight = 4.0
smooth_step = 0.8
coarse_step = 0.7
weight_unit = 0.125

BOTH = ("slab", "row")
NEED = 5
VMEM_LIMIT = 60 * 1024 * 1024


def pairing(n_slab, n_row, axis, distance, phase):
    count = n_slab if axis == "slab" else n_row
    spare = n_row if axis == "slab" else n_slab
    pairs = []
    for s in range(n_slab):
        for r in range(n_row):
            i, other = (s, r) if axis == "slab" else (r, s)
            if (i // distance) % 2 == phase and i + distance < count:
                j, k = i + distance, other
            elif i >= distance and (i // distance - 1) % 2 == phase:
                j, k = i - distance, other
            elif spare % 2 == 0:
                j, k = i, other ^ 1
            else:
                continue
            target = (j, k) if axis == "slab" else (k, j)
            pairs.append((s * n_row + r, target[0] * n_row + target[1]))
    return pairs


def swap(block, axis, distance, phase):
    n_slab, n_row = lax.axis_size("slab"), lax.axis_size("row")
    return lax.ppermute(block, BOTH, pairing(n_slab, n_row, axis, distance, phase))


def vmem(count):
    return [pl.BlockSpec(memory_space=pltpu.VMEM)] * count


def params():
    return pltpu.CompilerParams(vmem_limit_bytes=VMEM_LIMIT)


class Shape:
    def __init__(self, edge_weights, coarse_blocks):
        self.cz, self.cy, self.nx = edge_weights.shape[1:]
        self.cc = coarse_blocks.shape[1]
        self.group = coarse_blocks.shape[2] // self.cc
        self.n_slab = lax.axis_size("slab")
        self.n_row = lax.axis_size("row")
        self.sections = self.n_slab // self.group
        self.reach = -(-(NEED + 1) // self.cz)
        self.oz = self.reach * self.cz
        self.planes = self.cz + 2 * self.oz
        self.rows = 3 * self.cy
        self.oy = self.cy

    def away(self, z):
        return -z if z < 0 else max(0, z - self.cz + 1)

    def strips(self):
        out, at = [], 0
        for z in range(-self.oz, self.cz + self.oz):
            take = NEED + 1 - self.away(z)
            if take > 0:
                out.append((z, at, take))
                at += take
        return out, -(-at // 8) * 8


def parity_of(index, distance):
    return (index // distance) % 2


def pack_kernel(shape, own_ref, *refs):
    recvs, (frame_ref, even_ref, odd_ref) = refs[:-3], refs[-3:]
    cz, oz = shape.cz, shape.oz
    slab = lax.axis_index("slab")
    row = lax.axis_index("row")
    for a in range(5):
        for z in range(cz):
            frame_ref[a, oz + z] = own_ref[a, z]
    for d in range(1, shape.reach + 1):
        first, second = recvs[2 * d - 2], recvs[2 * d - 1]
        par = parity_of(slab, d)

        def place(above, below, d=d):
            for a in range(5):
                for z in range(cz):
                    frame_ref[a, oz + d * cz + z] = above[a, z]
                    frame_ref[a, oz - d * cz + z] = below[a, z]

        @pl.when(par == 0)
        def _():
            place(first, second)

        @pl.when(par == 1)
        def _():
            place(second, first)

    strips, _ = shape.strips()

    def fill(last_ref, first_ref):
        for z, at, take in strips:
            for a in range(5):
                tile = frame_ref[a, oz + z]
                last_ref[a, at : at + take] = tile[shape.cy - take :]
                first_ref[a, at : at + take] = tile[:take]

    @pl.when(row % 2 == 0)
    def _():
        fill(even_ref, odd_ref)

    @pl.when(row % 2 == 1)
    def _():
        fill(odd_ref, even_ref)


def row_of(ref, z, y, count):
    return jnp.broadcast_to(ref[z, y : y + 1, :], (LABELS, count))


class Fields:
    def __init__(self, shape, wz, wy, wx, wxl, k, seeds):
        self.s = shape
        self.wz, self.wy, self.wx, self.wxl, self.k, self.seeds = wz, wy, wx, wxl, k, seeds
        self.lab = lax.broadcasted_iota(jnp.int32, (LABELS, shape.nx), 0)

    def region(self, layers, body):
        s = self.s
        for m in range(layers + 1):
            lo, hi = -(layers - m), s.cy + layers - m
            if m == 0:
                def inner(i, c, lo=lo, hi=hi):
                    body(i, lo, hi)
                    return c

                lax.fori_loop(0, s.cz, inner, 0)
            else:
                def inner(i, c, m=m, lo=lo, hi=hi):
                    body(jnp.where(i == 0, -m, s.cz - 1 + m), lo, hi)
                    return c

                lax.fori_loop(0, 2, inner, 0)

    def source(self, z, y):
        s = self.s
        seeds = row_of(self.seeds, z + s.oz, y + s.oy, s.nx)
        return jnp.where(seeds == self.lab, seed_weight, 0.0)

    def near_rows(self, src, pz, py, z, lo, hi, use):
        s = self.s
        zz = z + s.oz
        before = src[z + pz, lo - 1 + py]
        centre = src[z + pz, lo + py]
        w_before = row_of(self.wy, zz, lo - 1 + s.oy, s.nx)
        for y in range(lo, hi):
            yy = y + s.oy
            after = src[z + pz, y + 1 + py]
            w_after = row_of(self.wy, zz, yy, s.nx)
            near = row_of(self.wz, zz, yy, s.nx) * src[z + 1 + pz, y + py]
            near = near + row_of(self.wz, zz - 1, yy, s.nx) * src[z - 1 + pz, y + py]
            near = near + w_after * after + w_before * before
            near = near + row_of(self.wx, zz, yy, s.nx) * pltpu.roll(centre, s.nx - 1, axis=1)
            near = near + row_of(self.wxl, zz, yy, s.nx) * pltpu.roll(centre, 1, axis=1)
            use(y, centre, near)
            before, centre, w_before = centre, after, w_after

    def sweep(self, src, src_at, dst, dst_at, layers):
        s = self.s

        def body(z, lo, hi):
            def use(y, centre, near):
                k = row_of(self.k, z + s.oz, y + s.oy, s.nx)
                dst[z + dst_at[0], y + dst_at[1]] = (1.0 - smooth_step) * centre + k * (
                    self.source(z, y) + near
                )

            self.near_rows(src, *src_at, z, lo, hi, use)

        self.region(layers, body)

    def coarse_sums(self, src, src_at, diag, diag_z, owners, acc):
        s = self.s
        acc[...] = jnp.zeros_like(acc)
        cells = lax.broadcasted_iota(jnp.int32, (s.cc, s.nx), 0)

        def body(z, lo, hi):
            def use(y, centre, near):
                d = row_of(diag, z + diag_z, y + s.oy, s.nx)
                rest = self.source(z, y) - (d * centre - near)
                top = rest.astype(jnp.bfloat16).astype(jnp.float32)
                mid = (rest - top).astype(jnp.bfloat16).astype(jnp.float32)
                low = rest - top - mid
                parts = jnp.concatenate([top, mid, low], axis=0).astype(jnp.bfloat16)
                ids = jnp.broadcast_to(owners[z + s.oz, y + s.oy : y + s.oy + 1, :], (s.cc, s.nx))
                onehot = jnp.where(ids == cells, 1.0, 0.0).astype(jnp.bfloat16)
                acc[...] += lax.dot_general(
                    parts, onehot, (((1,), (1,)), ((), ())), preferred_element_type=jnp.float32
                )

            self.near_rows(src, *src_at, z, lo, hi, use)

        self.region(0, body)
        return acc[0:LABELS] + acc[LABELS : 2 * LABELS] + acc[2 * LABELS : 3 * LABELS]


def take(table, ids, shape):
    ids = jnp.broadcast_to(ids, (LABELS, shape.nx))
    parts = [
        jnp.take_along_axis(table, ids[:, i : i + shape.cc], axis=1, mode="promise_in_bounds")
        for i in range(0, shape.nx, shape.cc)
    ]
    return jnp.concatenate(parts, axis=1)


def own_diagonal(blocks_ref, shape):
    turn = lax.axis_index("slab") // shape.sections
    own = blocks_ref[:, pl.ds(pl.multiple_of(turn * shape.cc, shape.cc), shape.cc)]
    a = lax.broadcasted_iota(jnp.int32, own.shape, 0)
    b = lax.broadcasted_iota(jnp.int32, own.shape, 1)
    return jnp.sum(jnp.where(a == b, own, 0.0), axis=0, keepdims=True)


def down_kernel(shape, frame_ref, even_ref, odd_ref, blocks_ref, *refs):
    (wz, wy, wx, wxl, k, seeds, owners, diag, u2, rhs_ref, first_ref, ints, u1, acc) = refs
    s = shape
    slab = lax.axis_index("slab")
    row = lax.axis_index("row")
    cy, oy, oz = s.cy, s.oy, s.oz
    strips, _ = s.strips()

    def sides(below_ref, above_ref):
        for z, at, count in strips:
            for a in range(5):
                ints[a, oz + z, oy - count : oy] = below_ref[a, at : at + count]
                ints[a, oz + z, oy + cy : oy + cy + count] = above_ref[a, at : at + count]

    @pl.when(row % 2 == 0)
    def _():
        sides(odd_ref, even_ref)

    @pl.when(row % 2 == 1)
    def _():
        sides(even_ref, odd_ref)

    def prepare(i, lower_wz):
        for a in range(5):
            ints[a, i, oy : oy + cy] = frame_ref[a, i]
        plane = slab * s.cz + i - oz
        line = row * cy - oy + lax.broadcasted_iota(jnp.int32, (s.rows, s.nx), 0)
        column = lax.broadcasted_iota(jnp.int32, (s.rows, s.nx), 1)
        keep_plane = jnp.logical_and(plane != -1, plane != s.cz * s.n_slab - 1)
        keep_line = jnp.logical_and(line != -1, line != cy * s.n_row - 1)
        w_z = ints[0, i].astype(jnp.float32) * jnp.where(keep_plane, weight_unit, 0.0)
        w_y = jnp.where(keep_line, ints[1, i].astype(jnp.float32) * weight_unit, 0.0)
        w_x = jnp.where(column < s.nx - 1, ints[2, i].astype(jnp.float32) * weight_unit, 0.0)
        w_xl = pltpu.roll(w_x, 1, axis=1)
        seed = ints[3, i]
        d = (
            prior_mass
            + seed_weight * (seed >= 0).astype(jnp.float32)
            + w_z
            + w_y
            + w_x
            + lower_wz
            + pltpu.roll(w_y, 1, axis=0)
            + w_xl
        )
        wz[i] = w_z
        wy[i] = w_y
        wx[i] = w_x
        wxl[i] = w_xl
        k[i] = smooth_step / d
        diag[i] = d
        seeds[i] = seed
        owners[i] = ints[4, i]
        return w_z

    lax.fori_loop(0, s.planes, prepare, jnp.zeros((s.rows, s.nx), jnp.float32))
    fields = Fields(s, wz, wy, wx, wxl, k, seeds)
    at1 = (NEED, NEED)

    def start(z, lo, hi):
        for y in range(lo, hi):
            kk = row_of(k, z + oz, y + oy, s.nx)
            seed = row_of(seeds, z + oz, y + oy, s.nx)
            u1[z + at1[0], y + at1[1]] = jnp.where(seed == fields.lab, seed_weight * kk, 0.0)

    fields.region(NEED, start)
    at2 = (NEED - 1, NEED - 1)
    fields.sweep(u1, at1, u2, at2, NEED - 1)
    rhs = fields.coarse_sums(u2, at2, diag, oz, owners, acc)
    rhs_ref[...] = rhs
    first = coarse_step * rhs / own_diagonal(blocks_ref, s)
    for t in range(s.group):
        first_ref[t] = first


def coarse_kernel(shape, first_ref, rhs_ref, blocks_ref, second_ref):
    s = shape
    turn = lax.axis_index("slab") // s.sections
    mine = first_ref[turn]
    whole = jnp.concatenate([first_ref[t] for t in range(s.group)], axis=1)
    applied = lax.dot_general(
        whole,
        blocks_ref[...],
        (((1,), (1,)), ((), ())),
        precision=lax.Precision.HIGHEST,
        preferred_element_type=jnp.float32,
    )
    second = mine + coarse_step * (rhs_ref[...] - applied) / own_diagonal(blocks_ref, s)
    for i in range(second_ref.shape[0]):
        second_ref[i] = second


def middle_kernel(shape, second_ref, blocks_ref, wz, wy, wx, wxl, k, seeds, owners, diag, u2, *refs):
    (u5, rhs_ref, first_ref, u3, u4, acc) = refs
    s = shape
    slab = lax.axis_index("slab")
    row = lax.axis_index("row")
    fields = Fields(s, wz, wy, wx, wxl, k, seeds)
    layers = NEED - 1
    at2 = (layers, layers)

    def table(dz, dy):
        i = jnp.clip(slab + dz, 0, s.n_slab - 1) * s.n_row + jnp.clip(row + dy, 0, s.n_row - 1)
        return second_ref[i]

    def correct(z, lo, hi):
        dz = lax.div(z + s.oz, s.cz) - s.reach
        for dy in (-1, 0, 1):
            begin, end = max(lo, dy * s.cy), min(hi, (dy + 1) * s.cy)
            if begin >= end:
                continue
            tab = table(dz, dy)
            for y in range(begin, end):
                ids = owners[z + s.oz, y + s.oy : y + s.oy + 1, :]
                at = (z + at2[0], y + at2[1])
                u4[at] = u2[at] + take(tab, ids, s)

    fields.region(layers, correct)
    fields.sweep(u4, at2, u3, at2, layers - 1)
    fields.sweep(u3, at2, u4, at2, layers - 2)
    fields.sweep(u4, at2, u5, (1, 1), 1)
    rhs = fields.coarse_sums(u5, (1, 1), diag, s.oz, owners, acc)
    rhs_ref[...] = rhs
    first = coarse_step * rhs / own_diagonal(blocks_ref, s)
    for t in range(s.group):
        first_ref[t] = first


def last_kernel(shape, own_ref, z0, z1, y0, y1, wz, wy, wx, wxl, k, seeds, owners, u5, out_ref, u6):
    s = shape
    slab = lax.axis_index("slab")
    row = lax.axis_index("row")
    fields = Fields(s, wz, wy, wx, wxl, k, seeds)

    def pick(even, first, second):
        return jnp.where(even, first[0], second[0])

    up_z = pick(slab % 2 == 0, z0, z1)
    down_z = pick(slab % 2 == 0, z1, z0)
    up_y = pick(row % 2 == 0, y0, y1)
    down_y = pick(row % 2 == 0, y1, y0)

    def add(z, y, tab):
        ids = owners[z + s.oz, y + s.oy : y + s.oy + 1, :]
        u6[z + 1, y + 1] = u5[z + 1, y + 1] + take(tab, ids, s)

    own = own_ref[0]
    for y in range(s.cy):
        add(-1, y, down_z)
        add(s.cz, y, up_z)

    def plane(z, c):
        add(z, -1, down_y)
        add(z, s.cy, up_y)
        for y in range(s.cy):
            add(z, y, own)
        return c

    lax.fori_loop(0, s.cz, plane, 0)

    def body(z, lo, hi):
        def use(y, centre, near):
            kk = row_of(k, z + s.oz, y + s.oy, s.nx)
            out_ref[:, z, y, :] = (1.0 - smooth_step) * centre + kk * (fields.source(z, y) + near)

        fields.near_rows(u6, 1, 1, z, lo, hi, use)

    fields.region(0, body)


def f32(*dims):
    return jax.ShapeDtypeStruct(dims, jnp.float32)


def i32(*dims):
    return jax.ShapeDtypeStruct(dims, jnp.int32)


def per_device(edge_weights, seeds, supervoxel, coarse_blocks):
    import functools

    s = Shape(edge_weights, coarse_blocks)
    blocks = coarse_blocks[0]
    own = jnp.concatenate([edge_weights, seeds[None], supervoxel[None]], axis=0)
    recvs = [swap(own, "slab", d, ph) for d in range(1, s.reach + 1) for ph in (0, 1)]
    _, packed = s.strips()
    frame, even, odd = pl.pallas_call(
        functools.partial(pack_kernel, s),
        out_shape=(i32(5, s.planes, s.cy, s.nx), i32(5, packed, s.nx), i32(5, packed, s.nx)),
        in_specs=vmem(1 + len(recvs)),
        out_specs=tuple(vmem(3)),
        compiler_params=params(),
        name="pack",
    )(own, *recvs)
    even = swap(even, "row", 1, 0)
    odd = swap(odd, "row", 1, 1)
    plane = (s.planes, s.rows, s.nx)
    wide = 2 * (NEED - 1)
    *kept, u2, rhs, first = pl.pallas_call(
        functools.partial(down_kernel, s),
        out_shape=tuple(
            [f32(*plane)] * 5
            + [i32(*plane)] * 2
            + [f32(*plane), f32(s.cz + wide, s.cy + wide, LABELS, s.nx)]
            + [f32(LABELS, s.cc), f32(s.group, LABELS, s.cc)]
        ),
        in_specs=vmem(4),
        out_specs=tuple(vmem(11)),
        scratch_shapes=[
            pltpu.VMEM((5,) + plane, jnp.int32),
            pltpu.VMEM((s.cz + 2 * NEED, s.cy + 2 * NEED, LABELS, s.nx), jnp.float32),
            pltpu.VMEM((3 * LABELS, s.cc), jnp.float32),
        ],
        compiler_params=params(),
        name="down",
    )(frame, even, odd, blocks)
    diag = kept[7]

    groups = [[t * s.sections + g for t in range(s.group)] for g in range(s.sections)]

    def coarse(first, rhs, copies):
        gathered = lax.all_to_all(
            first, "slab", 0, 0, axis_index_groups=groups if s.sections > 1 else None, tiled=True
        )
        return pl.pallas_call(
            functools.partial(coarse_kernel, s),
            out_shape=f32(copies, LABELS, s.cc),
            in_specs=vmem(3),
            out_specs=vmem(1)[0],
            compiler_params=params(),
            name="coarse",
        )(gathered, rhs, blocks)

    second = coarse(first, rhs, s.n_slab * s.n_row)
    second = lax.all_to_all(second, BOTH, 0, 0, tiled=True)
    u5, rhs, first = pl.pallas_call(
        functools.partial(middle_kernel, s),
        out_shape=(
            f32(s.cz + 2, s.cy + 2, LABELS, s.nx),
            f32(LABELS, s.cc),
            f32(s.group, LABELS, s.cc),
        ),
        in_specs=vmem(11),
        out_specs=tuple(vmem(3)),
        scratch_shapes=[
            pltpu.VMEM((s.cz + wide, s.cy + wide, LABELS, s.nx), jnp.float32),
            pltpu.VMEM((s.cz + wide, s.cy + wide, LABELS, s.nx), jnp.float32),
            pltpu.VMEM((3 * LABELS, s.cc), jnp.float32),
        ],
        compiler_params=params(),
        name="middle",
    )(second, blocks, *kept[:7], diag, u2)
    second = coarse(first, rhs, 1)
    around = [swap(second, axis, 1, ph) for axis in ("slab", "row") for ph in (0, 1)]
    return pl.pallas_call(
        functools.partial(last_kernel, s),
        out_shape=f32(LABELS, s.cz, s.cy, s.nx),
        in_specs=vmem(13),
        out_specs=vmem(1)[0],
        scratch_shapes=[pltpu.VMEM((s.cz + 2, s.cy + 2, LABELS, s.nx), jnp.float32)],
        compiler_params=params(),
        name="last",
    )(second, *around, *kept[:7], u5)


def solution(mesh):
    in_specs = (
        P(None, "slab", "row", None),
        P("slab", "row", None),
        P("slab", "row", None),
        P("row", "slab", None),
    )
    out_specs = P(None, "slab", "row", None)
    return jax.shard_map(
        per_device, mesh=mesh, in_specs=in_specs, out_specs=out_specs, check_vma=False
    )
```

time: 298 us -> 103 us (0.35)
  the two profiles are of different devices: /device:TPU:6 before, /device:TPU:0 now
where the time goes in v1:
time: 103 us
  blocking collectives  33.6 us (33%)
  Pallas kernels  32.1 us (31%)
  waiting for transfers between devices  18.7 us (18%)
  starting transfers between devices  15.2 us (15%)
  local copies, waits for them, and re-layouts  2.07 us (2%)
    all_to_all x2, blocking collectives, coarse(): lax.all_to_all(first, 'slab', 0, 0, axis_index_groups=groups if s.section...  22.2 us
    ppermute x12, waiting for transfers between devices, swap(): lax.ppermute(block, BOTH, pairing(n_slab, n_row, axis, distance, phase))  18.7 us
    ppermute x12, starting transfers between devices, swap(): lax.ppermute(block, BOTH, pairing(n_slab, n_row, axis, distance, phase))  15.2 us
    all_to_all x1, blocking collectives, per_device(): second = lax.all_to_all(second, BOTH, 0, 0, tiled=True)  11.5 us
    pallas_call x1, Pallas kernels, per_device(): pl.pallas_call(functools.partial(middle_kernel, s), out_shape=(f32(s.cz +...  10.8 us
    pallas_call x1, Pallas kernels, per_device(): pl.pallas_call(functools.partial(down_kernel, s), out_shape=tuple([f32(*p...  9.75 us
    pallas_call x2, Pallas kernels, coarse(): pl.pallas_call(functools.partial(coarse_kernel, s), out_shape=f32(copies,...  4.43 us
    pallas_call x1, Pallas kernels, per_device(): pl.pallas_call(functools.partial(last_kernel, s), out_shape=f32(LABELS, s...  4.24 us
  transfers between devices with their start and end apart: 12, of which 6 were waited for; matrix products, arithmetic and copies ran while one was open for 0% of the time, Pallas kernels for 0%

profile of v1, /device:TPU:0, one launch (start us, length us, event | category | flops | bytes accessed | tf_op | source)
XLA Modules:
  0.0 102.8 jit_solution(15576146204804510423)
XLA Ops:
  0.0 0.9 pad_add_fusion.own_ref
  0.9 0.0 copy-start
  1.0 0.6 collective-permute-start.5
  1.5 6.0 %collective-permute-start.4 = (s32[5,2,8,512]{3,2,1,0:T(8,128)S(1)}, s32[5,2,8,512]{3,2,1,0:T(8,128)S(1)}, u32[]{:S(2)}, u32[]{:S(2)}) collective-permute-start(s32[5,2,8,512]{3,2,1,0:T(8,128)S(1)} %pad_add_fusion.own_ref), channel_id=1, source_target_pairs={{0,12},{1,13},{2,14},{3,15},{4,16},{5,17},{6,18},{7,19},{8,20},{9,... | collective-permute-start | bytes 491528 | tf_op jit(solution)/shard_map/ppermute | solution.py:46
  7.6 0.0 collective-permute-start.3
  7.6 0.6 collective-permute-start.2
  8.2 0.0 collective-permute-start.1
  8.2 0.0 collective-permute-done.5.refs_5_
  8.2 2.9 %collective-permute-start = (s32[5,2,8,512]{3,2,1,0:T(8,128)S(1)}, s32[5,2,8,512]{3,2,1,0:T(8,128)S(1)}, u32[]{:S(2)}, u32[]{:S(2)}) collective-permute-start(s32[5,2,8,512]{3,2,1,0:T(8,128)S(1)} %pad_add_fusion.own_ref), channel_id=1, source_target_pairs={{0,4},{1,5},{2,6},{3,7},{4,0},{5,1},{6,2},{7,3},{8,12},{9,13},{10,... | collective-permute-start | bytes 491528 | tf_op jit(solution)/shard_map/ppermute | solution.py:46
  11.1 2.3 %collective-permute-done.4.refs_4_ = s32[5,2,8,512]{3,2,1,0:T(8,128)S(1)} collective-permute-done((s32[5,2,8,512]{3,2,1,0:T(8,128)S(1)}, s32[5,2,8,512]{3,2,1,0:T(8,128)S(1)}, u32[]{:S(2)}, u32[]{:S(2)}) %collective-permute-start.4) | collective-permute-done | bytes 163872 | tf_op jit(solution)/shard_map/ppermute | solution.py:46
  13.3 0.0 collective-permute-done.3.refs_3_
  13.3 4.2 %collective-permute-done.2.refs_2_ = s32[5,2,8,512]{3,2,1,0:T(8,128)S(1)} collective-permute-done((s32[5,2,8,512]{3,2,1,0:T(8,128)S(1)}, s32[5,2,8,512]{3,2,1,0:T(8,128)S(1)}, u32[]{:S(2)}, u32[]{:S(2)}) %collective-permute-start.2) | collective-permute-done | bytes 163872 | tf_op jit(solution)/shard_map/ppermute | solution.py:46
  17.6 3.0 %collective-permute-done.refs_0_ = s32[5,2,8,512]{3,2,1,0:T(8,128)S(1)} collective-permute-done((s32[5,2,8,512]{3,2,1,0:T(8,128)S(1)}, s32[5,2,8,512]{3,2,1,0:T(8,128)S(1)}, u32[]{:S(2)}, u32[]{:S(2)}) %collective-permute-start) | collective-permute-done | bytes 163872 | tf_op jit(solution)/shard_map/ppermute | solution.py:46
  20.6 0.7 copy-done.8
  21.3 2.9 %pack.1 = (s32[5,14,8,512]{3,2,1,0:T(8,128)}, s32[5,48,512]{2,1,0:T(8,128)}, s32[5,48,512]{2,1,0:T(8,128)}) custom-call(s32[5,2,8,512]{3,2,1,0:T(8,128)} %copy-done, s32[5,2,8,512]{3,2,1,0:T(8,128)} %copy-done.8, s32[5,2,8,512]{3,2,1,0:T(8,128)} %copy-done.7, s32[5,2,8,512]{3,2,1,0:T(8,128)} %copy-done.6, s32[5,2,8,512]{3,2,1,0:T(8,128)} %copy-done.5, ...), custom_call_target="tpu_custom_call" | custom-call | tf_op jit(solution)/shard_map/pack/pallas_call | solution.py:424
  24.2 2.5 %collective-permute-start.7 = (s32[5,48,512]{2,1,0:T(8,128)}, s32[5,48,512]{2,1,0:T(8,128)S(1)}, u32[]{:S(2)}, u32[]{:S(2)}) collective-permute-start(s32[5,48,512]{2,1,0:T(8,128)} %get-tuple-element.24), channel_id=1, source_target_pairs={{0,4},{1,2},{2,1},{3,7},{4,0},{5,6},{6,5},{7,3},{8,12},{9,10},{10,... | collective-permute-start | bytes 1474568 | tf_op jit(solution)/shard_map/ppermute | solution.py:46
  26.7 7.0 %collective-permute-done.7.odd_ref = s32[5,48,512]{2,1,0:T(8,128)S(1)} collective-permute-done((s32[5,48,512]{2,1,0:T(8,128)}, s32[5,48,512]{2,1,0:T(8,128)S(1)}, u32[]{:S(2)}, u32[]{:S(2)}) %collective-permute-start.7) | collective-permute-done | bytes 491552 | tf_op jit(solution)/shard_map/ppermute | solution.py:46
  33.7 0.8 copy-done.2
  34.5 9.8 %down.1 = (f32[14,24,512]{2,1,0:T(8,128)}, f32[14,24,512]{2,1,0:T(8,128)}, f32[14,24,512]{2,1,0:T(8,128)}, f32[14,24,512]{2,1,0:T(8,128)}, f32[14,24,512]{2,1,0:...) custom-call(s32[5,14,8,512]{3,2,1,0:T(8,128)} %get-tuple-element.22., ...), custom_call_target="tpu_custom_call" | custom-call | tf_op jit(solution)/shard_map/down/pallas_call | solution.py:436
  44.3 11.5 %all_to_all.15.first_ref = f32[8,8,128]{2,1,0:T(8,128)} all-to-all(f32[8,8,128]{2,1,0:T(8,128)} %get-tuple-element.25), channel_id=1, replica_groups=mesh['slab'=8,'row'=4] {'slab'}, dimensions={0} | all-to-all | bytes 65536 | tf_op jit(solution)/shard_map/all_to_all | solution.py:459
  55.8 2.3 %coarse.2 = f32[32,8,128]{2,1,0:T(8,128)} custom-call(f32[8,8,128]{2,1,0:T(8,128)} %all_to_all.15.first_ref, f32[8,128]{1,0:T(8,128)} %get-tuple-element.26.rhs_ref, f32[128,1024]{1,0:T(8,128)} %bitcast.4), custom_call_target="tpu_custom_call" | custom-call | tf_op jit(solution)/shard_map/coarse/pallas_call | solution.py:462
  58.1 11.5 %all_to_all.16.second_ref = f32[32,8,128]{2,1,0:T(8,128)} all-to-all(f32[32,8,128]{2,1,0:T(8,128)} %coarse.2), channel_id=1, replica_groups=mesh['slab'=8,'row'=4] {'slab','row'}, dimensions={0} | all-to-all | bytes 262144 | tf_op jit(solution)/shard_map/all_to_all | solution.py:472
  69.5 10.8 %middle.1 = (f32[4,10,8,512]{3,2,1,0:T(8,128)}, f32[8,128]{1,0:T(8,128)}, f32[8,8,128]{2,1,0:T(8,128)}) custom-call(f32[32,8,128]{2,1,0:T(8,128)} %all_to_all.16.second_ref, f32[128,1024]{1,0:T(8,128)} %bitcast.5, f32[14,24,512]{2,1,0:T(8,128)} %get-tuple-element.27.wz, f32[14,24,512]{2,1,0:T(8,128)} %get-tuple-element.28.wy, ...), custom_call_target="tpu_custom_call" | custom-call | tf_op jit(solution)/shard_map/middle/pallas_call | solution.py:473
  80.3 10.6 %all_to_all.17.first_ref = f32[8,8,128]{2,1,0:T(8,128)} all-to-all(f32[8,8,128]{2,1,0:T(8,128)} %get-tuple-element.36), channel_id=1, replica_groups=mesh['slab'=8,'row'=4] {'slab'}, dimensions={0} | all-to-all | bytes 65536 | tf_op jit(solution)/shard_map/all_to_all | solution.py:459
  90.9 2.2 %coarse.3.own_ref = f32[1,8,128]{2,1,0:T(8,128)} custom-call(f32[8,8,128]{2,1,0:T(8,128)} %all_to_all.17.first_ref, f32[8,128]{1,0:T(8,128)} %get-tuple-element.37.rhs_ref, f32[128,1024]{1,0:T(8,128)} %bitcast.6), custom_call_target="tpu_custom_call" | custom-call | tf_op jit(solution)/shard_map/coarse/pallas_call | solution.py:462
  93.1 0.5 collective-permute-start.11
  93.6 0.5 collective-permute-start.9
  94.1 1.7 %collective-permute-start.8 = (f32[1,8,128]{2,1,0:T(8,128)}, f32[1,8,128]{2,1,0:T(8,128)S(1)}, u32[]{:S(2)}, u32[]{:S(2)}) collective-permute-start(f32[1,8,128]{2,1,0:T(8,128)} %coarse.3.own_ref), channel_id=1, source_target_pairs={{0,4},{1,5},{2,6},{3,7},{4,0},{5,1},{6,2},{7,3},{8,12},{9,13},{10,... | collective-permute-start | bytes 12296 | tf_op jit(solution)/shard_map/ppermute | solution.py:46
  95.8 1.2 %collective-permute-done.11.y1 = f32[1,8,128]{2,1,0:T(8,128)S(1)} collective-permute-done((f32[1,8,128]{2,1,0:T(8,128)}, f32[1,8,128]{2,1,0:T(8,128)S(1)}, u32[]{:S(2)}, u32[]{:S(2)}) %collective-permute-start.11) | collective-permute-done | bytes 4128 | tf_op jit(solution)/shard_map/ppermute | solution.py:46
  97.0 1.0 collective-permute-done.8.z0
  97.9 0.6 copy-done.12
  98.5 4.2 %last.1 = f32[8,2,8,512]{3,2,1,0:T(8,128)} custom-call(f32[1,8,128]{2,1,0:T(8,128)} %coarse.3.own_ref, f32[1,8,128]{2,1,0:T(8,128)} %copy-done.12, f32[1,8,128]{2,1,0:T(8,128)} %copy-done.11, f32[1,8,128]{2,1,0:T(8,128)} %copy-done.10, f32[1,8,128]{2,1,0:T(8,128)} %copy-done.9, f32[14,24,512]{2,1,0:T(8,128)} %get-tuple-element.27.wz, ...), custom_call_target="tpu_custom_call" | custom-call | tf_op jit(solution)/shard_map/last/pallas_call | solution.py:492
  (28 shorter events, 0.1 us)
Async XLA Ops:
  0.9 19.7 %copy-start = (s32[5,2,8,512]{3,2,1,0:T(8,128)}, s32[5,2,8,512]{3,2,1,0:T(8,128)S(1)}, u32[]{:S(2)}) copy-start(s32[5,2,8,512]{3,2,1,0:T(8,128)S(1)} %pad_add_fusion.own_ref) | copy-start | bytes 491524
  1.0 7.2 %collective-permute-start.5 = (s32[5,2,8,512]{3,2,1,0:T(8,128)S(1)}, s32[5,2,8,512]{3,2,1,0:T(8,128)S(1)}, u32[]{:S(2)}, u32[]{:S(2)}) collective-permute-start(s32[5,2,8,512]{3,2,1,0:T(8,128)S(1)} %pad_add_fusion.own_ref), channel_id=1, source_target_pairs={{0,1},{1,0},{2,3},{3,2},{4,5},{5,4},{6,7},{7,6},{8,9},{9,8},{10,11... | collective-permute-start | bytes 491528 | tf_op jit(solution)/shard_map/ppermute | solution.py:46
  1.5 11.8 %collective-permute-start.4 = (s32[5,2,8,512]{3,2,1,0:T(8,128)S(1)}, s32[5,2,8,512]{3,2,1,0:T(8,128)S(1)}, u32[]{:S(2)}, u32[]{:S(2)}) collective-permute-start(s32[5,2,8,512]{3,2,1,0:T(8,128)S(1)} %pad_add_fusion.own_ref), channel_id=1, source_target_pairs={{0,12},{1,13},{2,14},{3,15},{4,16},{5,17},{6,18},{7,19},{8,20},{9,... | collective-permute-start | bytes 491528 | tf_op jit(solution)/shard_map/ppermute | solution.py:46
  7.6 5.8 %collective-permute-start.3 = (s32[5,2,8,512]{3,2,1,0:T(8,128)S(1)}, s32[5,2,8,512]{3,2,1,0:T(8,128)S(1)}, u32[]{:S(2)}, u32[]{:S(2)}) collective-permute-start(s32[5,2,8,512]{3,2,1,0:T(8,128)S(1)} %pad_add_fusion.own_ref), channel_id=1, source_target_pairs={{0,1},{1,0},{2,3},{3,2},{4,5},{5,4},{6,7},{7,6},{8,16},{9,17},{10,... | collective-permute-start | bytes 491528 | tf_op jit(solution)/shard_map/ppermute | solution.py:46
  7.6 10.0 %collective-permute-start.2 = (s32[5,2,8,512]{3,2,1,0:T(8,128)S(1)}, s32[5,2,8,512]{3,2,1,0:T(8,128)S(1)}, u32[]{:S(2)}, u32[]{:S(2)}) collective-permute-start(s32[5,2,8,512]{3,2,1,0:T(8,128)S(1)} %pad_add_fusion.own_ref), channel_id=1, source_target_pairs={{0,8},{1,9},{2,10},{3,11},{4,12},{5,13},{6,14},{7,15},{8,0},{9,1},... | collective-permute-start | bytes 491528 | tf_op jit(solution)/shard_map/ppermute | solution.py:46
  8.2 9.4 %collective-permute-start.1 = (s32[5,2,8,512]{3,2,1,0:T(8,128)S(1)}, s32[5,2,8,512]{3,2,1,0:T(8,128)S(1)}, u32[]{:S(2)}, u32[]{:S(2)}) collective-permute-start(s32[5,2,8,512]{3,2,1,0:T(8,128)S(1)} %pad_add_fusion.own_ref), channel_id=1, source_target_pairs={{0,1},{1,0},{2,3},{3,2},{4,8},{5,9},{6,10},{7,11},{8,4},{9,5},{10,... | collective-permute-start | bytes 491528 | tf_op jit(solution)/shard_map/ppermute | solution.py:46
  8.2 12.4 %copy-start.3 = (s32[5,2,8,512]{3,2,1,0:T(8,128)}, s32[5,2,8,512]{3,2,1,0:T(8,128)S(1)}, u32[]{:S(2)}) copy-start(s32[5,2,8,512]{3,2,1,0:T(8,128)S(1)} %collective-permute-done.5.refs_5_) | copy-start | bytes 491524
  8.2 12.4 %collective-permute-start = (s32[5,2,8,512]{3,2,1,0:T(8,128)S(1)}, s32[5,2,8,512]{3,2,1,0:T(8,128)S(1)}, u32[]{:S(2)}, u32[]{:S(2)}) collective-permute-start(s32[5,2,8,512]{3,2,1,0:T(8,128)S(1)} %pad_add_fusion.own_ref), channel_id=1, source_target_pairs={{0,4},{1,5},{2,6},{3,7},{4,0},{5,1},{6,2},{7,3},{8,12},{9,13},{10,... | collective-permute-start | bytes 491528 | tf_op jit(solution)/shard_map/ppermute | solution.py:46
  13.3 7.3 %copy-start.4 = (s32[5,2,8,512]{3,2,1,0:T(8,128)}, s32[5,2,8,512]{3,2,1,0:T(8,128)S(1)}, u32[]{:S(2)}) copy-start(s32[5,2,8,512]{3,2,1,0:T(8,128)S(1)} %collective-permute-done.4.refs_4_) | copy-start | bytes 491524
  13.3 7.3 %copy-start.5 = (s32[5,2,8,512]{3,2,1,0:T(8,128)}, s32[5,2,8,512]{3,2,1,0:T(8,128)S(1)}, u32[]{:S(2)}) copy-start(s32[5,2,8,512]{3,2,1,0:T(8,128)S(1)} %collective-permute-done.3.refs_3_) | copy-start | bytes 491524
  17.6 3.0 %copy-start.6 = (s32[5,2,8,512]{3,2,1,0:T(8,128)}, s32[5,2,8,512]{3,2,1,0:T(8,128)S(1)}, u32[]{:S(2)}) copy-start(s32[5,2,8,512]{3,2,1,0:T(8,128)S(1)} %collective-permute-done.2.refs_2_) | copy-start | bytes 491524
  17.6 3.0 %copy-start.7 = (s32[5,2,8,512]{3,2,1,0:T(8,128)}, s32[5,2,8,512]{3,2,1,0:T(8,128)S(1)}, u32[]{:S(2)}) copy-start(s32[5,2,8,512]{3,2,1,0:T(8,128)S(1)} %collective-permute-done.1.refs_1_) | copy-start | bytes 491524
  20.6 0.7 copy-start.8
  24.2 2.5 %collective-permute-start.6 = (s32[5,48,512]{2,1,0:T(8,128)}, s32[5,48,512]{2,1,0:T(8,128)S(1)}, u32[]{:S(2)}, u32[]{:S(2)}) collective-permute-start(s32[5,48,512]{2,1,0:T(8,128)} %get-tuple-element.23), channel_id=1, source_target_pairs={{0,1},{1,0},{2,3},{3,2},{4,5},{5,4},{6,7},{7,6},{8,9},{9,8},{10,11... | collective-permute-start | bytes 1474568 | tf_op jit(solution)/shard_map/ppermute | solution.py:46
  24.2 9.5 %collective-permute-start.7 = (s32[5,48,512]{2,1,0:T(8,128)}, s32[5,48,512]{2,1,0:T(8,128)S(1)}, u32[]{:S(2)}, u32[]{:S(2)}) collective-permute-start(s32[5,48,512]{2,1,0:T(8,128)} %get-tuple-element.24), channel_id=1, source_target_pairs={{0,4},{1,2},{2,1},{3,7},{4,0},{5,6},{6,5},{7,3},{8,12},{9,10},{10,... | collective-permute-start | bytes 1474568 | tf_op jit(solution)/shard_map/ppermute | solution.py:46
  26.7 7.0 %copy-start.1 = (s32[5,48,512]{2,1,0:T(8,128)}, s32[5,48,512]{2,1,0:T(8,128)S(1)}, u32[]{:S(2)}) copy-start(s32[5,48,512]{2,1,0:T(8,128)S(1)} %collective-permute-done.6.even_ref) | copy-start | bytes 1474564
  33.7 0.8 copy-start.2
  93.1 3.8 %collective-permute-start.11 = (f32[1,8,128]{2,1,0:T(8,128)}, f32[1,8,128]{2,1,0:T(8,128)S(1)}, u32[]{:S(2)}, u32[]{:S(2)}) collective-permute-start(f32[1,8,128]{2,1,0:T(8,128)} %coarse.3.own_ref), channel_id=1, source_target_pairs={{0,4},{1,2},{2,1},{3,7},{4,0},{5,6},{6,5},{7,3},{8,12},{9,10},{10,... | collective-permute-start | bytes 12296 | tf_op jit(solution)/shard_map/ppermute | solution.py:46
  93.6 3.3 %collective-permute-start.10 = (f32[1,8,128]{2,1,0:T(8,128)}, f32[1,8,128]{2,1,0:T(8,128)S(1)}, u32[]{:S(2)}, u32[]{:S(2)}) collective-permute-start(f32[1,8,128]{2,1,0:T(8,128)} %coarse.3.own_ref), channel_id=1, source_target_pairs={{0,1},{1,0},{2,3},{3,2},{4,5},{5,4},{6,7},{7,6},{8,9},{9,8},{10,11... | collective-permute-start | bytes 12296 | tf_op jit(solution)/shard_map/ppermute | solution.py:46
  93.6 3.3 %collective-permute-start.9 = (f32[1,8,128]{2,1,0:T(8,128)}, f32[1,8,128]{2,1,0:T(8,128)S(1)}, u32[]{:S(2)}, u32[]{:S(2)}) collective-permute-start(f32[1,8,128]{2,1,0:T(8,128)} %coarse.3.own_ref), channel_id=1, source_target_pairs={{0,1},{1,0},{2,3},{3,2},{4,8},{5,9},{6,10},{7,11},{8,4},{9,5},{10,... | collective-permute-start | bytes 12296 | tf_op jit(solution)/shard_map/ppermute | solution.py:46
  94.1 3.8 %collective-permute-start.8 = (f32[1,8,128]{2,1,0:T(8,128)}, f32[1,8,128]{2,1,0:T(8,128)S(1)}, u32[]{:S(2)}, u32[]{:S(2)}) collective-permute-start(f32[1,8,128]{2,1,0:T(8,128)} %coarse.3.own_ref), channel_id=1, source_target_pairs={{0,4},{1,5},{2,6},{3,7},{4,0},{5,1},{6,2},{7,3},{8,12},{9,13},{10,... | collective-permute-start | bytes 12296 | tf_op jit(solution)/shard_map/ppermute | solution.py:46
  96.9 1.0 copy-start.9
  96.9 1.0 copy-start.10
  97.0 1.0 copy-start.11
  97.9 0.6 copy-start.12

commit v2 on v1

--- a/solution.py
+++ b/solution.py
@@ -18,7 +18,7 @@
 
 BOTH = ("slab", "row")
 NEED = 5
-VMEM_LIMIT = 60 * 1024 * 1024
+VMEM_LIMIT = 24 * 1024 * 1024
 
 
 def pairing(n_slab, n_row, axis, distance, phase):

time: 103 us -> 81 us (0.79)
  Pallas kernels: 32.1 us -> 14.8 us
  blocking collectives: 33.6 us -> 30.2 us
    pallas_call x1, Pallas kernels: 9.75 us -> 5.22 us  [per_device(): pl.pallas_call(functools.partial(down_kernel, s), out_shape=tuple([f32(*p...]
    pallas_call x1, Pallas kernels: 10.8 us -> 6.54 us  [per_device(): pl.pallas_call(functools.partial(middle_kernel, s), out_shape=(f32(s.cz +...]
    pallas_call x2, Pallas kernels: 4.43 us -> 1.05 us  [coarse(): pl.pallas_call(functools.partial(coarse_kernel, s), out_shape=f32(copies,...]
    pallas_call x1, Pallas kernels: 2.91 us -> 0.28 us  [per_device(): pl.pallas_call(functools.partial(pack_kernel, s), out_shape=(i32(5, s.pla...]
    pallas_call x1, Pallas kernels: 4.24 us -> 1.69 us  [per_device(): pl.pallas_call(functools.partial(last_kernel, s), out_shape=f32(LABELS, s...]
    all_to_all x2, blocking collectives: 22.2 us -> 20.3 us  [coarse(): lax.all_to_all(first, 'slab', 0, 0, axis_index_groups=groups if s.section...]
    all_to_all x1, blocking collectives: 11.5 us -> 9.91 us  [per_device(): second = lax.all_to_all(second, BOTH, 0, 0, tiled=True)]
    unnamed x26 -> x4, local copies, waits for them, and re-layouts: 2.07 us -> 1.05 us
where the time goes in v2:
time: 81 us; the launch traced here: 80.8 us
  blocking collectives  30.2 us (37%)
  waiting for transfers between devices  18.3 us (23%)
  starting transfers between devices  15.4 us (19%)
  Pallas kernels  14.8 us (18%)
  local copies, waits for them, and re-layouts  1.05 us (1%)
  other arithmetic  1 us (1%)
    all_to_all x2, blocking collectives, coarse(): lax.all_to_all(first, 'slab', 0, 0, axis_index_groups=groups if s.section...  20.3 us
    ppermute x12, waiting for transfers between devices, swap(): lax.ppermute(block, BOTH, pairing(n_slab, n_row, axis, distance, phase))  18.3 us
    ppermute x12, starting transfers between devices, swap(): lax.ppermute(block, BOTH, pairing(n_slab, n_row, axis, distance, phase))  15.4 us
    all_to_all x1, blocking collectives, per_device(): second = lax.all_to_all(second, BOTH, 0, 0, tiled=True)  9.91 us
    pallas_call x1, Pallas kernels, per_device(): pl.pallas_call(functools.partial(middle_kernel, s), out_shape=(f32(s.cz +...  6.54 us
    pallas_call x1, Pallas kernels, per_device(): pl.pallas_call(functools.partial(down_kernel, s), out_shape=tuple([f32(*p...  5.22 us
    pallas_call x1, Pallas kernels, per_device(): pl.pallas_call(functools.partial(last_kernel, s), out_shape=f32(LABELS, s...  1.69 us
  transfers between devices with their start and end apart: 12, of which 6 were waited for; matrix products, arithmetic and copies ran while one was open for 0% of the time, Pallas kernels for 0%

profile of v2, /device:TPU:0, one launch (start us, length us, event | category | flops | bytes accessed | tf_op | source)
XLA Modules:
  0.0 80.8 jit_solution(13210168013955031165)
XLA Ops:
  0.0 1.0 %pad_add_fusion.own_ref = s32[5,2,8,512]{3,2,1,0:T(8,128)S(1)} fusion(s32[1,2,8,512]{3,2,1,0:T(8,128)} %bitcast.7, s32[1,2,8,512]{3,2,1,0:T(8,128)} %bitcast.8, s32[3,2,8,512]{3,2,1,0:T(8,128)} %param.4), kind=kLoop, calls=%fused_computation | loop fusion | flops 81920 | bytes 327680 | tf_op jit(solution)/shard_map/concatenate | solution.py:421
  1.0 0.6 collective-permute-start.5
  1.6 6.0 %collective-permute-start.4 = (s32[5,2,8,512]{3,2,1,0:T(8,128)S(1)}, s32[5,2,8,512]{3,2,1,0:T(8,128)S(1)}, u32[]{:S(2)}, u32[]{:S(2)}) collective-permute-start(s32[5,2,8,512]{3,2,1,0:T(8,128)S(1)} %pad_add_fusion.own_ref), channel_id=1, source_target_pairs={{0,12},{1,13},{2,14},{3,15},{4,16},{5,17},{6,18},{7,19},{8,20},{9,... | collective-permute-start | bytes 491528 | tf_op jit(solution)/shard_map/ppermute | solution.py:46
  7.6 0.0 collective-permute-start.3
  7.6 0.6 collective-permute-start.2
  8.2 0.0 collective-permute-start.1
  8.2 0.0 collective-permute-done.5.refs_5_
  8.2 2.9 %collective-permute-start = (s32[5,2,8,512]{3,2,1,0:T(8,128)S(1)}, s32[5,2,8,512]{3,2,1,0:T(8,128)S(1)}, u32[]{:S(2)}, u32[]{:S(2)}) collective-permute-start(s32[5,2,8,512]{3,2,1,0:T(8,128)S(1)} %pad_add_fusion.own_ref), channel_id=1, source_target_pairs={{0,4},{1,5},{2,6},{3,7},{4,0},{5,1},{6,2},{7,3},{8,12},{9,13},{10,... | collective-permute-start | bytes 491528 | tf_op jit(solution)/shard_map/ppermute | solution.py:46
  11.1 2.3 %collective-permute-done.4.refs_4_ = s32[5,2,8,512]{3,2,1,0:T(8,128)S(1)} collective-permute-done((s32[5,2,8,512]{3,2,1,0:T(8,128)S(1)}, s32[5,2,8,512]{3,2,1,0:T(8,128)S(1)}, u32[]{:S(2)}, u32[]{:S(2)}) %collective-permute-start.4) | collective-permute-done | bytes 163872 | tf_op jit(solution)/shard_map/ppermute | solution.py:46
  13.4 0.0 collective-permute-done.3.refs_3_
  13.4 4.3 %collective-permute-done.2.refs_2_ = s32[5,2,8,512]{3,2,1,0:T(8,128)S(1)} collective-permute-done((s32[5,2,8,512]{3,2,1,0:T(8,128)S(1)}, s32[5,2,8,512]{3,2,1,0:T(8,128)S(1)}, u32[]{:S(2)}, u32[]{:S(2)}) %collective-permute-start.2) | collective-permute-done | bytes 163872 | tf_op jit(solution)/shard_map/ppermute | solution.py:46
  17.6 0.0 collective-permute-done.1.refs_1_
  17.6 3.0 %collective-permute-done.refs_0_ = s32[5,2,8,512]{3,2,1,0:T(8,128)S(1)} collective-permute-done((s32[5,2,8,512]{3,2,1,0:T(8,128)S(1)}, s32[5,2,8,512]{3,2,1,0:T(8,128)S(1)}, u32[]{:S(2)}, u32[]{:S(2)}) %collective-permute-start) | collective-permute-done | bytes 163872 | tf_op jit(solution)/shard_map/ppermute | solution.py:46
  20.6 0.3 pack.1
  20.9 0.1 collective-permute-start.6
  21.0 2.5 %collective-permute-start.7 = (s32[5,48,512]{2,1,0:T(8,128)S(1)}, s32[5,48,512]{2,1,0:T(8,128)S(1)}, u32[]{:S(2)}, u32[]{:S(2)}) collective-permute-start(s32[5,48,512]{2,1,0:T(8,128)S(1)} %get-tuple-element.24), channel_id=1, source_target_pairs={{0,4},{1,2},{2,1},{3,7},{4,0},{5,6},{6,5},{7,3},{8,12},{9,10},{10,... | collective-permute-start | bytes 1474568 | tf_op jit(solution)/shard_map/ppermute | solution.py:46
  23.6 6.8 %collective-permute-done.7.odd_ref = s32[5,48,512]{2,1,0:T(8,128)S(1)} collective-permute-done((s32[5,48,512]{2,1,0:T(8,128)S(1)}, s32[5,48,512]{2,1,0:T(8,128)S(1)}, u32[]{:S(2)}, u32[]{:S(2)}) %collective-permute-start.7) | collective-permute-done | bytes 491552 | tf_op jit(solution)/shard_map/ppermute | solution.py:46
  30.4 1.0 %copy-done = f32[1,128,1024]{2,1,0:T(8,128)S(1)} copy-done((f32[1,128,1024]{2,1,0:T(8,128)S(1)}, f32[1,128,1024]{2,1,0:T(8,128)}, u32[]{:S(2)}) %copy-start) | copy-done | bytes 524312
  31.4 5.2 %down.1 = (f32[14,24,512]{2,1,0:T(8,128)S(1)}, f32[14,24,512]{2,1,0:T(8,128)S(1)}, f32[14,24,512]{2,1,0:T(8,128)S(1)}, f32[14,24,512]{2,1,0:T(8,128)S(1)}, f32[1...) custom-call(s32[5,14,8,512]{3,2,1,0:T(8,128)S(1)} %get-tuple-element, ...), custom_call_target="tpu_custom_call" | custom-call | tf_op jit(solution)/shard_map/down/pallas_call | solution.py:436
  36.6 11.2 %all_to_all.15.first_ref = f32[8,8,128]{2,1,0:T(8,128)S(1)} all-to-all(f32[8,8,128]{2,1,0:T(8,128)S(1)} %get-tuple-element.25), channel_id=1, replica_groups=mesh['slab'=8,'row'=4] {'slab'}, dimensions={0} | all-to-all | bytes 65536 | tf_op jit(solution)/shard_map/all_to_all | solution.py:459
  47.9 0.5 coarse.2
  48.4 9.9 %all_to_all.16.second_ref = f32[32,8,128]{2,1,0:T(8,128)S(1)} all-to-all(f32[32,8,128]{2,1,0:T(8,128)S(1)} %coarse.2), channel_id=1, replica_groups=mesh['slab'=8,'row'=4] {'slab','row'}, dimensions={0} | all-to-all | bytes 262144 | tf_op jit(solution)/shard_map/all_to_all | solution.py:472
  58.3 6.5 %middle.1 = (f32[4,10,8,512]{3,2,1,0:T(8,128)S(1)}, f32[8,128]{1,0:T(8,128)S(1)}, f32[8,8,128]{2,1,0:T(8,128)S(1)}) custom-call(f32[32,8,128]{2,1,0:T(8,128)S(1)} %all_to_all.16.second_ref, f32[128,1024]{1,0:T(8,128)S(1)} %bitcast.5, f32[14,24,512]{2,1,0:T(8,128)S(1)} %get-tuple-element.27.wz, f32[14,24,512]{2,1,0:T(8,128)S(1)} %get-tuple-element.28.wy, ...), custom_call_target="tpu_custom_call" | custom-call | tf_op jit(solution)/shard_map/middle/pallas_call | solution.py:473
  64.9 9.1 %all_to_all.17.first_ref = f32[8,8,128]{2,1,0:T(8,128)S(1)} all-to-all(f32[8,8,128]{2,1,0:T(8,128)S(1)} %get-tuple-element.36), channel_id=1, replica_groups=mesh['slab'=8,'row'=4] {'slab'}, dimensions={0} | all-to-all | bytes 65536 | tf_op jit(solution)/shard_map/all_to_all | solution.py:459
  74.0 0.5 coarse.3.own_ref
  74.5 0.5 collective-permute-start.11
  75.0 0.4 collective-permute-start.10
  75.3 0.2 collective-permute-start.9
  75.5 1.7 %collective-permute-start.8 = (f32[1,8,128]{2,1,0:T(8,128)S(1)}, f32[1,8,128]{2,1,0:T(8,128)S(1)}, u32[]{:S(2)}, u32[]{:S(2)}) collective-permute-start(f32[1,8,128]{2,1,0:T(8,128)S(1)} %coarse.3.own_ref), channel_id=1, source_target_pairs={{0,4},{1,5},{2,6},{3,7},{4,0},{5,1},{6,2},{7,3},{8,12},{9,13},{10,... | collective-permute-start | bytes 12296 | tf_op jit(solution)/shard_map/ppermute | solution.py:46
  77.2 0.9 %collective-permute-done.11.y1 = f32[1,8,128]{2,1,0:T(8,128)S(1)} collective-permute-done((f32[1,8,128]{2,1,0:T(8,128)S(1)}, f32[1,8,128]{2,1,0:T(8,128)S(1)}, u32[]{:S(2)}, u32[]{:S(2)}) %collective-permute-start.11) | collective-permute-done | bytes 4128 | tf_op jit(solution)/shard_map/ppermute | solution.py:46
  78.1 1.0 %collective-permute-done.8.z0 = f32[1,8,128]{2,1,0:T(8,128)S(1)} collective-permute-done((f32[1,8,128]{2,1,0:T(8,128)S(1)}, f32[1,8,128]{2,1,0:T(8,128)S(1)}, u32[]{:S(2)}, u32[]{:S(2)}) %collective-permute-start.8) | collective-permute-done | bytes 4128 | tf_op jit(solution)/shard_map/ppermute | solution.py:46
  79.1 1.7 %last.1 = f32[8,2,8,512]{3,2,1,0:T(8,128)} custom-call(f32[1,8,128]{2,1,0:T(8,128)S(1)} %coarse.3.own_ref, f32[1,8,128]{2,1,0:T(8,128)S(1)} %collective-permute-done.8.z0, f32[1,8,128]{2,1,0:T(8,128)S(1)} %collective-permute-done.9.z1, f32[1,8,128]{2,1,0:T(8,128)S(1)} %collective-permute-done.10.y0, f32[1,8,128]{2,1,0:T(8,128)S(1)} %collective-permute-done.11.y1, ...), custom_call_target="tpu_custom_call" | custom-call | tf_op jit(solution)/shard_map/last/pallas_call | solution.py:492
  (6 shorter events, 0.0 us)
Async XLA Ops:
  0.0 58.3 %copy-start.1 = (f32[1,128,1024]{2,1,0:T(8,128)S(1)}, f32[1,128,1024]{2,1,0:T(8,128)}, u32[]{:S(2)}) copy-start(f32[1,128,1024]{2,1,0:T(8,128)} %param.7) | copy-start | bytes 1572868
  1.0 7.2 %collective-permute-start.5 = (s32[5,2,8,512]{3,2,1,0:T(8,128)S(1)}, s32[5,2,8,512]{3,2,1,0:T(8,128)S(1)}, u32[]{:S(2)}, u32[]{:S(2)}) collective-permute-start(s32[5,2,8,512]{3,2,1,0:T(8,128)S(1)} %pad_add_fusion.own_ref), channel_id=1, source_target_pairs={{0,1},{1,0},{2,3},{3,2},{4,5},{5,4},{6,7},{7,6},{8,9},{9,8},{10,11... | collective-permute-start | bytes 491528 | tf_op jit(solution)/shard_map/ppermute | solution.py:46
  1.6 11.8 %collective-permute-start.4 = (s32[5,2,8,512]{3,2,1,0:T(8,128)S(1)}, s32[5,2,8,512]{3,2,1,0:T(8,128)S(1)}, u32[]{:S(2)}, u32[]{:S(2)}) collective-permute-start(s32[5,2,8,512]{3,2,1,0:T(8,128)S(1)} %pad_add_fusion.own_ref), channel_id=1, source_target_pairs={{0,12},{1,13},{2,14},{3,15},{4,16},{5,17},{6,18},{7,19},{8,20},{9,... | collective-permute-start | bytes 491528 | tf_op jit(solution)/shard_map/ppermute | solution.py:46
  7.6 5.8 %collective-permute-start.3 = (s32[5,2,8,512]{3,2,1,0:T(8,128)S(1)}, s32[5,2,8,512]{3,2,1,0:T(8,128)S(1)}, u32[]{:S(2)}, u32[]{:S(2)}) collective-permute-start(s32[5,2,8,512]{3,2,1,0:T(8,128)S(1)} %pad_add_fusion.own_ref), channel_id=1, source_target_pairs={{0,1},{1,0},{2,3},{3,2},{4,5},{5,4},{6,7},{7,6},{8,16},{9,17},{10,... | collective-permute-start | bytes 491528 | tf_op jit(solution)/shard_map/ppermute | solution.py:46
  7.6 10.0 %collective-permute-start.2 = (s32[5,2,8,512]{3,2,1,0:T(8,128)S(1)}, s32[5,2,8,512]{3,2,1,0:T(8,128)S(1)}, u32[]{:S(2)}, u32[]{:S(2)}) collective-permute-start(s32[5,2,8,512]{3,2,1,0:T(8,128)S(1)} %pad_add_fusion.own_ref), channel_id=1, source_target_pairs={{0,8},{1,9},{2,10},{3,11},{4,12},{5,13},{6,14},{7,15},{8,0},{9,1},... | collective-permute-start | bytes 491528 | tf_op jit(solution)/shard_map/ppermute | solution.py:46
  8.2 9.4 %collective-permute-start.1 = (s32[5,2,8,512]{3,2,1,0:T(8,128)S(1)}, s32[5,2,8,512]{3,2,1,0:T(8,128)S(1)}, u32[]{:S(2)}, u32[]{:S(2)}) collective-permute-start(s32[5,2,8,512]{3,2,1,0:T(8,128)S(1)} %pad_add_fusion.own_ref), channel_id=1, source_target_pairs={{0,1},{1,0},{2,3},{3,2},{4,8},{5,9},{6,10},{7,11},{8,4},{9,5},{10,... | collective-permute-start | bytes 491528 | tf_op jit(solution)/shard_map/ppermute | solution.py:46
  8.2 12.4 %collective-permute-start = (s32[5,2,8,512]{3,2,1,0:T(8,128)S(1)}, s32[5,2,8,512]{3,2,1,0:T(8,128)S(1)}, u32[]{:S(2)}, u32[]{:S(2)}) collective-permute-start(s32[5,2,8,512]{3,2,1,0:T(8,128)S(1)} %pad_add_fusion.own_ref), channel_id=1, source_target_pairs={{0,4},{1,5},{2,6},{3,7},{4,0},{5,1},{6,2},{7,3},{8,12},{9,13},{10,... | collective-permute-start | bytes 491528 | tf_op jit(solution)/shard_map/ppermute | solution.py:46
  20.9 2.6 %collective-permute-start.6 = (s32[5,48,512]{2,1,0:T(8,128)S(1)}, s32[5,48,512]{2,1,0:T(8,128)S(1)}, u32[]{:S(2)}, u32[]{:S(2)}) collective-permute-start(s32[5,48,512]{2,1,0:T(8,128)S(1)} %get-tuple-element.23), channel_id=1, source_target_pairs={{0,1},{1,0},{2,3},{3,2},{4,5},{5,4},{6,7},{7,6},{8,9},{9,8},{10,11... | collective-permute-start | bytes 1474568 | tf_op jit(solution)/shard_map/ppermute | solution.py:46
  21.0 9.4 %collective-permute-start.7 = (s32[5,48,512]{2,1,0:T(8,128)S(1)}, s32[5,48,512]{2,1,0:T(8,128)S(1)}, u32[]{:S(2)}, u32[]{:S(2)}) collective-permute-start(s32[5,48,512]{2,1,0:T(8,128)S(1)} %get-tuple-element.24), channel_id=1, source_target_pairs={{0,4},{1,2},{2,1},{3,7},{4,0},{5,6},{6,5},{7,3},{8,12},{9,10},{10,... | collective-permute-start | bytes 1474568 | tf_op jit(solution)/shard_map/ppermute | solution.py:46
  30.4 1.0 %copy-start = (f32[1,128,1024]{2,1,0:T(8,128)S(1)}, f32[1,128,1024]{2,1,0:T(8,128)}, u32[]{:S(2)}) copy-start(f32[1,128,1024]{2,1,0:T(8,128)} %param.7) | copy-start | bytes 1572868
  74.5 3.6 %collective-permute-start.11 = (f32[1,8,128]{2,1,0:T(8,128)S(1)}, f32[1,8,128]{2,1,0:T(8,128)S(1)}, u32[]{:S(2)}, u32[]{:S(2)}) collective-permute-start(f32[1,8,128]{2,1,0:T(8,128)S(1)} %coarse.3.own_ref), channel_id=1, source_target_pairs={{0,4},{1,2},{2,1},{3,7},{4,0},{5,6},{6,5},{7,3},{8,12},{9,10},{10,... | collective-permute-start | bytes 12296 | tf_op jit(solution)/shard_map/ppermute | solution.py:46
  75.0 3.1 %collective-permute-start.10 = (f32[1,8,128]{2,1,0:T(8,128)S(1)}, f32[1,8,128]{2,1,0:T(8,128)S(1)}, u32[]{:S(2)}, u32[]{:S(2)}) collective-permute-start(f32[1,8,128]{2,1,0:T(8,128)S(1)} %coarse.3.own_ref), channel_id=1, source_target_pairs={{0,1},{1,0},{2,3},{3,2},{4,5},{5,4},{6,7},{7,6},{8,9},{9,8},{10,11... | collective-permute-start | bytes 12296 | tf_op jit(solution)/shard_map/ppermute | solution.py:46
  75.3 2.8 %collective-permute-start.9 = (f32[1,8,128]{2,1,0:T(8,128)S(1)}, f32[1,8,128]{2,1,0:T(8,128)S(1)}, u32[]{:S(2)}, u32[]{:S(2)}) collective-permute-start(f32[1,8,128]{2,1,0:T(8,128)S(1)} %coarse.3.own_ref), channel_id=1, source_target_pairs={{0,1},{1,0},{2,3},{3,2},{4,8},{5,9},{6,10},{7,11},{8,4},{9,5},{10,... | collective-permute-start | bytes 12296 | tf_op jit(solution)/shard_map/ppermute | solution.py:46
  75.5 3.6 %collective-permute-start.8 = (f32[1,8,128]{2,1,0:T(8,128)S(1)}, f32[1,8,128]{2,1,0:T(8,128)S(1)}, u32[]{:S(2)}, u32[]{:S(2)}) collective-permute-start(f32[1,8,128]{2,1,0:T(8,128)S(1)} %coarse.3.own_ref), channel_id=1, source_target_pairs={{0,4},{1,5},{2,6},{3,7},{4,0},{5,1},{6,2},{7,3},{8,12},{9,13},{10,... | collective-permute-start | bytes 12296 | tf_op jit(solution)/shard_map/ppermute | solution.py:46

commit v3 on v2

v3 whole, which is shorter than its diff:
```python
import functools

import jax
import jax.numpy as jnp
from jax import lax
from jax.experimental import pallas as pl
from jax.experimental.pallas import tpu as pltpu
from jax.sharding import PartitionSpec as P

LABELS = 8
ARRAYS = 5

prior_mass = 0.25
seed_weight = 4.0
smooth_step = 0.8
coarse_step = 0.7
weight_unit = 0.125

BOTH = ("slab", "row")
NEED = 5
VMEM_LIMIT = 24 * 1024 * 1024


def pairing(n_slab, n_row, axis, distance, phase):
    count = n_slab if axis == "slab" else n_row
    spare = n_row if axis == "slab" else n_slab
    pairs = []
    for s in range(n_slab):
        for r in range(n_row):
            i, other = (s, r) if axis == "slab" else (r, s)
            if (i // distance) % 2 == phase and i + distance < count:
                j, k = i + distance, other
            elif i >= distance and (i // distance - 1) % 2 == phase:
                j, k = i - distance, other
            elif spare % 2 == 0:
                j, k = i, other ^ 1
            else:
                continue
            target = (j, k) if axis == "slab" else (k, j)
            pairs.append((s * n_row + r, target[0] * n_row + target[1]))
    return pairs


def swap(block, axis, distance, phase):
    n_slab, n_row = lax.axis_size("slab"), lax.axis_size("row")
    return lax.ppermute(block, BOTH, pairing(n_slab, n_row, axis, distance, phase))


def vmem(count):
    return [pl.BlockSpec(memory_space=pltpu.VMEM)] * count


def params():
    return pltpu.CompilerParams(vmem_limit_bytes=VMEM_LIMIT)


class Shape:
    def __init__(self, edge_weights, coarse_blocks):
        self.cz, self.cy, self.nx = edge_weights.shape[1:]
        self.cc = coarse_blocks.shape[1]
        self.group = coarse_blocks.shape[2] // self.cc
        self.n_slab = lax.axis_size("slab")
        self.n_row = lax.axis_size("row")
        self.sections = self.n_slab // self.group
        self.reach = -(-(NEED + 1) // self.cz)
        self.oz = self.reach * self.cz
        self.planes = self.cz + 2 * self.oz
        self.rows = 3 * self.cy
        self.oy = self.cy
        full = ARRAYS * self.cz
        self.partial = [
            d for d in range(1, self.reach + 1) if min(map(len, self.plane_items(d))) < full
        ]

    def away(self, z):
        return -z if z < 0 else max(0, z - self.cz + 1)

    def needed(self, z):
        base = NEED - self.away(z)
        next_plane = 1 if z < 0 else 0
        below = (base + next_plane, base + 1, base, base, base - 1)
        above = (base + next_plane, base, base, base, base - 1)
        return [(max(-1, lo), max(-1, hi)) for lo, hi in zip(below, above)]

    def plane_items(self, distance):
        items = [(a, z) for a in range(ARRAYS) for z in range(self.cz)]
        shift = distance * self.cz
        up = [(a, z) for a, z in items if self.wanted(a, z - shift) >= 0]
        down = [(a, z) for a, z in items if self.wanted(a, z + shift) >= 0]
        return up, down

    def wanted(self, a, z):
        base = NEED - self.away(z)
        return (base + (1 if z < 0 else 0), base, base, base, base - 1)[a]

    def row_items(self, side):
        out, at = [], 0
        for z in range(-self.oz, self.cz + self.oz):
            for a, counts in enumerate(self.needed(z)):
                if counts[side] > 0:
                    out.append((a, z, at, counts[side]))
                    at += counts[side]
        return out, at


def parity_of(index, distance):
    return (index // distance) % 2


def start_kernel(shape, edge_ref, seeds_ref, owners_ref, blocks_in, own_ref, blocks_ref, *refs):
    sems = refs[-1]
    cz = shape.cz
    copies = [
        pltpu.make_async_copy(source, own_ref.at[pl.ds(a * cz, cz)], sems.at[a])
        for a, source in enumerate([edge_ref.at[0], edge_ref.at[1], edge_ref.at[2], seeds_ref, owners_ref])
    ]
    fetch = pltpu.make_async_copy(blocks_in, blocks_ref, sems.at[ARRAYS])
    for copy in copies:
        copy.start()
    fetch.start()
    for copy in copies:
        copy.wait()
    slab = lax.axis_index("slab")
    for i, d in enumerate(shape.partial):
        first_ref, second_ref = refs[2 * i], refs[2 * i + 1]
        up, down = shape.plane_items(d)

        def fill(up_ref, down_ref, up=up, down=down):
            for items, ref in ((up, up_ref), (down, down_ref)):
                for n in range(ref.shape[0]):
                    a, z = items[min(n, len(items) - 1)]
                    ref[n] = own_ref[a * cz + z]

        @pl.when(parity_of(slab, d) == 0)
        def _():
            fill(first_ref, second_ref)

        @pl.when(parity_of(slab, d) == 1)
        def _():
            fill(second_ref, first_ref)

    fetch.wait()


def pack_kernel(shape, own_ref, blocks_ref, *refs):
    recvs, (frame_ref, even_ref, odd_ref, dc_ref) = refs[:-4], refs[-4:]
    cz, oz = shape.cz, shape.oz
    slab = lax.axis_index("slab")
    row = lax.axis_index("row")
    for a in range(ARRAYS):
        for z in range(cz):
            frame_ref[a, oz + z] = own_ref[a * cz + z]
    for d in range(1, shape.reach + 1):
        first, second = recvs[2 * d - 2], recvs[2 * d - 1]
        up, down = shape.plane_items(d)

        def place(above, below, d=d, up=up, down=down):
            for n, (a, z) in enumerate(down):
                frame_ref[a, oz + d * cz + z] = above[n]
            for n, (a, z) in enumerate(up):
                frame_ref[a, oz - d * cz + z] = below[n]

        @pl.when(parity_of(slab, d) == 0)
        def _():
            place(first, second)

        @pl.when(parity_of(slab, d) == 1)
        def _():
            place(second, first)

    def fill(last_ref, first_ref):
        for a, z, at, count in shape.row_items(0)[0]:
            last_ref[at : at + count] = frame_ref[a, oz + z, shape.cy - count :]
        for a, z, at, count in shape.row_items(1)[0]:
            first_ref[at : at + count] = frame_ref[a, oz + z, :count]

    @pl.when(row % 2 == 0)
    def _():
        fill(even_ref, odd_ref)

    @pl.when(row % 2 == 1)
    def _():
        fill(odd_ref, even_ref)

    turn = slab // shape.sections
    block = blocks_ref[:, pl.ds(pl.multiple_of(turn * shape.cc, shape.cc), shape.cc)]
    a = lax.broadcasted_iota(jnp.int32, block.shape, 0)
    b = lax.broadcasted_iota(jnp.int32, block.shape, 1)
    dc_ref[...] = jnp.sum(jnp.where(a == b, block, 0.0), axis=0, keepdims=True)


def row_of(ref, z, y, count):
    return jnp.broadcast_to(ref[z, y : y + 1, :], (LABELS, count))


class Fields:
    def __init__(self, shape, faces, u1):
        self.s, self.faces, self.u1 = shape, faces, u1

    def region(self, layers, body):
        s = self.s
        for m in range(layers + 1):
            lo, hi = -(layers - m), s.cy + layers - m

            def inner(i, c, m=m, lo=lo, hi=hi):
                body(i if m == 0 else jnp.where(i == 0, -m, s.cz - 1 + m), lo, hi)
                return c

            lax.fori_loop(0, s.cz if m == 0 else 2, inner, 0)

    def moved_rows(self, src, at, z, lo, hi, use):
        s = self.s
        zz, z, z1 = z + s.oz, z + at, z + NEED
        before = src[z, lo - 1 + at]
        centre = src[z, lo + at]
        for y in range(lo, hi):
            above_z, below_z, above_y, below_y, above_x, below_x = [
                row_of(face, zz, y + s.oy, s.nx) for face in self.faces
            ]
            after = src[z, y + 1 + at]
            total = above_x * pltpu.roll(centre, s.nx - 1, axis=1)
            total += below_x * pltpu.roll(centre, 1, axis=1)
            total += above_y * after + below_y * before
            total += above_z * src[z + 1, y + at] + below_z * src[z - 1, y + at]
            use(y, centre, total + self.u1[z1, y + NEED])
            before, centre = centre, after

    def sweep(self, src, src_at, dst, dst_at, layers):
        def body(z, lo, hi):
            def use(y, centre, total):
                dst[z + dst_at, y + dst_at] = (1.0 - smooth_step) * centre + total

            self.moved_rows(src, src_at, z, lo, hi, use)

        self.region(layers, body)

    def coarse_sums(self, src, src_at, scale, owners, acc):
        s = self.s
        acc[...] = jnp.zeros_like(acc)
        cells = lax.broadcasted_iota(jnp.int32, (s.cc, s.nx), 0)

        def body(z, lo, hi):
            def use(y, centre, total):
                rest = row_of(scale, z, y + s.oy, s.nx) * (total - smooth_step * centre)
                top = rest.astype(jnp.bfloat16).astype(jnp.float32)
                mid = (rest - top).astype(jnp.bfloat16).astype(jnp.float32)
                low = rest - top - mid
                parts = jnp.concatenate([top, mid, low], axis=0).astype(jnp.bfloat16)
                ids = jnp.broadcast_to(owners[z + s.oz, y + s.oy : y + s.oy + 1, :], (s.cc, s.nx))
                onehot = jnp.where(ids == cells, 1.0, 0.0).astype(jnp.bfloat16)
                acc[...] += lax.dot_general(
                    parts, onehot, (((1,), (1,)), ((), ())), preferred_element_type=jnp.float32
                )

            self.moved_rows(src, src_at, z, lo, hi, use)

        self.region(0, body)
        return acc[0:LABELS] + acc[LABELS : 2 * LABELS] + acc[2 * LABELS : 3 * LABELS]


def take(table, ids, shape):
    ids = jnp.broadcast_to(ids, (LABELS, shape.nx))
    numbers = lax.GatherDimensionNumbers(
        offset_dims=(),
        collapsed_slice_dims=(1,),
        start_index_map=(1,),
        operand_batching_dims=(0,),
        start_indices_batching_dims=(0,),
    )
    parts = [
        lax.gather(
            table,
            ids[:, i : i + shape.cc, None],
            numbers,
            (1, 1),
            mode=lax.GatherScatterMode.PROMISE_IN_BOUNDS,
        )
        for i in range(0, shape.nx, shape.cc)
    ]
    return jnp.concatenate(parts, axis=1)


def down_kernel(shape, frame_ref, even_ref, odd_ref, dc_ref, *refs):
    faces, (u1, owners, scale, u2, rhs_ref, first_ref, kept, ints, acc) = refs[:6], refs[6:]
    s = shape
    slab = lax.axis_index("slab")
    row = lax.axis_index("row")
    cz, cy, oy, oz = s.cz, s.cy, s.oy, s.oz

    def sides(below_ref, above_ref):
        for a, z, at, count in s.row_items(0)[0]:
            ints[a, oz + z, oy - count : oy] = below_ref[at : at + count]
        for a, z, at, count in s.row_items(1)[0]:
            ints[a, oz + z, oy + cy : oy + cy + count] = above_ref[at : at + count]

    @pl.when(row % 2 == 0)
    def _():
        sides(odd_ref, even_ref)

    @pl.when(row % 2 == 1)
    def _():
        sides(even_ref, odd_ref)

    labels = lax.broadcasted_iota(jnp.int32, (LABELS, s.nx), 0)
    line = row * cy - oy + lax.broadcasted_iota(jnp.int32, (s.rows, s.nx), 0)
    column = lax.broadcasted_iota(jnp.int32, (s.rows, s.nx), 1)
    inside_y = jnp.logical_and(line >= 0, line < cy * s.n_row)
    unit_y = jnp.where(jnp.logical_and(line != -1, line != cy * s.n_row - 1), weight_unit, 0.0)
    unit_x = jnp.where(column < s.nx - 1, weight_unit, 0.0)

    def weights_z(i):
        plane = slab * cz + i - oz
        inside = jnp.logical_and(plane != -1, plane != cz * s.n_slab - 1)
        return ints[0, i].astype(jnp.float32) * jnp.where(inside, weight_unit, 0.0)

    def prepare(i, below_z):
        for a in range(ARRAYS):
            ints[a, i, oy : oy + cy] = frame_ref[a, i]
        w_z = weights_z(i)
        w_y = ints[1, i].astype(jnp.float32) * unit_y
        w_x = ints[2, i].astype(jnp.float32) * unit_x
        below_y = pltpu.roll(w_y, 1, axis=0)
        below_x = pltpu.roll(w_x, 1, axis=1)
        seeded = jnp.where(ints[3, i] >= 0, seed_weight + prior_mass, prior_mass)
        d = seeded + w_z + w_y + w_x + below_z + below_y + below_x
        plane = slab * cz + i - oz
        inside_z = jnp.logical_and(plane >= 0, plane < cz * s.n_slab)
        inside = jnp.logical_and(inside_y, inside_z)
        k = jnp.where(inside, smooth_step / d, 0.0)
        for face, w in zip(faces, (w_z, below_z, w_y, below_y, w_x, below_x)):
            face[i] = k * w
        kept[i] = seed_weight * k
        owners[i] = jnp.where(inside, ints[4, i], 0)

        @pl.when(jnp.logical_and(i >= oz, i < oz + cz))
        def _():
            scale[jnp.clip(i - oz, 0, cz - 1)] = d / smooth_step

        return w_z

    ints[0, 0, oy : oy + cy] = frame_ref[0, 0]
    lax.fori_loop(1, s.planes - 1, prepare, weights_z(0))
    fields = Fields(s, faces, u1)

    def start(z, lo, hi):
        for y in range(lo, hi):
            seed = jnp.broadcast_to(ints[3, z + oz, y + oy : y + oy + 1, :], (LABELS, s.nx))
            value = row_of(kept, z + oz, y + oy, s.nx)
            u1[z + NEED, y + NEED] = jnp.where(seed == labels, value, 0.0)

    fields.region(NEED, start)
    fields.sweep(u1, NEED, u2, NEED - 1, NEED - 1)
    rhs = fields.coarse_sums(u2, NEED - 1, scale, owners, acc)
    rhs_ref[...] = rhs
    first = coarse_step * rhs / dc_ref[...]
    for t in range(s.group):
        first_ref[t] = first


def coarse_kernel(shape, first_ref, rhs_ref, blocks_ref, dc_ref, second_ref):
    s = shape
    turn = lax.axis_index("slab") // s.sections
    mine = first_ref[turn]
    whole = jnp.concatenate([first_ref[t] for t in range(s.group)], axis=1)
    applied = lax.dot_general(
        whole,
        blocks_ref[...],
        (((1,), (1,)), ((), ())),
        precision=lax.Precision.HIGHEST,
        preferred_element_type=jnp.float32,
    )
    second = mine + coarse_step * (rhs_ref[...] - applied) / dc_ref[...]
    for i in range(second_ref.shape[0]):
        second_ref[i] = second


def middle_kernel(shape, second_ref, dc_ref, *refs):
    faces, (u1, owners, scale, u2, u5, rhs_ref, first_ref, u3, u4, acc) = refs[:6], refs[6:]
    s = shape
    slab = lax.axis_index("slab")
    row = lax.axis_index("row")
    fields = Fields(s, faces, u1)
    layers = NEED - 1

    def table(dz, dy):
        i = jnp.clip(slab + dz, 0, s.n_slab - 1) * s.n_row + jnp.clip(row + dy, 0, s.n_row - 1)
        return second_ref[i]

    def correct(z, lo, hi):
        dz = lax.div(z + s.oz, s.cz) - s.reach
        for dy in (-1, 0, 1):
            begin, end = max(lo, dy * s.cy), min(hi, (dy + 1) * s.cy)
            if begin >= end:
                continue
            tab = table(dz, dy)
            for y in range(begin, end):
                ids = owners[z + s.oz, y + s.oy : y + s.oy + 1, :]
                at = (z + layers, y + layers)
                u4[at] = u2[at] + take(tab, ids, s)

    fields.region(layers, correct)
    fields.sweep(u4, layers, u3, layers, layers - 1)
    fields.sweep(u3, layers, u4, layers, layers - 2)
    fields.sweep(u4, layers, u5, 1, 1)
    rhs = fields.coarse_sums(u5, 1, scale, owners, acc)
    rhs_ref[...] = rhs
    first = coarse_step * rhs / dc_ref[...]
    for t in range(s.group):
        first_ref[t] = first


def last_kernel(shape, own_ref, z0, z1, y0, y1, *refs):
    faces, (u1, owners, u5, out_ref, u6) = refs[:6], refs[6:]
    s = shape
    slab = lax.axis_index("slab")
    row = lax.axis_index("row")
    fields = Fields(s, faces, u1)

    def pick(even, first, second):
        return jnp.where(even, first[0], second[0])

    up_z = pick(slab % 2 == 0, z0, z1)
    down_z = pick(slab % 2 == 0, z1, z0)
    up_y = pick(row % 2 == 0, y0, y1)
    down_y = pick(row % 2 == 0, y1, y0)

    def add(z, y, tab):
        ids = owners[z + s.oz, y + s.oy : y + s.oy + 1, :]
        u6[z + 1, y + 1] = u5[z + 1, y + 1] + take(tab, ids, s)

    own = own_ref[0]
    for y in range(s.cy):
        add(-1, y, down_z)
        add(s.cz, y, up_z)

    def plane(z, c):
        add(z, -1, down_y)
        add(z, s.cy, up_y)
        for y in range(s.cy):
            add(z, y, own)
        return c

    lax.fori_loop(0, s.cz, plane, 0)

    def body(z, lo, hi):
        def use(y, centre, total):
            out_ref[:, z, y, :] = (1.0 - smooth_step) * centre + total

        fields.moved_rows(u6, 1, z, lo, hi, use)

    fields.region(0, body)


def f32(*dims):
    return jax.ShapeDtypeStruct(dims, jnp.float32)


def i32(*dims):
    return jax.ShapeDtypeStruct(dims, jnp.int32)


def per_device(edge_weights, seeds, supervoxel, coarse_blocks):
    s = Shape(edge_weights, coarse_blocks)
    messages = []
    for d in s.partial:
        count = max(len(items) for items in s.plane_items(d))
        messages += [i32(count, s.cy, s.nx)] * 2
    own, blocks, *messages = pl.pallas_call(
        functools.partial(start_kernel, s),
        out_shape=tuple(
            [i32(ARRAYS * s.cz, s.cy, s.nx), f32(*coarse_blocks.shape[1:])] + messages
        ),
        in_specs=[pl.BlockSpec(memory_space=pltpu.HBM)] * 4,
        out_specs=tuple(vmem(2 + len(messages))),
        scratch_shapes=[pltpu.SemaphoreType.DMA((ARRAYS + 1,))],
        compiler_params=params(),
        name="start",
    )(*[pltpu.with_memory_space_constraint(x, pltpu.HBM) for x in (edge_weights, seeds, supervoxel, coarse_blocks[0])])
    recvs = []
    for d in range(1, s.reach + 1):
        for ph in (0, 1):
            sent = messages[2 * s.partial.index(d) + ph] if d in s.partial else own
            recvs.append(swap(sent, "slab", d, ph))
    rows = -(-max(s.row_items(0)[1], s.row_items(1)[1]) // 8) * 8
    frame, even, odd, dc = pl.pallas_call(
        functools.partial(pack_kernel, s),
        out_shape=(
            i32(ARRAYS, s.planes, s.cy, s.nx),
            i32(rows, s.nx),
            i32(rows, s.nx),
            f32(1, s.cc),
        ),
        in_specs=vmem(2 + len(recvs)),
        out_specs=tuple(vmem(4)),
        compiler_params=params(),
        name="pack",
    )(own, blocks, *recvs)
    even = swap(even, "row", 1, 0)
    odd = swap(odd, "row", 1, 1)
    plane = (s.planes, s.rows, s.nx)
    wide = 2 * (NEED - 1)
    *faces, u1, owners, scale, u2, rhs, first = pl.pallas_call(
        functools.partial(down_kernel, s),
        out_shape=tuple(
            [f32(*plane)] * 6
            + [f32(s.cz + 2 * NEED, s.cy + 2 * NEED, LABELS, s.nx), i32(*plane)]
            + [f32(s.cz, s.rows, s.nx), f32(s.cz + wide, s.cy + wide, LABELS, s.nx)]
            + [f32(LABELS, s.cc), f32(s.group, LABELS, s.cc)]
        ),
        in_specs=vmem(4),
        out_specs=tuple(vmem(12)),
        scratch_shapes=[
            pltpu.VMEM(plane, jnp.float32),
            pltpu.VMEM((ARRAYS,) + plane, jnp.int32),
            pltpu.VMEM((3 * LABELS, s.cc), jnp.float32),
        ],
        compiler_params=params(),
        name="down",
    )(frame, even, odd, dc)

    groups = [[t * s.sections + g for t in range(s.group)] for g in range(s.sections)]

    def coarse(first, rhs, copies):
        gathered = lax.all_to_all(
            first, "slab", 0, 0, axis_index_groups=groups if s.sections > 1 else None, tiled=True
        )
        return pl.pallas_call(
            functools.partial(coarse_kernel, s),
            out_shape=f32(copies, LABELS, s.cc),
            in_specs=vmem(4),
            out_specs=vmem(1)[0],
            compiler_params=params(),
            name="coarse",
        )(gathered, rhs, blocks, dc)

    second = coarse(first, rhs, s.n_slab * s.n_row)
    second = lax.all_to_all(second, BOTH, 0, 0, tiled=True)
    u5, rhs, first = pl.pallas_call(
        functools.partial(middle_kernel, s),
        out_shape=(
            f32(s.cz + 2, s.cy + 2, LABELS, s.nx),
            f32(LABELS, s.cc),
            f32(s.group, LABELS, s.cc),
        ),
        in_specs=vmem(12),
        out_specs=tuple(vmem(3)),
        scratch_shapes=[
            pltpu.VMEM((s.cz + wide, s.cy + wide, LABELS, s.nx), jnp.float32),
            pltpu.VMEM((s.cz + wide, s.cy + wide, LABELS, s.nx), jnp.float32),
            pltpu.VMEM((3 * LABELS, s.cc), jnp.float32),
        ],
        compiler_params=params(),
        name="middle",
    )(second, dc, *faces, u1, owners, scale, u2)
    second = coarse(first, rhs, 1)
    around = [swap(second, axis, 1, ph) for axis in ("slab", "row") for ph in (0, 1)]
    return pl.pallas_call(
        functools.partial(last_kernel, s),
        out_shape=f32(LABELS, s.cz, s.cy, s.nx),
        in_specs=vmem(14),
        out_specs=vmem(1)[0],
        scratch_shapes=[pltpu.VMEM((s.cz + 2, s.cy + 2, LABELS, s.nx), jnp.float32)],
        compiler_params=params(),
        name="last",
    )(second, *around, *faces, u1, owners, u5)


def solution(mesh):
    in_specs = (
        P(None, "slab", "row", None),
        P("slab", "row", None),
        P("slab", "row", None),
        P("row", "slab", None),
    )
    out_specs = P(None, "slab", "row", None)
    return jax.shard_map(
        per_device, mesh=mesh, in_specs=in_specs, out_specs=out_specs, check_vma=False
    )
```

time: 81 us -> 74.6 us (0.921)
  waiting for transfers between devices: 18.3 us -> 14 us
  starting transfers between devices: 15.4 us -> 12.9 us
  blocking collectives: 30.2 us -> 31.6 us
  local copies, waits for them, and re-layouts: 1.05 us -> 0 us
  Pallas kernels: 14.8 us -> 15.8 us
  other arithmetic: 1 us -> 0 us
    ppermute x12, waiting for transfers between devices: 18.3 us -> 14 us  [swap(): lax.ppermute(block, BOTH, pairing(n_slab, n_row, axis, distance, phase))]
    ppermute x12, starting transfers between devices: 15.4 us -> 12.9 us  [swap(): lax.ppermute(block, BOTH, pairing(n_slab, n_row, axis, distance, phase))]
    all_to_all x2, blocking collectives: 20.3 us -> 21.7 us  [coarse(): lax.all_to_all(first, 'slab', 0, 0, axis_index_groups=groups if s.section...]
    pallas_call x1 -> x2, Pallas kernels: 0.28 us -> 1.49 us  [the longest x1 1.19 us: per_device(): pl.pallas_call(functools.partial(start_kernel, s), out_shape=tuple([i32(A...]
    unnamed x4 -> x0, local copies, waits for them, and re-layouts: 1.05 us -> none
    concatenate x1 -> x0, other arithmetic: 1 us -> none  [per_device(): own = jnp.concatenate([edge_weights, seeds[None], supervoxel[None]], axis=0)]
where the time goes in v3:
time: 74.6 us; the launch traced here: 74.4 us
  blocking collectives  31.6 us (42%)
  Pallas kernels  15.8 us (21%)
  waiting for transfers between devices  14 us (19%)
  starting transfers between devices  12.9 us (17%)
    all_to_all x2, blocking collectives, coarse(): lax.all_to_all(first, 'slab', 0, 0, axis_index_groups=groups if s.section...  21.7 us
    ppermute x12, waiting for transfers between devices, swap(): lax.ppermute(block, BOTH, pairing(n_slab, n_row, axis, distance, phase))  14 us
    ppermute x12, starting transfers between devices, swap(): lax.ppermute(block, BOTH, pairing(n_slab, n_row, axis, distance, phase))  12.9 us
    all_to_all x1, blocking collectives, per_device(): second = lax.all_to_all(second, BOTH, 0, 0, tiled=True)  9.91 us
    pallas_call x1, Pallas kernels, per_device(): pl.pallas_call(functools.partial(middle_kernel, s), out_shape=(f32(s.cz +...  6.54 us
    pallas_call x1, Pallas kernels, per_device(): pl.pallas_call(functools.partial(down_kernel, s), out_shape=tuple([f32(*p...  5.02 us
    pallas_call x1, Pallas kernels, per_device(): pl.pallas_call(functools.partial(last_kernel, s), out_shape=f32(LABELS, s...  1.69 us
  transfers between devices with their start and end apart: 12, of which 6 were waited for; matrix products, arithmetic and copies ran while one was open for 0% of the time, Pallas kernels for 0%

profile of v3, /device:TPU:0, one launch (start us, length us, event | category | flops | bytes accessed | tf_op | source)
XLA Modules:
  0.0 74.4 jit_solution(2374313415844626788)
XLA Ops:
  0.0 1.2 %start.1 = (s32[10,8,512]{2,1,0:T(8,128)S(1)}, f32[128,1024]{1,0:T(8,128)S(1)}, s32[5,8,512]{2,1,0:T(8,128)S(1)}, s32[5,8,512]{2,1,0:T(8,128)S(1)}) custom-call(s32[3,2,8,512]{3,2,1,0:T(8,128)} %edge_ref.1, s32[2,8,512]{2,1,0:T(8,128)} %seeds_ref.1, s32[2,8,512]{2,1,0:T(8,128)} %owners_ref.1, f32[128,1024]{1,0:T(8,128)} %bitcast.1), custom_call_target="tpu_custom_call" | custom-call | tf_op jit(solution)/shard_map/start/pallas_call | solution.py:468
  1.2 4.0 %collective-permute-start.4 = (s32[5,8,512]{2,1,0:T(8,128)S(1)}, s32[5,8,512]{2,1,0:T(8,128)S(1)}, u32[]{:S(2)}, u32[]{:S(2)}) collective-permute-start(s32[5,8,512]{2,1,0:T(8,128)S(1)} %get-tuple-element.30), channel_id=1, source_target_pairs={{0,12},{1,13},{2,14},{3,15},{4,16},{5,17},{6,18},{7,19},{8,20},{9,... | collective-permute-start | bytes 245768 | tf_op jit(solution)/shard_map/ppermute | solution.py:46
  5.2 0.0 collective-permute-start.3
  5.2 1.9 %collective-permute-start.2 = (s32[10,8,512]{2,1,0:T(8,128)S(1)}, s32[10,8,512]{2,1,0:T(8,128)S(1)}, u32[]{:S(2)}, u32[]{:S(2)}) collective-permute-start(s32[10,8,512]{2,1,0:T(8,128)S(1)} %get-tuple-element.28.own_ref), channel_id=1, source_target_pairs={{0,8},{1,9},{2,10},{3,11},{4,12},{5,13},{6,14},{7,15},{8,0},{9,1},... | collective-permute-start | bytes 491528 | tf_op jit(solution)/shard_map/ppermute | solution.py:46
  7.2 0.0 collective-permute-start.1
  7.2 1.6 %collective-permute-start = (s32[10,8,512]{2,1,0:T(8,128)S(1)}, s32[10,8,512]{2,1,0:T(8,128)S(1)}, u32[]{:S(2)}, u32[]{:S(2)}) collective-permute-start(s32[10,8,512]{2,1,0:T(8,128)S(1)} %get-tuple-element.28.own_ref), channel_id=1, source_target_pairs={{0,4},{1,5},{2,6},{3,7},{4,0},{5,1},{6,2},{7,3},{8,12},{9,13},{10,... | collective-permute-start | bytes 491528 | tf_op jit(solution)/shard_map/ppermute | solution.py:46
  8.7 0.0 collective-permute-done.4.refs_4_
  8.7 0.0 collective-permute-start.5
  8.7 1.3 %collective-permute-done.5.refs_5_ = s32[5,8,512]{2,1,0:T(8,128)S(1)} collective-permute-done((s32[5,8,512]{2,1,0:T(8,128)S(1)}, s32[5,8,512]{2,1,0:T(8,128)S(1)}, u32[]{:S(2)}, u32[]{:S(2)}) %collective-permute-start.5) | collective-permute-done | bytes 81952 | tf_op jit(solution)/shard_map/ppermute | solution.py:46
  10.0 0.0 collective-permute-done.3.refs_3_
  10.0 2.7 %collective-permute-done.2.refs_2_ = s32[10,8,512]{2,1,0:T(8,128)S(1)} collective-permute-done((s32[10,8,512]{2,1,0:T(8,128)S(1)}, s32[10,8,512]{2,1,0:T(8,128)S(1)}, u32[]{:S(2)}, u32[]{:S(2)}) %collective-permute-start.2) | collective-permute-done | bytes 163872 | tf_op jit(solution)/shard_map/ppermute | solution.py:46
  12.7 0.0 collective-permute-done.1.refs_1_
  12.7 3.1 %collective-permute-done.refs_0_ = s32[10,8,512]{2,1,0:T(8,128)S(1)} collective-permute-done((s32[10,8,512]{2,1,0:T(8,128)S(1)}, s32[10,8,512]{2,1,0:T(8,128)S(1)}, u32[]{:S(2)}, u32[]{:S(2)}) %collective-permute-start) | collective-permute-done | bytes 163872 | tf_op jit(solution)/shard_map/ppermute | solution.py:46
  15.8 0.3 pack.1
  16.1 0.1 collective-permute-start.6
  16.2 2.5 %collective-permute-start.7 = (s32[160,512]{1,0:T(8,128)S(1)}, s32[160,512]{1,0:T(8,128)S(1)}, u32[]{:S(2)}, u32[]{:S(2)}) collective-permute-start(s32[160,512]{1,0:T(8,128)S(1)} %get-tuple-element.34), channel_id=1, source_target_pairs={{0,4},{1,2},{2,1},{3,7},{4,0},{5,6},{6,5},{7,3},{8,12},{9,10},{10,... | collective-permute-start | bytes 983048 | tf_op jit(solution)/shard_map/ppermute | solution.py:46
  18.7 0.0 collective-permute-done.6.even_ref
  18.7 5.1 %collective-permute-done.7.odd_ref = s32[160,512]{1,0:T(8,128)S(1)} collective-permute-done((s32[160,512]{1,0:T(8,128)S(1)}, s32[160,512]{1,0:T(8,128)S(1)}, u32[]{:S(2)}, u32[]{:S(2)}) %collective-permute-start.7) | collective-permute-done | bytes 327712 | tf_op jit(solution)/shard_map/ppermute | solution.py:46
  23.8 5.0 %down.1 = (f32[14,24,512]{2,1,0:T(8,128)S(1)}, f32[14,24,512]{2,1,0:T(8,128)S(1)}, f32[14,24,512]{2,1,0:T(8,128)S(1)}, f32[14,24,512]{2,1,0:T(8,128)S(1)}, f32[1...) custom-call(s32[5,14,8,512]{3,2,1,0:T(8,128)S(1)} %get-tuple-element, ...), custom_call_target="tpu_custom_call" | custom-call | tf_op jit(solution)/shard_map/down/pallas_call | solution.py:502
  28.8 12.6 %all_to_all.15.first_ref = f32[8,8,128]{2,1,0:T(8,128)S(1)} all-to-all(f32[8,8,128]{2,1,0:T(8,128)S(1)} %get-tuple-element.36), channel_id=1, replica_groups=mesh['slab'=8,'row'=4] {'slab'}, dimensions={0} | all-to-all | bytes 65536 | tf_op jit(solution)/shard_map/all_to_all | solution.py:524
  41.4 0.5 coarse.2
  42.0 9.9 %all_to_all.16.second_ref = f32[32,8,128]{2,1,0:T(8,128)S(1)} all-to-all(f32[32,8,128]{2,1,0:T(8,128)S(1)} %coarse.2), channel_id=1, replica_groups=mesh['slab'=8,'row'=4] {'slab','row'}, dimensions={0} | all-to-all | bytes 262144 | tf_op jit(solution)/shard_map/all_to_all | solution.py:537
  51.9 6.5 %middle.1 = (f32[4,10,8,512]{3,2,1,0:T(8,128)S(1)}, f32[8,128]{1,0:T(8,128)S(1)}, f32[8,8,128]{2,1,0:T(8,128)S(1)}) custom-call(f32[32,8,128]{2,1,0:T(8,128)S(1)} %all_to_all.16.second_ref, f32[1,128]{1,0:T(1,128)S(1)} %get-tuple-element.35.dc_ref, f32[14,24,512]{2,1,0:T(8,128)S(1)} %get-tuple-element.38.refs_0_, ...), custom_call_target="tpu_custom_call" | custom-call | tf_op jit(solution)/shard_map/middle/pallas_call | solution.py:538
  58.4 9.1 %all_to_all.17.first_ref = f32[8,8,128]{2,1,0:T(8,128)S(1)} all-to-all(f32[8,8,128]{2,1,0:T(8,128)S(1)} %get-tuple-element.48), channel_id=1, replica_groups=mesh['slab'=8,'row'=4] {'slab'}, dimensions={0} | all-to-all | bytes 65536 | tf_op jit(solution)/shard_map/all_to_all | solution.py:524
  67.5 0.5 coarse.3.own_ref
  68.1 0.5 collective-permute-start.11
  68.6 0.4 collective-permute-start.10
  68.9 0.2 collective-permute-start.9
  69.1 1.7 %collective-permute-start.8 = (f32[1,8,128]{2,1,0:T(8,128)S(1)}, f32[1,8,128]{2,1,0:T(8,128)S(1)}, u32[]{:S(2)}, u32[]{:S(2)}) collective-permute-start(f32[1,8,128]{2,1,0:T(8,128)S(1)} %coarse.3.own_ref), channel_id=1, source_target_pairs={{0,4},{1,5},{2,6},{3,7},{4,0},{5,1},{6,2},{7,3},{8,12},{9,13},{10,... | collective-permute-start | bytes 12296 | tf_op jit(solution)/shard_map/ppermute | solution.py:46
  70.8 0.9 %collective-permute-done.11.y1 = f32[1,8,128]{2,1,0:T(8,128)S(1)} collective-permute-done((f32[1,8,128]{2,1,0:T(8,128)S(1)}, f32[1,8,128]{2,1,0:T(8,128)S(1)}, u32[]{:S(2)}, u32[]{:S(2)}) %collective-permute-start.11) | collective-permute-done | bytes 4128 | tf_op jit(solution)/shard_map/ppermute | solution.py:46
  71.7 1.0 %collective-permute-done.8.z0 = f32[1,8,128]{2,1,0:T(8,128)S(1)} collective-permute-done((f32[1,8,128]{2,1,0:T(8,128)S(1)}, f32[1,8,128]{2,1,0:T(8,128)S(1)}, u32[]{:S(2)}, u32[]{:S(2)}) %collective-permute-start.8) | collective-permute-done | bytes 4128 | tf_op jit(solution)/shard_map/ppermute | solution.py:46
  72.7 1.7 %last.1 = f32[8,2,8,512]{3,2,1,0:T(8,128)} custom-call(f32[1,8,128]{2,1,0:T(8,128)S(1)} %coarse.3.own_ref, f32[1,8,128]{2,1,0:T(8,128)S(1)} %collective-permute-done.8.z0, f32[1,8,128]{2,1,0:T(8,128)S(1)} %collective-permute-done.9.z1, f32[1,8,128]{2,1,0:T(8,128)S(1)} %collective-permute-done.10.y0, f32[1,8,128]{2,1,0:T(8,128)S(1)} %collective-permute-done.11.y1, ...), custom_call_target="tpu_custom_call" | custom-call | tf_op jit(solution)/shard_map/last/pallas_call | solution.py:557
  (2 shorter events, 0.0 us)
Async XLA Ops:
  1.2 7.5 %collective-permute-start.4 = (s32[5,8,512]{2,1,0:T(8,128)S(1)}, s32[5,8,512]{2,1,0:T(8,128)S(1)}, u32[]{:S(2)}, u32[]{:S(2)}) collective-permute-start(s32[5,8,512]{2,1,0:T(8,128)S(1)} %get-tuple-element.30), channel_id=1, source_target_pairs={{0,12},{1,13},{2,14},{3,15},{4,16},{5,17},{6,18},{7,19},{8,20},{9,... | collective-permute-start | bytes 245768 | tf_op jit(solution)/shard_map/ppermute | solution.py:46
  5.2 4.8 %collective-permute-start.3 = (s32[10,8,512]{2,1,0:T(8,128)S(1)}, s32[10,8,512]{2,1,0:T(8,128)S(1)}, u32[]{:S(2)}, u32[]{:S(2)}) collective-permute-start(s32[10,8,512]{2,1,0:T(8,128)S(1)} %get-tuple-element.28.own_ref), channel_id=1, source_target_pairs={{0,1},{1,0},{2,3},{3,2},{4,5},{5,4},{6,7},{7,6},{8,16},{9,17},{10,... | collective-permute-start | bytes 491528 | tf_op jit(solution)/shard_map/ppermute | solution.py:46
  5.2 7.5 %collective-permute-start.2 = (s32[10,8,512]{2,1,0:T(8,128)S(1)}, s32[10,8,512]{2,1,0:T(8,128)S(1)}, u32[]{:S(2)}, u32[]{:S(2)}) collective-permute-start(s32[10,8,512]{2,1,0:T(8,128)S(1)} %get-tuple-element.28.own_ref), channel_id=1, source_target_pairs={{0,8},{1,9},{2,10},{3,11},{4,12},{5,13},{6,14},{7,15},{8,0},{9,1},... | collective-permute-start | bytes 491528 | tf_op jit(solution)/shard_map/ppermute | solution.py:46
  7.2 5.6 %collective-permute-start.1 = (s32[10,8,512]{2,1,0:T(8,128)S(1)}, s32[10,8,512]{2,1,0:T(8,128)S(1)}, u32[]{:S(2)}, u32[]{:S(2)}) collective-permute-start(s32[10,8,512]{2,1,0:T(8,128)S(1)} %get-tuple-element.28.own_ref), channel_id=1, source_target_pairs={{0,1},{1,0},{2,3},{3,2},{4,8},{5,9},{6,10},{7,11},{8,4},{9,5},{10,... | collective-permute-start | bytes 491528 | tf_op jit(solution)/shard_map/ppermute | solution.py:46
  7.2 8.7 %collective-permute-start = (s32[10,8,512]{2,1,0:T(8,128)S(1)}, s32[10,8,512]{2,1,0:T(8,128)S(1)}, u32[]{:S(2)}, u32[]{:S(2)}) collective-permute-start(s32[10,8,512]{2,1,0:T(8,128)S(1)} %get-tuple-element.28.own_ref), channel_id=1, source_target_pairs={{0,4},{1,5},{2,6},{3,7},{4,0},{5,1},{6,2},{7,3},{8,12},{9,13},{10,... | collective-permute-start | bytes 491528 | tf_op jit(solution)/shard_map/ppermute | solution.py:46
  8.7 1.3 %collective-permute-start.5 = (s32[5,8,512]{2,1,0:T(8,128)S(1)}, s32[5,8,512]{2,1,0:T(8,128)S(1)}, u32[]{:S(2)}, u32[]{:S(2)}) collective-permute-start(s32[5,8,512]{2,1,0:T(8,128)S(1)} %get-tuple-element.31), channel_id=1, source_target_pairs={{0,1},{1,0},{2,3},{3,2},{4,5},{5,4},{6,7},{7,6},{8,9},{9,8},{10,11... | collective-permute-start | bytes 245768 | tf_op jit(solution)/shard_map/ppermute | solution.py:46
  16.1 2.6 %collective-permute-start.6 = (s32[160,512]{1,0:T(8,128)S(1)}, s32[160,512]{1,0:T(8,128)S(1)}, u32[]{:S(2)}, u32[]{:S(2)}) collective-permute-start(s32[160,512]{1,0:T(8,128)S(1)} %get-tuple-element.33), channel_id=1, source_target_pairs={{0,1},{1,0},{2,3},{3,2},{4,5},{5,4},{6,7},{7,6},{8,9},{9,8},{10,11... | collective-permute-start | bytes 983048 | tf_op jit(solution)/shard_map/ppermute | solution.py:46
  16.2 7.6 %collective-permute-start.7 = (s32[160,512]{1,0:T(8,128)S(1)}, s32[160,512]{1,0:T(8,128)S(1)}, u32[]{:S(2)}, u32[]{:S(2)}) collective-permute-start(s32[160,512]{1,0:T(8,128)S(1)} %get-tuple-element.34), channel_id=1, source_target_pairs={{0,4},{1,2},{2,1},{3,7},{4,0},{5,6},{6,5},{7,3},{8,12},{9,10},{10,... | collective-permute-start | bytes 983048 | tf_op jit(solution)/shard_map/ppermute | solution.py:46
  68.1 3.6 %collective-permute-start.11 = (f32[1,8,128]{2,1,0:T(8,128)S(1)}, f32[1,8,128]{2,1,0:T(8,128)S(1)}, u32[]{:S(2)}, u32[]{:S(2)}) collective-permute-start(f32[1,8,128]{2,1,0:T(8,128)S(1)} %coarse.3.own_ref), channel_id=1, source_target_pairs={{0,4},{1,2},{2,1},{3,7},{4,0},{5,6},{6,5},{7,3},{8,12},{9,10},{10,... | collective-permute-start | bytes 12296 | tf_op jit(solution)/shard_map/ppermute | solution.py:46
  68.6 3.1 %collective-permute-start.10 = (f32[1,8,128]{2,1,0:T(8,128)S(1)}, f32[1,8,128]{2,1,0:T(8,128)S(1)}, u32[]{:S(2)}, u32[]{:S(2)}) collective-permute-start(f32[1,8,128]{2,1,0:T(8,128)S(1)} %coarse.3.own_ref), channel_id=1, source_target_pairs={{0,1},{1,0},{2,3},{3,2},{4,5},{5,4},{6,7},{7,6},{8,9},{9,8},{10,11... | collective-permute-start | bytes 12296 | tf_op jit(solution)/shard_map/ppermute | solution.py:46
  68.9 2.8 %collective-permute-start.9 = (f32[1,8,128]{2,1,0:T(8,128)S(1)}, f32[1,8,128]{2,1,0:T(8,128)S(1)}, u32[]{:S(2)}, u32[]{:S(2)}) collective-permute-start(f32[1,8,128]{2,1,0:T(8,128)S(1)} %coarse.3.own_ref), channel_id=1, source_target_pairs={{0,1},{1,0},{2,3},{3,2},{4,8},{5,9},{6,10},{7,11},{8,4},{9,5},{10,... | collective-permute-start | bytes 12296 | tf_op jit(solution)/shard_map/ppermute | solution.py:46
  69.1 3.6 %collective-permute-start.8 = (f32[1,8,128]{2,1,0:T(8,128)S(1)}, f32[1,8,128]{2,1,0:T(8,128)S(1)}, u32[]{:S(2)}, u32[]{:S(2)}) collective-permute-start(f32[1,8,128]{2,1,0:T(8,128)S(1)} %coarse.3.own_ref), channel_id=1, source_target_pairs={{0,4},{1,5},{2,6},{3,7},{4,0},{5,1},{6,2},{7,3},{8,12},{9,13},{10,... | collective-permute-start | bytes 12296 | tf_op jit(solution)/shard_map/ppermute | solution.py:46

commit v4 on v3

--- a/solution.py
+++ b/solution.py
@@ -199,14 +199,9 @@
 
     def region(self, layers, body):
         s = self.s
-        for m in range(layers + 1):
-            lo, hi = -(layers - m), s.cy + layers - m
-
-            def inner(i, c, m=m, lo=lo, hi=hi):
-                body(i if m == 0 else jnp.where(i == 0, -m, s.cz - 1 + m), lo, hi)
-                return c
-
-            lax.fori_loop(0, s.cz if m == 0 else 2, inner, 0)
+        for z in range(-layers, s.cz + layers):
+            reach = layers - s.away(z)
+            body(z, -reach, s.cy + reach)
 
     def moved_rows(self, src, at, z, lo, hi, use):
         s = self.s
@@ -237,7 +232,10 @@
     def coarse_sums(self, src, src_at, scale, owners, acc):
         s = self.s
         acc[...] = jnp.zeros_like(acc)
-        cells = lax.broadcasted_iota(jnp.int32, (s.cc, s.nx), 0)
+        pack = 16
+        cells = lax.broadcasted_iota(jnp.int32, (s.cc, s.nx), 0).astype(jnp.float32)
+        cells = cells.astype(jnp.bfloat16).reshape(s.cc // pack, pack, s.nx)
+        one, none = jnp.bfloat16(1), jnp.bfloat16(0)
 
         def body(z, lo, hi):
             def use(y, centre, total):
@@ -246,8 +244,9 @@
                 mid = (rest - top).astype(jnp.bfloat16).astype(jnp.float32)
                 low = rest - top - mid
                 parts = jnp.concatenate([top, mid, low], axis=0).astype(jnp.bfloat16)
-                ids = jnp.broadcast_to(owners[z + s.oz, y + s.oy : y + s.oy + 1, :], (s.cc, s.nx))
-                onehot = jnp.where(ids == cells, 1.0, 0.0).astype(jnp.bfloat16)
+                ids = owners[z + s.oz, y + s.oy : y + s.oy + 1, :].astype(jnp.float32)
+                ids = jnp.broadcast_to(ids, (pack, s.nx)).astype(jnp.bfloat16)
+                onehot = jnp.where(ids[None] == cells, one, none).reshape(s.cc, s.nx)
                 acc[...] += lax.dot_general(
                     parts, onehot, (((1,), (1,)), ((), ())), preferred_element_type=jnp.float32
                 )
@@ -280,6 +279,25 @@
     return jnp.concatenate(parts, axis=1)
 
 
+def spread(tables, index, ids, dst, z, y):
+    numbers = lax.GatherDimensionNumbers(
+        offset_dims=(),
+        collapsed_slice_dims=(1,),
+        start_index_map=(1,),
+        operand_batching_dims=(0,),
+        start_indices_batching_dims=(0,),
+    )
+    count, width = ids.shape
+    lanes = tables.shape[2]
+    for x in range(0, width, lanes):
+        part = ids[:, x : x + lanes, None]
+        for l in range(LABELS):
+            row = jnp.broadcast_to(tables[index, l : l + 1, :], (count, lanes))
+            dst[z, y : y + count, l, x : x + lanes] = lax.gather(
+                row, part, numbers, (1, 1), mode=lax.GatherScatterMode.PROMISE_IN_BOUNDS
+            )
+
+
 def down_kernel(shape, frame_ref, even_ref, odd_ref, dc_ref, *refs):
     faces, (u1, owners, scale, u2, rhs_ref, first_ref, kept, ints, acc) = refs[:6], refs[6:]
     s = shape
@@ -375,28 +393,25 @@
 
 
 def middle_kernel(shape, second_ref, dc_ref, *refs):
-    faces, (u1, owners, scale, u2, u5, rhs_ref, first_ref, u3, u4, acc) = refs[:6], refs[6:]
+    faces, (u1, owners, scale, u2, u5, rhs_ref, first_ref, u3, u4, moves, acc) = refs[:6], refs[6:]
     s = shape
     slab = lax.axis_index("slab")
     row = lax.axis_index("row")
     fields = Fields(s, faces, u1)
     layers = NEED - 1
 
-    def table(dz, dy):
-        i = jnp.clip(slab + dz, 0, s.n_slab - 1) * s.n_row + jnp.clip(row + dy, 0, s.n_row - 1)
-        return second_ref[i]
-
     def correct(z, lo, hi):
-        dz = lax.div(z + s.oz, s.cz) - s.reach
+        dz = (z + s.oz) // s.cz - s.reach
         for dy in (-1, 0, 1):
             begin, end = max(lo, dy * s.cy), min(hi, (dy + 1) * s.cy)
             if begin >= end:
                 continue
-            tab = table(dz, dy)
-            for y in range(begin, end):
-                ids = owners[z + s.oz, y + s.oy : y + s.oy + 1, :]
-                at = (z + layers, y + layers)
-                u4[at] = u2[at] + take(tab, ids, s)
+            p = jnp.clip(slab + dz, 0, s.n_slab - 1)
+            q = jnp.clip(row + dy, 0, s.n_row - 1)
+            at = s.oy + dy * s.cy
+            spread(second_ref, p * s.n_row + q, owners[z + s.oz, at : at + s.cy], moves, z + layers, at)
+        for y in range(lo, hi):
+            u4[z + layers, y + layers] = u2[z + layers, y + layers] + moves[z + layers, y + s.oy]
 
     fields.region(layers, correct)
     fields.sweep(u4, layers, u3, layers, layers - 1)
@@ -410,7 +425,7 @@
 
 
 def last_kernel(shape, own_ref, z0, z1, y0, y1, *refs):
-    faces, (u1, owners, u5, out_ref, u6) = refs[:6], refs[6:]
+    faces, (u1, owners, u5, out_ref, u6, tables) = refs[:6], refs[6:]
     s = shape
     slab = lax.axis_index("slab")
     row = lax.axis_index("row")
@@ -419,28 +434,20 @@
     def pick(even, first, second):
         return jnp.where(even, first[0], second[0])
 
-    up_z = pick(slab % 2 == 0, z0, z1)
-    down_z = pick(slab % 2 == 0, z1, z0)
+    tables[0] = own_ref[0]
+    tables[1] = pick(slab % 2 == 0, z0, z1)
+    tables[2] = pick(slab % 2 == 0, z1, z0)
     up_y = pick(row % 2 == 0, y0, y1)
     down_y = pick(row % 2 == 0, y1, y0)
-
-    def add(z, y, tab):
-        ids = owners[z + s.oz, y + s.oy : y + s.oy + 1, :]
-        u6[z + 1, y + 1] = u5[z + 1, y + 1] + take(tab, ids, s)
-
-    own = own_ref[0]
-    for y in range(s.cy):
-        add(-1, y, down_z)
-        add(s.cz, y, up_z)
-
-    def plane(z, c):
-        add(z, -1, down_y)
-        add(z, s.cy, up_y)
+    for z in range(-1, s.cz + 1):
+        index = 2 if z < 0 else 1 if z == s.cz else 0
+        spread(tables, index, owners[z + s.oz, s.oy : s.oy + s.cy], u6, z + 1, 1)
         for y in range(s.cy):
-            add(z, y, own)
-        return c
-
-    lax.fori_loop(0, s.cz, plane, 0)
+            u6[z + 1, y + 1] += u5[z + 1, y + 1]
+        if index == 0:
+            for y, tab in ((-1, down_y), (s.cy, up_y)):
+                ids = owners[z + s.oz, y + s.oy : y + s.oy + 1, :]
+                u6[z + 1, y + 1] = u5[z + 1, y + 1] + take(tab, ids, s)
 
     def body(z, lo, hi):
         def use(y, centre, total):
@@ -547,6 +554,7 @@
         scratch_shapes=[
             pltpu.VMEM((s.cz + wide, s.cy + wide, LABELS, s.nx), jnp.float32),
             pltpu.VMEM((s.cz + wide, s.cy + wide, LABELS, s.nx), jnp.float32),
+            pltpu.VMEM((s.cz + wide, s.rows, LABELS, s.nx), jnp.float32),
             pltpu.VMEM((3 * LABELS, s.cc), jnp.float32),
         ],
         compiler_params=params(),
@@ -559,7 +567,10 @@
         out_shape=f32(LABELS, s.cz, s.cy, s.nx),
         in_specs=vmem(14),
         out_specs=vmem(1)[0],
-        scratch_shapes=[pltpu.VMEM((s.cz + 2, s.cy + 2, LABELS, s.nx), jnp.float32)],
+        scratch_shapes=[
+            pltpu.VMEM((s.cz + 2, s.cy + 2, LABELS, s.nx), jnp.float32),
+            pltpu.VMEM((3, LABELS, s.cc), jnp.float32),
+        ],
         compiler_params=params(),
         name="last",
     )(second, *around, *faces, u1, owners, u5)

time: 74.6 us -> 71.7 us (0.961)
  Pallas kernels: 15.8 us -> 12.9 us
    pallas_call x1, Pallas kernels: 6.54 us -> 4.97 us  [per_device(): pl.pallas_call(functools.partial(middle_kernel, s), out_shape=(f32(s.cz +...]
    pallas_call x1, Pallas kernels: 5.02 us -> 3.9 us  [per_device(): pl.pallas_call(functools.partial(down_kernel, s), out_shape=tuple([f32(*p...]
where the time goes in v4:
time: 71.7 us; the launch traced here: 71.4 us
  blocking collectives  31.6 us (44%)
  waiting for transfers between devices  14 us (20%)
  Pallas kernels  12.9 us (18%)
  starting transfers between devices  12.9 us (18%)
    all_to_all x2, blocking collectives, coarse(): lax.all_to_all(first, 'slab', 0, 0, axis_index_groups=groups if s.section...  21.7 us
    ppermute x12, waiting for transfers between devices, swap(): lax.ppermute(block, BOTH, pairing(n_slab, n_row, axis, distance, phase))  14 us
    ppermute x12, starting transfers between devices, swap(): lax.ppermute(block, BOTH, pairing(n_slab, n_row, axis, distance, phase))  12.9 us
    all_to_all x1, blocking collectives, per_device(): second = lax.all_to_all(second, BOTH, 0, 0, tiled=True)  9.91 us
    pallas_call x1, Pallas kernels, per_device(): pl.pallas_call(functools.partial(middle_kernel, s), out_shape=(f32(s.cz +...  4.97 us
    pallas_call x1, Pallas kernels, per_device(): pl.pallas_call(functools.partial(down_kernel, s), out_shape=tuple([f32(*p...  3.9 us
    pallas_call x1, Pallas kernels, per_device(): pl.pallas_call(functools.partial(last_kernel, s), out_shape=f32(LABELS, s...  1.45 us
  transfers between devices with their start and end apart: 12, of which 6 were waited for; matrix products, arithmetic and copies ran while one was open for 0% of the time, Pallas kernels for 0%

profile of v4, /device:TPU:0, one launch (start us, length us, event | category | flops | bytes accessed | tf_op | source)
XLA Modules:
  0.0 71.4 jit_solution(17504553850827822676)
XLA Ops:
  0.0 1.2 %start.1 = (s32[10,8,512]{2,1,0:T(8,128)S(1)}, f32[128,1024]{1,0:T(8,128)S(1)}, s32[5,8,512]{2,1,0:T(8,128)S(1)}, s32[5,8,512]{2,1,0:T(8,128)S(1)}) custom-call(s32[3,2,8,512]{3,2,1,0:T(8,128)} %edge_ref.1, s32[2,8,512]{2,1,0:T(8,128)} %seeds_ref.1, s32[2,8,512]{2,1,0:T(8,128)} %owners_ref.1, f32[128,1024]{1,0:T(8,128)} %bitcast.1), custom_call_target="tpu_custom_call" | custom-call | tf_op jit(solution)/shard_map/start/pallas_call | solution.py:475
  1.2 4.0 %collective-permute-start.4 = (s32[5,8,512]{2,1,0:T(8,128)S(1)}, s32[5,8,512]{2,1,0:T(8,128)S(1)}, u32[]{:S(2)}, u32[]{:S(2)}) collective-permute-start(s32[5,8,512]{2,1,0:T(8,128)S(1)} %get-tuple-element.30), channel_id=1, source_target_pairs={{0,12},{1,13},{2,14},{3,15},{4,16},{5,17},{6,18},{7,19},{8,20},{9,... | collective-permute-start | bytes 245768 | tf_op jit(solution)/shard_map/ppermute | solution.py:46
  5.2 0.0 collective-permute-start.3
  5.2 1.9 %collective-permute-start.2 = (s32[10,8,512]{2,1,0:T(8,128)S(1)}, s32[10,8,512]{2,1,0:T(8,128)S(1)}, u32[]{:S(2)}, u32[]{:S(2)}) collective-permute-start(s32[10,8,512]{2,1,0:T(8,128)S(1)} %get-tuple-element.28.own_ref), channel_id=1, source_target_pairs={{0,8},{1,9},{2,10},{3,11},{4,12},{5,13},{6,14},{7,15},{8,0},{9,1},... | collective-permute-start | bytes 491528 | tf_op jit(solution)/shard_map/ppermute | solution.py:46
  7.2 0.0 collective-permute-start.1
  7.2 1.6 %collective-permute-start = (s32[10,8,512]{2,1,0:T(8,128)S(1)}, s32[10,8,512]{2,1,0:T(8,128)S(1)}, u32[]{:S(2)}, u32[]{:S(2)}) collective-permute-start(s32[10,8,512]{2,1,0:T(8,128)S(1)} %get-tuple-element.28.own_ref), channel_id=1, source_target_pairs={{0,4},{1,5},{2,6},{3,7},{4,0},{5,1},{6,2},{7,3},{8,12},{9,13},{10,... | collective-permute-start | bytes 491528 | tf_op jit(solution)/shard_map/ppermute | solution.py:46
  8.7 0.0 collective-permute-done.4.refs_4_
  8.7 0.0 collective-permute-start.5
  8.7 1.3 %collective-permute-done.5.refs_5_ = s32[5,8,512]{2,1,0:T(8,128)S(1)} collective-permute-done((s32[5,8,512]{2,1,0:T(8,128)S(1)}, s32[5,8,512]{2,1,0:T(8,128)S(1)}, u32[]{:S(2)}, u32[]{:S(2)}) %collective-permute-start.5) | collective-permute-done | bytes 81952 | tf_op jit(solution)/shard_map/ppermute | solution.py:46
  10.0 0.0 collective-permute-done.3.refs_3_
  10.0 2.7 %collective-permute-done.2.refs_2_ = s32[10,8,512]{2,1,0:T(8,128)S(1)} collective-permute-done((s32[10,8,512]{2,1,0:T(8,128)S(1)}, s32[10,8,512]{2,1,0:T(8,128)S(1)}, u32[]{:S(2)}, u32[]{:S(2)}) %collective-permute-start.2) | collective-permute-done | bytes 163872 | tf_op jit(solution)/shard_map/ppermute | solution.py:46
  12.7 0.0 collective-permute-done.1.refs_1_
  12.7 3.1 %collective-permute-done.refs_0_ = s32[10,8,512]{2,1,0:T(8,128)S(1)} collective-permute-done((s32[10,8,512]{2,1,0:T(8,128)S(1)}, s32[10,8,512]{2,1,0:T(8,128)S(1)}, u32[]{:S(2)}, u32[]{:S(2)}) %collective-permute-start) | collective-permute-done | bytes 163872 | tf_op jit(solution)/shard_map/ppermute | solution.py:46
  15.8 0.3 pack.1
  16.1 0.1 collective-permute-start.6
  16.2 2.5 %collective-permute-start.7 = (s32[160,512]{1,0:T(8,128)S(1)}, s32[160,512]{1,0:T(8,128)S(1)}, u32[]{:S(2)}, u32[]{:S(2)}) collective-permute-start(s32[160,512]{1,0:T(8,128)S(1)} %get-tuple-element.34), channel_id=1, source_target_pairs={{0,4},{1,2},{2,1},{3,7},{4,0},{5,6},{6,5},{7,3},{8,12},{9,10},{10,... | collective-permute-start | bytes 983048 | tf_op jit(solution)/shard_map/ppermute | solution.py:46
  18.7 0.0 collective-permute-done.6.even_ref
  18.7 5.1 %collective-permute-done.7.odd_ref = s32[160,512]{1,0:T(8,128)S(1)} collective-permute-done((s32[160,512]{1,0:T(8,128)S(1)}, s32[160,512]{1,0:T(8,128)S(1)}, u32[]{:S(2)}, u32[]{:S(2)}) %collective-permute-start.7) | collective-permute-done | bytes 327712 | tf_op jit(solution)/shard_map/ppermute | solution.py:46
  23.8 3.9 %down.1 = (f32[14,24,512]{2,1,0:T(8,128)S(1)}, f32[14,24,512]{2,1,0:T(8,128)S(1)}, f32[14,24,512]{2,1,0:T(8,128)S(1)}, f32[14,24,512]{2,1,0:T(8,128)S(1)}, f32[1...) custom-call(s32[5,14,8,512]{3,2,1,0:T(8,128)S(1)} %get-tuple-element, ...), custom_call_target="tpu_custom_call" | custom-call | tf_op jit(solution)/shard_map/down/pallas_call | solution.py:509
  27.7 12.6 %all_to_all.15.first_ref = f32[8,8,128]{2,1,0:T(8,128)S(1)} all-to-all(f32[8,8,128]{2,1,0:T(8,128)S(1)} %get-tuple-element.36), channel_id=1, replica_groups=mesh['slab'=8,'row'=4] {'slab'}, dimensions={0} | all-to-all | bytes 65536 | tf_op jit(solution)/shard_map/all_to_all | solution.py:531
  40.3 0.5 coarse.2
  40.9 9.9 %all_to_all.16.second_ref = f32[32,8,128]{2,1,0:T(8,128)S(1)} all-to-all(f32[32,8,128]{2,1,0:T(8,128)S(1)} %coarse.2), channel_id=1, replica_groups=mesh['slab'=8,'row'=4] {'slab','row'}, dimensions={0} | all-to-all | bytes 262144 | tf_op jit(solution)/shard_map/all_to_all | solution.py:544
  50.8 5.0 %middle.1 = (f32[4,10,8,512]{3,2,1,0:T(8,128)S(1)}, f32[8,128]{1,0:T(8,128)S(1)}, f32[8,8,128]{2,1,0:T(8,128)S(1)}) custom-call(f32[32,8,128]{2,1,0:T(8,128)S(1)} %all_to_all.16.second_ref, f32[1,128]{1,0:T(1,128)S(1)} %get-tuple-element.35.dc_ref, f32[14,24,512]{2,1,0:T(8,128)S(1)} %get-tuple-element.38.refs_0_, ...), custom_call_target="tpu_custom_call" | custom-call | tf_op jit(solution)/shard_map/middle/pallas_call | solution.py:545
  55.8 9.1 %all_to_all.17.first_ref = f32[8,8,128]{2,1,0:T(8,128)S(1)} all-to-all(f32[8,8,128]{2,1,0:T(8,128)S(1)} %get-tuple-element.48), channel_id=1, replica_groups=mesh['slab'=8,'row'=4] {'slab'}, dimensions={0} | all-to-all | bytes 65536 | tf_op jit(solution)/shard_map/all_to_all | solution.py:531
  64.9 0.5 coarse.3.own_ref
  65.4 0.5 collective-permute-start.11
  65.9 0.4 collective-permute-start.10
  66.2 0.2 collective-permute-start.9
  66.4 1.7 %collective-permute-start.8 = (f32[1,8,128]{2,1,0:T(8,128)S(1)}, f32[1,8,128]{2,1,0:T(8,128)S(1)}, u32[]{:S(2)}, u32[]{:S(2)}) collective-permute-start(f32[1,8,128]{2,1,0:T(8,128)S(1)} %coarse.3.own_ref), channel_id=1, source_target_pairs={{0,4},{1,5},{2,6},{3,7},{4,0},{5,1},{6,2},{7,3},{8,12},{9,13},{10,... | collective-permute-start | bytes 12296 | tf_op jit(solution)/shard_map/ppermute | solution.py:46
  68.1 0.9 %collective-permute-done.11.y1 = f32[1,8,128]{2,1,0:T(8,128)S(1)} collective-permute-done((f32[1,8,128]{2,1,0:T(8,128)S(1)}, f32[1,8,128]{2,1,0:T(8,128)S(1)}, u32[]{:S(2)}, u32[]{:S(2)}) %collective-permute-start.11) | collective-permute-done | bytes 4128 | tf_op jit(solution)/shard_map/ppermute | solution.py:46
  69.0 1.0 %collective-permute-done.8.z0 = f32[1,8,128]{2,1,0:T(8,128)S(1)} collective-permute-done((f32[1,8,128]{2,1,0:T(8,128)S(1)}, f32[1,8,128]{2,1,0:T(8,128)S(1)}, u32[]{:S(2)}, u32[]{:S(2)}) %collective-permute-start.8) | collective-permute-done | bytes 4128 | tf_op jit(solution)/shard_map/ppermute | solution.py:46
  70.0 1.4 %last.1 = f32[8,2,8,512]{3,2,1,0:T(8,128)} custom-call(f32[1,8,128]{2,1,0:T(8,128)S(1)} %coarse.3.own_ref, f32[1,8,128]{2,1,0:T(8,128)S(1)} %collective-permute-done.8.z0, f32[1,8,128]{2,1,0:T(8,128)S(1)} %collective-permute-done.9.z1, f32[1,8,128]{2,1,0:T(8,128)S(1)} %collective-permute-done.10.y0, f32[1,8,128]{2,1,0:T(8,128)S(1)} %collective-permute-done.11.y1, ...), custom_call_target="tpu_custom_call" | custom-call | tf_op jit(solution)/shard_map/last/pallas_call | solution.py:565
  (2 shorter events, 0.0 us)
Async XLA Ops:
  1.2 7.5 %collective-permute-start.4 = (s32[5,8,512]{2,1,0:T(8,128)S(1)}, s32[5,8,512]{2,1,0:T(8,128)S(1)}, u32[]{:S(2)}, u32[]{:S(2)}) collective-permute-start(s32[5,8,512]{2,1,0:T(8,128)S(1)} %get-tuple-element.30), channel_id=1, source_target_pairs={{0,12},{1,13},{2,14},{3,15},{4,16},{5,17},{6,18},{7,19},{8,20},{9,... | collective-permute-start | bytes 245768 | tf_op jit(solution)/shard_map/ppermute | solution.py:46
  5.2 4.8 %collective-permute-start.3 = (s32[10,8,512]{2,1,0:T(8,128)S(1)}, s32[10,8,512]{2,1,0:T(8,128)S(1)}, u32[]{:S(2)}, u32[]{:S(2)}) collective-permute-start(s32[10,8,512]{2,1,0:T(8,128)S(1)} %get-tuple-element.28.own_ref), channel_id=1, source_target_pairs={{0,1},{1,0},{2,3},{3,2},{4,5},{5,4},{6,7},{7,6},{8,16},{9,17},{10,... | collective-permute-start | bytes 491528 | tf_op jit(solution)/shard_map/ppermute | solution.py:46
  5.2 7.5 %collective-permute-start.2 = (s32[10,8,512]{2,1,0:T(8,128)S(1)}, s32[10,8,512]{2,1,0:T(8,128)S(1)}, u32[]{:S(2)}, u32[]{:S(2)}) collective-permute-start(s32[10,8,512]{2,1,0:T(8,128)S(1)} %get-tuple-element.28.own_ref), channel_id=1, source_target_pairs={{0,8},{1,9},{2,10},{3,11},{4,12},{5,13},{6,14},{7,15},{8,0},{9,1},... | collective-permute-start | bytes 491528 | tf_op jit(solution)/shard_map/ppermute | solution.py:46
  7.2 5.6 %collective-permute-start.1 = (s32[10,8,512]{2,1,0:T(8,128)S(1)}, s32[10,8,512]{2,1,0:T(8,128)S(1)}, u32[]{:S(2)}, u32[]{:S(2)}) collective-permute-start(s32[10,8,512]{2,1,0:T(8,128)S(1)} %get-tuple-element.28.own_ref), channel_id=1, source_target_pairs={{0,1},{1,0},{2,3},{3,2},{4,8},{5,9},{6,10},{7,11},{8,4},{9,5},{10,... | collective-permute-start | bytes 491528 | tf_op jit(solution)/shard_map/ppermute | solution.py:46
  7.2 8.7 %collective-permute-start = (s32[10,8,512]{2,1,0:T(8,128)S(1)}, s32[10,8,512]{2,1,0:T(8,128)S(1)}, u32[]{:S(2)}, u32[]{:S(2)}) collective-permute-start(s32[10,8,512]{2,1,0:T(8,128)S(1)} %get-tuple-element.28.own_ref), channel_id=1, source_target_pairs={{0,4},{1,5},{2,6},{3,7},{4,0},{5,1},{6,2},{7,3},{8,12},{9,13},{10,... | collective-permute-start | bytes 491528 | tf_op jit(solution)/shard_map/ppermute | solution.py:46
  8.7 1.3 %collective-permute-start.5 = (s32[5,8,512]{2,1,0:T(8,128)S(1)}, s32[5,8,512]{2,1,0:T(8,128)S(1)}, u32[]{:S(2)}, u32[]{:S(2)}) collective-permute-start(s32[5,8,512]{2,1,0:T(8,128)S(1)} %get-tuple-element.31), channel_id=1, source_target_pairs={{0,1},{1,0},{2,3},{3,2},{4,5},{5,4},{6,7},{7,6},{8,9},{9,8},{10,11... | collective-permute-start | bytes 245768 | tf_op jit(solution)/shard_map/ppermute | solution.py:46
  16.1 2.6 %collective-permute-start.6 = (s32[160,512]{1,0:T(8,128)S(1)}, s32[160,512]{1,0:T(8,128)S(1)}, u32[]{:S(2)}, u32[]{:S(2)}) collective-permute-start(s32[160,512]{1,0:T(8,128)S(1)} %get-tuple-element.33), channel_id=1, source_target_pairs={{0,1},{1,0},{2,3},{3,2},{4,5},{5,4},{6,7},{7,6},{8,9},{9,8},{10,11... | collective-permute-start | bytes 983048 | tf_op jit(solution)/shard_map/ppermute | solution.py:46
  16.2 7.6 %collective-permute-start.7 = (s32[160,512]{1,0:T(8,128)S(1)}, s32[160,512]{1,0:T(8,128)S(1)}, u32[]{:S(2)}, u32[]{:S(2)}) collective-permute-start(s32[160,512]{1,0:T(8,128)S(1)} %get-tuple-element.34), channel_id=1, source_target_pairs={{0,4},{1,2},{2,1},{3,7},{4,0},{5,6},{6,5},{7,3},{8,12},{9,10},{10,... | collective-permute-start | bytes 983048 | tf_op jit(solution)/shard_map/ppermute | solution.py:46
  65.4 3.6 %collective-permute-start.11 = (f32[1,8,128]{2,1,0:T(8,128)S(1)}, f32[1,8,128]{2,1,0:T(8,128)S(1)}, u32[]{:S(2)}, u32[]{:S(2)}) collective-permute-start(f32[1,8,128]{2,1,0:T(8,128)S(1)} %coarse.3.own_ref), channel_id=1, source_target_pairs={{0,4},{1,2},{2,1},{3,7},{4,0},{5,6},{6,5},{7,3},{8,12},{9,10},{10,... | collective-permute-start | bytes 12296 | tf_op jit(solution)/shard_map/ppermute | solution.py:46
  65.9 3.1 %collective-permute-start.10 = (f32[1,8,128]{2,1,0:T(8,128)S(1)}, f32[1,8,128]{2,1,0:T(8,128)S(1)}, u32[]{:S(2)}, u32[]{:S(2)}) collective-permute-start(f32[1,8,128]{2,1,0:T(8,128)S(1)} %coarse.3.own_ref), channel_id=1, source_target_pairs={{0,1},{1,0},{2,3},{3,2},{4,5},{5,4},{6,7},{7,6},{8,9},{9,8},{10,11... | collective-permute-start | bytes 12296 | tf_op jit(solution)/shard_map/ppermute | solution.py:46
  66.2 2.8 %collective-permute-start.9 = (f32[1,8,128]{2,1,0:T(8,128)S(1)}, f32[1,8,128]{2,1,0:T(8,128)S(1)}, u32[]{:S(2)}, u32[]{:S(2)}) collective-permute-start(f32[1,8,128]{2,1,0:T(8,128)S(1)} %coarse.3.own_ref), channel_id=1, source_target_pairs={{0,1},{1,0},{2,3},{3,2},{4,8},{5,9},{6,10},{7,11},{8,4},{9,5},{10,... | collective-permute-start | bytes 12296 | tf_op jit(solution)/shard_map/ppermute | solution.py:46
  66.4 3.6 %collective-permute-start.8 = (f32[1,8,128]{2,1,0:T(8,128)S(1)}, f32[1,8,128]{2,1,0:T(8,128)S(1)}, u32[]{:S(2)}, u32[]{:S(2)}) collective-permute-start(f32[1,8,128]{2,1,0:T(8,128)S(1)} %coarse.3.own_ref), channel_id=1, source_target_pairs={{0,4},{1,5},{2,6},{3,7},{4,0},{5,1},{6,2},{7,3},{8,12},{9,13},{10,... | collective-permute-start | bytes 12296 | tf_op jit(solution)/shard_map/ppermute | solution.py:46

commit v5 on v4

--- a/solution.py
+++ b/solution.py
@@ -93,9 +93,13 @@
         base = NEED - self.away(z)
         return (base + (1 if z < 0 else 0), base, base, base, base - 1)[a]
 
-    def row_items(self, side):
+    def group_planes(self, group):
+        planes = range(-self.oz, self.cz + self.oz)
+        return [z for z in planes if (-self.cz <= z < 2 * self.cz) == (group == 0)]
+
+    def row_items(self, side, group):
         out, at = [], 0
-        for z in range(-self.oz, self.cz + self.oz):
+        for z in self.group_planes(group):
             for a, counts in enumerate(self.needed(z)):
                 if counts[side] > 0:
                     out.append((a, z, at, counts[side]))
@@ -142,17 +146,24 @@
     fetch.wait()
 
 
-def pack_kernel(shape, own_ref, blocks_ref, *refs):
-    recvs, (frame_ref, even_ref, odd_ref, dc_ref) = refs[:-4], refs[-4:]
-    cz, oz = shape.cz, shape.oz
+def pack_kernel(shape, group, *refs):
+    s = shape
+    distances = [1] if group == 0 else list(range(2, s.reach + 1))
+    outs = 4 if group == 0 else 3
+    ins, (frame_ref, even_ref, odd_ref, *more) = refs[:-outs], refs[-outs:]
     slab = lax.axis_index("slab")
     row = lax.axis_index("row")
-    for a in range(ARRAYS):
-        for z in range(cz):
-            frame_ref[a, oz + z] = own_ref[a * cz + z]
-    for d in range(1, shape.reach + 1):
-        first, second = recvs[2 * d - 2], recvs[2 * d - 1]
-        up, down = shape.plane_items(d)
+    cz, oz = s.cz, s.oz
+    if group == 0:
+        own_ref, blocks_ref, *recvs = ins
+        for a in range(ARRAYS):
+            for z in range(cz):
+                frame_ref[a, oz + z] = own_ref[a * cz + z]
+    else:
+        recvs = ins
+    for n, d in enumerate(distances):
+        first, second = recvs[2 * n], recvs[2 * n + 1]
+        up, down = s.plane_items(d)
 
         def place(above, below, d=d, up=up, down=down):
             for n, (a, z) in enumerate(down):
@@ -169,9 +180,9 @@
             place(second, first)
 
     def fill(last_ref, first_ref):
-        for a, z, at, count in shape.row_items(0)[0]:
-            last_ref[at : at + count] = frame_ref[a, oz + z, shape.cy - count :]
-        for a, z, at, count in shape.row_items(1)[0]:
+        for a, z, at, count in s.row_items(0, group)[0]:
+            last_ref[at : at + count] = frame_ref[a, oz + z, s.cy - count :]
+        for a, z, at, count in s.row_items(1, group)[0]:
             first_ref[at : at + count] = frame_ref[a, oz + z, :count]
 
     @pl.when(row % 2 == 0)
@@ -182,11 +193,12 @@
     def _():
         fill(odd_ref, even_ref)
 
-    turn = slab // shape.sections
-    block = blocks_ref[:, pl.ds(pl.multiple_of(turn * shape.cc, shape.cc), shape.cc)]
-    a = lax.broadcasted_iota(jnp.int32, block.shape, 0)
-    b = lax.broadcasted_iota(jnp.int32, block.shape, 1)
-    dc_ref[...] = jnp.sum(jnp.where(a == b, block, 0.0), axis=0, keepdims=True)
+    if group == 0:
+        turn = slab // s.sections
+        block = blocks_ref[:, pl.ds(pl.multiple_of(turn * s.cc, s.cc), s.cc)]
+        a = lax.broadcasted_iota(jnp.int32, block.shape, 0)
+        b = lax.broadcasted_iota(jnp.int32, block.shape, 1)
+        more[0][...] = jnp.sum(jnp.where(a == b, block, 0.0), axis=0, keepdims=True)
 
 
 def row_of(ref, z, y, count):
@@ -298,26 +310,28 @@
             )
 
 
-def down_kernel(shape, frame_ref, even_ref, odd_ref, dc_ref, *refs):
+def down_kernel(shape, near_ref, even0, odd0, far_ref, even1, odd1, dc_ref, *refs):
     faces, (u1, owners, scale, u2, rhs_ref, first_ref, kept, ints, acc) = refs[:6], refs[6:]
     s = shape
     slab = lax.axis_index("slab")
     row = lax.axis_index("row")
     cz, cy, oy, oz = s.cz, s.cy, s.oy, s.oz
 
-    def sides(below_ref, above_ref):
-        for a, z, at, count in s.row_items(0)[0]:
+    def sides(group, below_ref, above_ref):
+        for a, z, at, count in s.row_items(0, group)[0]:
             ints[a, oz + z, oy - count : oy] = below_ref[at : at + count]
-        for a, z, at, count in s.row_items(1)[0]:
+        for a, z, at, count in s.row_items(1, group)[0]:
             ints[a, oz + z, oy + cy : oy + cy + count] = above_ref[at : at + count]
 
     @pl.when(row % 2 == 0)
     def _():
-        sides(odd_ref, even_ref)
+        sides(0, odd0, even0)
+        sides(1, odd1, even1)
 
     @pl.when(row % 2 == 1)
     def _():
-        sides(even_ref, odd_ref)
+        sides(0, even0, odd0)
+        sides(1, even1, odd1)
 
     labels = lax.broadcasted_iota(jnp.int32, (LABELS, s.nx), 0)
     line = row * cy - oy + lax.broadcasted_iota(jnp.int32, (s.rows, s.nx), 0)
@@ -331,9 +345,14 @@
         inside = jnp.logical_and(plane != -1, plane != cz * s.n_slab - 1)
         return ints[0, i].astype(jnp.float32) * jnp.where(inside, weight_unit, 0.0)
 
+    near = [oz + z for z in s.group_planes(0)]
+
+    def centre(a, i):
+        ints[a, i, oy : oy + cy] = (near_ref if i in near else far_ref)[a, i]
+
     def prepare(i, below_z):
         for a in range(ARRAYS):
-            ints[a, i, oy : oy + cy] = frame_ref[a, i]
+            centre(a, i)
         w_z = weights_z(i)
         w_y = ints[1, i].astype(jnp.float32) * unit_y
         w_x = ints[2, i].astype(jnp.float32) * unit_x
@@ -350,14 +369,14 @@
         kept[i] = seed_weight * k
         owners[i] = jnp.where(inside, ints[4, i], 0)
 
-        @pl.when(jnp.logical_and(i >= oz, i < oz + cz))
-        def _():
-            scale[jnp.clip(i - oz, 0, cz - 1)] = d / smooth_step
-
+        if oz <= i < oz + cz:
+            scale[i - oz] = d / smooth_step
         return w_z
 
-    ints[0, 0, oy : oy + cy] = frame_ref[0, 0]
-    lax.fori_loop(1, s.planes - 1, prepare, weights_z(0))
+    centre(0, 0)
+    below = weights_z(0)
+    for i in range(1, s.planes - 1):
+        below = prepare(i, below)
     fields = Fields(s, faces, u1)
 
     def start(z, lo, hi):
@@ -488,22 +507,24 @@
         for ph in (0, 1):
             sent = messages[2 * s.partial.index(d) + ph] if d in s.partial else own
             recvs.append(swap(sent, "slab", d, ph))
-    rows = -(-max(s.row_items(0)[1], s.row_items(1)[1]) // 8) * 8
-    frame, even, odd, dc = pl.pallas_call(
-        functools.partial(pack_kernel, s),
-        out_shape=(
-            i32(ARRAYS, s.planes, s.cy, s.nx),
-            i32(rows, s.nx),
-            i32(rows, s.nx),
-            f32(1, s.cc),
-        ),
-        in_specs=vmem(2 + len(recvs)),
-        out_specs=tuple(vmem(4)),
-        compiler_params=params(),
-        name="pack",
-    )(own, blocks, *recvs)
-    even = swap(even, "row", 1, 0)
-    odd = swap(odd, "row", 1, 1)
+
+    def pack(group, *operands):
+        rows = -(-max(s.row_items(0, group)[1], s.row_items(1, group)[1]) // 8) * 8
+        shapes = [i32(ARRAYS, s.planes, s.cy, s.nx), i32(rows, s.nx), i32(rows, s.nx)]
+        shapes += [f32(1, s.cc)] * (group == 0)
+        frame, even, odd, *more = pl.pallas_call(
+            functools.partial(pack_kernel, s, group),
+            out_shape=tuple(shapes),
+            in_specs=vmem(len(operands)),
+            out_specs=tuple(vmem(len(shapes))),
+            compiler_params=params(),
+        )(*operands)
+        odd = swap(odd, "row", 1, 1)
+        even = swap(even, "row", 1, 0)
+        return [frame, even, odd], more
+
+    near, (dc,) = pack(0, own, blocks, *recvs[:2])
+    far, _ = pack(1, *recvs[2:])
     plane = (s.planes, s.rows, s.nx)
     wide = 2 * (NEED - 1)
     *faces, u1, owners, scale, u2, rhs, first = pl.pallas_call(
@@ -514,7 +535,7 @@
             + [f32(s.cz, s.rows, s.nx), f32(s.cz + wide, s.cy + wide, LABELS, s.nx)]
             + [f32(LABELS, s.cc), f32(s.group, LABELS, s.cc)]
         ),
-        in_specs=vmem(4),
+        in_specs=vmem(7),
         out_specs=tuple(vmem(12)),
         scratch_shapes=[
             pltpu.VMEM(plane, jnp.float32),
@@ -523,7 +544,7 @@
         ],
         compiler_params=params(),
         name="down",
-    )(frame, even, odd, dc)
+    )(*near, *far, dc)
 
     groups = [[t * s.sections + g for t in range(s.group)] for g in range(s.sections)]
 

time: 71.7 us -> 76.9 us (1.073)
  waiting for transfers between devices: 14 us -> 17.6 us
  starting transfers between devices: 12.9 us -> 14.5 us
  Pallas kernels: 12.9 us -> 12.1 us
  blocking collectives: 31.6 us -> 32.4 us
    ppermute x12 -> x14, waiting for transfers between devices: 14 us -> 17.6 us  [swap(): lax.ppermute(block, BOTH, pairing(n_slab, n_row, axis, distance, phase))]
    ppermute x12 -> x14, starting transfers between devices: 12.9 us -> 14.5 us  [swap(): lax.ppermute(block, BOTH, pairing(n_slab, n_row, axis, distance, phase))]
    all_to_all x2, blocking collectives: 21.7 us -> 22.5 us  [coarse(): lax.all_to_all(first, 'slab', 0, 0, axis_index_groups=groups if s.section...]
  transfers between devices with their start and end apart: 12 -> 14, of which waited for: 6 -> 7; matrix products, arithmetic and copies ran while one was open for 0% -> 0% of each run, Pallas kernels for 0% -> 0%
where the time goes in v5:
time: 76.9 us; the launch traced here: 76.7 us
  blocking collectives  32.4 us (42%)
  waiting for transfers between devices  17.6 us (23%)
  starting transfers between devices  14.5 us (19%)
  Pallas kernels  12.1 us (16%)
    all_to_all x2, blocking collectives, coarse(): lax.all_to_all(first, 'slab', 0, 0, axis_index_groups=groups if s.section...  22.5 us
    ppermute x14, waiting for transfers between devices, swap(): lax.ppermute(block, BOTH, pairing(n_slab, n_row, axis, distance, phase))  17.6 us
    ppermute x14, starting transfers between devices, swap(): lax.ppermute(block, BOTH, pairing(n_slab, n_row, axis, distance, phase))  14.5 us
    all_to_all x1, blocking collectives, per_device(): second = lax.all_to_all(second, BOTH, 0, 0, tiled=True)  9.91 us
    pallas_call x1, Pallas kernels, per_device(): pl.pallas_call(functools.partial(middle_kernel, s), out_shape=(f32(s.cz +...  4.96 us
    pallas_call x1, Pallas kernels, per_device(): pl.pallas_call(functools.partial(down_kernel, s), out_shape=tuple([f32(*p...  3.18 us
  transfers between devices with their start and end apart: 14, of which 7 were waited for; matrix products, arithmetic and copies ran while one was open for 0% of the time, Pallas kernels for 0%

profile of v5, /device:TPU:0, one launch (start us, length us, event | category | flops | bytes accessed | tf_op | source)
XLA Modules:
  0.0 76.7 jit_solution(12043143789999635996)
XLA Ops:
  0.0 1.2 %start.1 = (s32[10,8,512]{2,1,0:T(8,128)S(1)}, f32[128,1024]{1,0:T(8,128)S(1)}, s32[5,8,512]{2,1,0:T(8,128)S(1)}, s32[5,8,512]{2,1,0:T(8,128)S(1)}) custom-call(s32[3,2,8,512]{3,2,1,0:T(8,128)} %edge_ref.1, s32[2,8,512]{2,1,0:T(8,128)} %seeds_ref.1, s32[2,8,512]{2,1,0:T(8,128)} %owners_ref.1, f32[128,1024]{1,0:T(8,128)} %bitcast.1), custom_call_target="tpu_custom_call" | custom-call | tf_op jit(solution)/shard_map/start/pallas_call | solution.py:494
  1.2 0.6 collective-permute-start.1
  1.8 4.0 %collective-permute-start = (s32[10,8,512]{2,1,0:T(8,128)S(1)}, s32[10,8,512]{2,1,0:T(8,128)S(1)}, u32[]{:S(2)}, u32[]{:S(2)}) collective-permute-start(s32[10,8,512]{2,1,0:T(8,128)S(1)} %get-tuple-element.31.refs_0_), channel_id=1, source_target_pairs={{0,4},{1,5},{2,6},{3,7},{4,0},{5,1},{6,2},{7,3},{8,12},{9,13},{10,... | collective-permute-start | bytes 491528 | tf_op jit(solution)/shard_map/ppermute | solution.py:46
  5.8 6.3 %collective-permute-done.refs_2_ = s32[10,8,512]{2,1,0:T(8,128)S(1)} collective-permute-done((s32[10,8,512]{2,1,0:T(8,128)S(1)}, s32[10,8,512]{2,1,0:T(8,128)S(1)}, u32[]{:S(2)}, u32[]{:S(2)}) %collective-permute-start) | collective-permute-done | bytes 163872 | tf_op jit(solution)/shard_map/ppermute | solution.py:46
  12.1 0.2 shard_map.46
  12.3 0.1 collective-permute-start.2
  12.4 2.5 %collective-permute-start.3 = (s32[128,512]{1,0:T(8,128)S(1)}, s32[128,512]{1,0:T(8,128)S(1)}, u32[]{:S(2)}, u32[]{:S(2)}) collective-permute-start(s32[128,512]{1,0:T(8,128)S(1)} %get-tuple-element.35), channel_id=1, source_target_pairs={{0,4},{1,2},{2,1},{3,7},{4,0},{5,6},{6,5},{7,3},{8,12},{9,10},{10,... | collective-permute-start | bytes 786440 | tf_op jit(solution)/shard_map/ppermute | solution.py:46
  14.9 1.5 %collective-permute-start.6 = (s32[5,8,512]{2,1,0:T(8,128)S(1)}, s32[5,8,512]{2,1,0:T(8,128)S(1)}, u32[]{:S(2)}, u32[]{:S(2)}) collective-permute-start(s32[5,8,512]{2,1,0:T(8,128)S(1)} %get-tuple-element.36), channel_id=1, source_target_pairs={{0,12},{1,13},{2,14},{3,15},{4,16},{5,17},{6,18},{7,19},{8,20},{9,... | collective-permute-start | bytes 245768 | tf_op jit(solution)/shard_map/ppermute | solution.py:46
  16.5 0.8 %collective-permute-start.5 = (s32[10,8,512]{2,1,0:T(8,128)S(1)}, s32[10,8,512]{2,1,0:T(8,128)S(1)}, u32[]{:S(2)}, u32[]{:S(2)}) collective-permute-start(s32[10,8,512]{2,1,0:T(8,128)S(1)} %get-tuple-element.31.refs_0_), channel_id=1, source_target_pairs={{0,1},{1,0},{2,3},{3,2},{4,5},{5,4},{6,7},{7,6},{8,16},{9,17},{10,... | collective-permute-start | bytes 491528 | tf_op jit(solution)/shard_map/ppermute | solution.py:46
  17.3 0.8 %collective-permute-start.4 = (s32[10,8,512]{2,1,0:T(8,128)S(1)}, s32[10,8,512]{2,1,0:T(8,128)S(1)}, u32[]{:S(2)}, u32[]{:S(2)}) collective-permute-start(s32[10,8,512]{2,1,0:T(8,128)S(1)} %get-tuple-element.31.refs_0_), channel_id=1, source_target_pairs={{0,8},{1,9},{2,10},{3,11},{4,12},{5,13},{6,14},{7,15},{8,0},{9,1},... | collective-permute-start | bytes 491528 | tf_op jit(solution)/shard_map/ppermute | solution.py:46
  18.1 2.2 %collective-permute-done.6.refs_2_ = s32[5,8,512]{2,1,0:T(8,128)S(1)} collective-permute-done((s32[5,8,512]{2,1,0:T(8,128)S(1)}, s32[5,8,512]{2,1,0:T(8,128)S(1)}, u32[]{:S(2)}, u32[]{:S(2)}) %collective-permute-start.6) | collective-permute-done | bytes 81952 | tf_op jit(solution)/shard_map/ppermute | solution.py:46
  20.3 0.0 collective-permute-start.7
  20.3 1.3 %collective-permute-done.7.refs_3_ = s32[5,8,512]{2,1,0:T(8,128)S(1)} collective-permute-done((s32[5,8,512]{2,1,0:T(8,128)S(1)}, s32[5,8,512]{2,1,0:T(8,128)S(1)}, u32[]{:S(2)}, u32[]{:S(2)}) %collective-permute-start.7) | collective-permute-done | bytes 81952 | tf_op jit(solution)/shard_map/ppermute | solution.py:46
  21.5 2.8 %collective-permute-done.4.refs_0_ = s32[10,8,512]{2,1,0:T(8,128)S(1)} collective-permute-done((s32[10,8,512]{2,1,0:T(8,128)S(1)}, s32[10,8,512]{2,1,0:T(8,128)S(1)}, u32[]{:S(2)}, u32[]{:S(2)}) %collective-permute-start.4) | collective-permute-done | bytes 163872 | tf_op jit(solution)/shard_map/ppermute | solution.py:46
  24.3 0.1 shard_map.47
  24.4 0.1 collective-permute-start.8
  24.5 1.3 %collective-permute-start.9 = (s32[40,512]{1,0:T(8,128)S(1)}, s32[40,512]{1,0:T(8,128)S(1)}, u32[]{:S(2)}, u32[]{:S(2)}) collective-permute-start(s32[40,512]{1,0:T(8,128)S(1)} %get-tuple-element.40), channel_id=1, source_target_pairs={{0,4},{1,2},{2,1},{3,7},{4,0},{5,6},{6,5},{7,3},{8,12},{9,10},{10,... | collective-permute-start | bytes 245768 | tf_op jit(solution)/shard_map/ppermute | solution.py:46
  25.8 3.2 %collective-permute-done.9.odd1 = s32[40,512]{1,0:T(8,128)S(1)} collective-permute-done((s32[40,512]{1,0:T(8,128)S(1)}, s32[40,512]{1,0:T(8,128)S(1)}, u32[]{:S(2)}, u32[]{:S(2)}) %collective-permute-start.9) | collective-permute-done | bytes 81952 | tf_op jit(solution)/shard_map/ppermute | solution.py:46
  29.0 3.2 %down.1 = (f32[14,24,512]{2,1,0:T(8,128)S(1)}, f32[14,24,512]{2,1,0:T(8,128)S(1)}, f32[14,24,512]{2,1,0:T(8,128)S(1)}, f32[14,24,512]{2,1,0:T(8,128)S(1)}, f32[1...) custom-call(s32[5,14,8,512]{3,2,1,0:T(8,128)S(1)} %get-tuple-element, ...), custom_call_target="tpu_custom_call" | custom-call | tf_op jit(solution)/shard_map/down/pallas_call | solution.py:530
  32.2 13.4 %all_to_all.15.first_ref = f32[8,8,128]{2,1,0:T(8,128)S(1)} all-to-all(f32[8,8,128]{2,1,0:T(8,128)S(1)} %get-tuple-element.42), channel_id=1, replica_groups=mesh['slab'=8,'row'=4] {'slab'}, dimensions={0} | all-to-all | bytes 65536 | tf_op jit(solution)/shard_map/all_to_all | solution.py:552
  45.6 0.5 coarse.2
  46.2 9.9 %all_to_all.16.second_ref = f32[32,8,128]{2,1,0:T(8,128)S(1)} all-to-all(f32[32,8,128]{2,1,0:T(8,128)S(1)} %coarse.2), channel_id=1, replica_groups=mesh['slab'=8,'row'=4] {'slab','row'}, dimensions={0} | all-to-all | bytes 262144 | tf_op jit(solution)/shard_map/all_to_all | solution.py:565
  56.1 5.0 %middle.1 = (f32[4,10,8,512]{3,2,1,0:T(8,128)S(1)}, f32[8,128]{1,0:T(8,128)S(1)}, f32[8,8,128]{2,1,0:T(8,128)S(1)}) custom-call(f32[32,8,128]{2,1,0:T(8,128)S(1)} %all_to_all.16.second_ref, f32[1,128]{1,0:T(1,128)S(1)} %get-tuple-element.41.dc_ref, f32[14,24,512]{2,1,0:T(8,128)S(1)} %get-tuple-element.44.refs_0_, ...), custom_call_target="tpu_custom_call" | custom-call | tf_op jit(solution)/shard_map/middle/pallas_call | solution.py:566
  61.0 9.1 %all_to_all.17.first_ref = f32[8,8,128]{2,1,0:T(8,128)S(1)} all-to-all(f32[8,8,128]{2,1,0:T(8,128)S(1)} %get-tuple-element.54), channel_id=1, replica_groups=mesh['slab'=8,'row'=4] {'slab'}, dimensions={0} | all-to-all | bytes 65536 | tf_op jit(solution)/shard_map/all_to_all | solution.py:552
  70.2 0.5 coarse.3.own_ref
  70.7 0.5 collective-permute-start.13
  71.2 0.4 collective-permute-start.12
  71.5 0.2 collective-permute-start.11
  71.7 1.7 %collective-permute-start.10 = (f32[1,8,128]{2,1,0:T(8,128)S(1)}, f32[1,8,128]{2,1,0:T(8,128)S(1)}, u32[]{:S(2)}, u32[]{:S(2)}) collective-permute-start(f32[1,8,128]{2,1,0:T(8,128)S(1)} %coarse.3.own_ref), channel_id=1, source_target_pairs={{0,4},{1,5},{2,6},{3,7},{4,0},{5,1},{6,2},{7,3},{8,12},{9,13},{10,... | collective-permute-start | bytes 12296 | tf_op jit(solution)/shard_map/ppermute | solution.py:46
  73.4 0.9 %collective-permute-done.13.y1 = f32[1,8,128]{2,1,0:T(8,128)S(1)} collective-permute-done((f32[1,8,128]{2,1,0:T(8,128)S(1)}, f32[1,8,128]{2,1,0:T(8,128)S(1)}, u32[]{:S(2)}, u32[]{:S(2)}) %collective-permute-start.13) | collective-permute-done | bytes 4128 | tf_op jit(solution)/shard_map/ppermute | solution.py:46
  74.3 1.0 %collective-permute-done.10.z0 = f32[1,8,128]{2,1,0:T(8,128)S(1)} collective-permute-done((f32[1,8,128]{2,1,0:T(8,128)S(1)}, f32[1,8,128]{2,1,0:T(8,128)S(1)}, u32[]{:S(2)}, u32[]{:S(2)}) %collective-permute-start.10) | collective-permute-done | bytes 4128 | tf_op jit(solution)/shard_map/ppermute | solution.py:46
  75.3 1.4 %last.1 = f32[8,2,8,512]{3,2,1,0:T(8,128)} custom-call(f32[1,8,128]{2,1,0:T(8,128)S(1)} %coarse.3.own_ref, f32[1,8,128]{2,1,0:T(8,128)S(1)} %collective-permute-done.10.z0, f32[1,8,128]{2,1,0:T(8,128)S(1)} %collective-permute-done.11.z1, f32[1,8,128]{2,1,0:T(8,128)S(1)} %collective-permute-done.12.y0, f32[1,8,128]{2,1,0:T(8,128)S(1)} %collective-permute-done.13.y1, ...), custom_call_target="tpu_custom_call" | custom-call | tf_op jit(solution)/shard_map/last/pallas_call | solution.py:586
  (7 shorter events, 0.0 us)
Async XLA Ops:
  1.2 4.6 %collective-permute-start.1 = (s32[10,8,512]{2,1,0:T(8,128)S(1)}, s32[10,8,512]{2,1,0:T(8,128)S(1)}, u32[]{:S(2)}, u32[]{:S(2)}) collective-permute-start(s32[10,8,512]{2,1,0:T(8,128)S(1)} %get-tuple-element.31.refs_0_), channel_id=1, source_target_pairs={{0,1},{1,0},{2,3},{3,2},{4,8},{5,9},{6,10},{7,11},{8,4},{9,5},{10,... | collective-permute-start | bytes 491528 | tf_op jit(solution)/shard_map/ppermute | solution.py:46
  1.8 10.3 %collective-permute-start = (s32[10,8,512]{2,1,0:T(8,128)S(1)}, s32[10,8,512]{2,1,0:T(8,128)S(1)}, u32[]{:S(2)}, u32[]{:S(2)}) collective-permute-start(s32[10,8,512]{2,1,0:T(8,128)S(1)} %get-tuple-element.31.refs_0_), channel_id=1, source_target_pairs={{0,4},{1,5},{2,6},{3,7},{4,0},{5,1},{6,2},{7,3},{8,12},{9,13},{10,... | collective-permute-start | bytes 491528 | tf_op jit(solution)/shard_map/ppermute | solution.py:46
  12.3 16.7 %collective-permute-start.2 = (s32[128,512]{1,0:T(8,128)S(1)}, s32[128,512]{1,0:T(8,128)S(1)}, u32[]{:S(2)}, u32[]{:S(2)}) collective-permute-start(s32[128,512]{1,0:T(8,128)S(1)} %get-tuple-element.34), channel_id=1, source_target_pairs={{0,1},{1,0},{2,3},{3,2},{4,5},{5,4},{6,7},{7,6},{8,9},{9,8},{10,11... | collective-permute-start | bytes 786440 | tf_op jit(solution)/shard_map/ppermute | solution.py:46
  12.4 16.6 %collective-permute-start.3 = (s32[128,512]{1,0:T(8,128)S(1)}, s32[128,512]{1,0:T(8,128)S(1)}, u32[]{:S(2)}, u32[]{:S(2)}) collective-permute-start(s32[128,512]{1,0:T(8,128)S(1)} %get-tuple-element.35), channel_id=1, source_target_pairs={{0,4},{1,2},{2,1},{3,7},{4,0},{5,6},{6,5},{7,3},{8,12},{9,10},{10,... | collective-permute-start | bytes 786440 | tf_op jit(solution)/shard_map/ppermute | solution.py:46
  14.9 5.4 %collective-permute-start.6 = (s32[5,8,512]{2,1,0:T(8,128)S(1)}, s32[5,8,512]{2,1,0:T(8,128)S(1)}, u32[]{:S(2)}, u32[]{:S(2)}) collective-permute-start(s32[5,8,512]{2,1,0:T(8,128)S(1)} %get-tuple-element.36), channel_id=1, source_target_pairs={{0,12},{1,13},{2,14},{3,15},{4,16},{5,17},{6,18},{7,19},{8,20},{9,... | collective-permute-start | bytes 245768 | tf_op jit(solution)/shard_map/ppermute | solution.py:46
  16.5 5.1 %collective-permute-start.5 = (s32[10,8,512]{2,1,0:T(8,128)S(1)}, s32[10,8,512]{2,1,0:T(8,128)S(1)}, u32[]{:S(2)}, u32[]{:S(2)}) collective-permute-start(s32[10,8,512]{2,1,0:T(8,128)S(1)} %get-tuple-element.31.refs_0_), channel_id=1, source_target_pairs={{0,1},{1,0},{2,3},{3,2},{4,5},{5,4},{6,7},{7,6},{8,16},{9,17},{10,... | collective-permute-start | bytes 491528 | tf_op jit(solution)/shard_map/ppermute | solution.py:46
  17.3 7.0 %collective-permute-start.4 = (s32[10,8,512]{2,1,0:T(8,128)S(1)}, s32[10,8,512]{2,1,0:T(8,128)S(1)}, u32[]{:S(2)}, u32[]{:S(2)}) collective-permute-start(s32[10,8,512]{2,1,0:T(8,128)S(1)} %get-tuple-element.31.refs_0_), channel_id=1, source_target_pairs={{0,8},{1,9},{2,10},{3,11},{4,12},{5,13},{6,14},{7,15},{8,0},{9,1},... | collective-permute-start | bytes 491528 | tf_op jit(solution)/shard_map/ppermute | solution.py:46
  20.3 1.3 %collective-permute-start.7 = (s32[5,8,512]{2,1,0:T(8,128)S(1)}, s32[5,8,512]{2,1,0:T(8,128)S(1)}, u32[]{:S(2)}, u32[]{:S(2)}) collective-permute-start(s32[5,8,512]{2,1,0:T(8,128)S(1)} %get-tuple-element.37), channel_id=1, source_target_pairs={{0,1},{1,0},{2,3},{3,2},{4,5},{5,4},{6,7},{7,6},{8,9},{9,8},{10,11... | collective-permute-start | bytes 245768 | tf_op jit(solution)/shard_map/ppermute | solution.py:46
  24.4 1.4 %collective-permute-start.8 = (s32[40,512]{1,0:T(8,128)S(1)}, s32[40,512]{1,0:T(8,128)S(1)}, u32[]{:S(2)}, u32[]{:S(2)}) collective-permute-start(s32[40,512]{1,0:T(8,128)S(1)} %get-tuple-element.39), channel_id=1, source_target_pairs={{0,1},{1,0},{2,3},{3,2},{4,5},{5,4},{6,7},{7,6},{8,9},{9,8},{10,11... | collective-permute-start | bytes 245768 | tf_op jit(solution)/shard_map/ppermute | solution.py:46
  24.5 4.5 %collective-permute-start.9 = (s32[40,512]{1,0:T(8,128)S(1)}, s32[40,512]{1,0:T(8,128)S(1)}, u32[]{:S(2)}, u32[]{:S(2)}) collective-permute-start(s32[40,512]{1,0:T(8,128)S(1)} %get-tuple-element.40), channel_id=1, source_target_pairs={{0,4},{1,2},{2,1},{3,7},{4,0},{5,6},{6,5},{7,3},{8,12},{9,10},{10,... | collective-permute-start | bytes 245768 | tf_op jit(solution)/shard_map/ppermute | solution.py:46
  70.7 3.6 %collective-permute-start.13 = (f32[1,8,128]{2,1,0:T(8,128)S(1)}, f32[1,8,128]{2,1,0:T(8,128)S(1)}, u32[]{:S(2)}, u32[]{:S(2)}) collective-permute-start(f32[1,8,128]{2,1,0:T(8,128)S(1)} %coarse.3.own_ref), channel_id=1, source_target_pairs={{0,4},{1,2},{2,1},{3,7},{4,0},{5,6},{6,5},{7,3},{8,12},{9,10},{10,... | collective-permute-start | bytes 12296 | tf_op jit(solution)/shard_map/ppermute | solution.py:46
  71.2 3.1 %collective-permute-start.12 = (f32[1,8,128]{2,1,0:T(8,128)S(1)}, f32[1,8,128]{2,1,0:T(8,128)S(1)}, u32[]{:S(2)}, u32[]{:S(2)}) collective-permute-start(f32[1,8,128]{2,1,0:T(8,128)S(1)} %coarse.3.own_ref), channel_id=1, source_target_pairs={{0,1},{1,0},{2,3},{3,2},{4,5},{5,4},{6,7},{7,6},{8,9},{9,8},{10,11... | collective-permute-start | bytes 12296 | tf_op jit(solution)/shard_map/ppermute | solution.py:46
  71.5 2.8 %collective-permute-start.11 = (f32[1,8,128]{2,1,0:T(8,128)S(1)}, f32[1,8,128]{2,1,0:T(8,128)S(1)}, u32[]{:S(2)}, u32[]{:S(2)}) collective-permute-start(f32[1,8,128]{2,1,0:T(8,128)S(1)} %coarse.3.own_ref), channel_id=1, source_target_pairs={{0,1},{1,0},{2,3},{3,2},{4,8},{5,9},{6,10},{7,11},{8,4},{9,5},{10,... | collective-permute-start | bytes 12296 | tf_op jit(solution)/shard_map/ppermute | solution.py:46
  71.7 3.6 %collective-permute-start.10 = (f32[1,8,128]{2,1,0:T(8,128)S(1)}, f32[1,8,128]{2,1,0:T(8,128)S(1)}, u32[]{:S(2)}, u32[]{:S(2)}) collective-permute-start(f32[1,8,128]{2,1,0:T(8,128)S(1)} %coarse.3.own_ref), channel_id=1, source_target_pairs={{0,4},{1,5},{2,6},{3,7},{4,0},{5,1},{6,2},{7,3},{8,12},{9,13},{10,... | collective-permute-start | bytes 12296 | tf_op jit(solution)/shard_map/ppermute | solution.py:46
